TPU v7x, 512 devices: a whole 4x4x16 slice. The times are simulated.
512 devices in a mesh: neuron: 16 (over y_lo, x, core), box: 16 (over z), spec: 2 (over y_hi).
Axes of the slice: x: 4, y: 4 (y_hi: 2, y_lo: 2; y = y_hi * 2 + y_lo), z: 16, core: 2. Of those that a mesh axis runs over, the one named last changes fastest.
Arguments:
- coeff: bfloat16 [384, 8, 8192], P('box', 'spec', 'neuron'), may hold values from -6 to 6
- weight: bfloat16 [8192, 8192], P('neuron', 'spec'), may hold values from -0.09375 to 0.09375
- upper_bound: float32 [384, 8192], P('box', 'neuron'), may hold values from 0.2 to 6, as said below
- lower_depth: float32 [384, 8192], P('box', 'neuron'), may hold values from 0.2 to 6, as said below
- slopes: float32 [384, 8192], P('box', 'neuron'), may hold values from 0 to 1
- state: int32 [384, 8192], P('box', 'neuron'), may hold values from 0 to 2
- adjoint: bfloat16 [384, 8, 8192], P('box', 'spec', 'neuron'), may hold values from -6 to 6
Outputs:
- new_coeff: bfloat16 [384, 8, 8192], P('box', 'spec', 'neuron')
- offset: float32 [384, 8], P('box', 'spec')
- slope_grad: float32 [384, 8192], P('box', 'neuron')
- coeff_grad: bfloat16 [384, 8, 8192], P('box', 'spec', 'neuron')
Inputs may be any that keep to these rules, and one draw needn't show every extreme that they name: `upper_bound`: positive. `lower_depth`: positive.
All inputs are finite; a program needn't handle non-finite values.
Results may differ from a plain program's by a relative error of at most 0.0095.
Values may be sent and summed in bfloat16 or wider, within the bound.
No kernel may reach another device: no remote copies, remote signals or barrier semaphores. Data moves between devices by JAX's collectives and lax.ppermute only.
A program may use at most 64 MiB of HBM per device.

v0:
```python
import jax
import jax.numpy as jnp
from jax import lax
from jax.experimental import pallas as pl
from jax.experimental.pallas import tpu as pltpu
from jax.sharding import PartitionSpec as P


D = 8192

CHIPS = 8
LINE = 4
VMEM = 24 * 1024 * 1024
SCALE = 64.0

BOTH = ("neuron", "spec")
CORE_SWAP = [(n, n ^ 1) for n in range(16)]
SPEC_SWAP = [(0, 1), (1, 0)]
SAME_CORE = [[n for n in range(16) if n % 2 == core] for core in range(2)]


def middle_swap():
    pairs = []
    for n in range(16):
        for s in range(2):
            y_lo, rest = n // 8, n % 8
            pairs.append((n * 2 + s, (s * 8 + rest) * 2 + y_lo))
    return pairs


MIDDLE_SWAP = middle_swap()


def halves(w_ref, buf_ref, sems, core):
    width = buf_ref.shape[2]
    return [
        pltpu.make_async_copy(
            w_ref.at[:, pl.ds(pl.multiple_of((2 * i + core) * width, width), width)], buf_ref.at[i], sems.at[i]
        )
        for i in range(LINE)
    ]


def stage_kernel(place, w_ref, out_ref, sems):
    copies = halves(w_ref, out_ref, sems, place[1])
    for copy in copies:
        copy.start()
    for copy in copies:
        copy.wait()


def in_hbm(w):
    return pltpu.with_memory_space_constraint(w, pltpu.HBM)


def in_vmem(w):
    return pltpu.with_memory_space_constraint(w, pltpu.VMEM)


SMEM_SPEC = pl.BlockSpec(memory_space=pltpu.SMEM)
VMEM_SPEC = pl.BlockSpec(memory_space=pltpu.VMEM)
HBM_SPEC = pl.BlockSpec(memory_space=pltpu.HBM)
SEMS = pltpu.SemaphoreType.DMA((LINE,))


def half_shape(w):
    return (LINE, w.shape[0], w.shape[0])


def cost(flops, moved):
    return pl.CostEstimate(flops=flops, bytes_accessed=moved, transcendentals=0)


def stage(place, w):
    return pl.pallas_call(
        stage_kernel,
        out_shape=pltpu.VMEM(half_shape(w), w.dtype),
        in_specs=[SMEM_SPEC, HBM_SPEC],
        out_specs=VMEM_SPEC,
        scratch_shapes=[SEMS],
        compiler_params=pltpu.CompilerParams(vmem_limit_bytes=VMEM),
        cost_estimate=cost(0, w.size * 2),
    )(place, in_hbm(w))


def part_block(place, x_ref, block, out_ref, col):
    own = place[0]
    rows = x_ref.shape[1]
    both = x_ref[...].reshape(2 * rows, x_ref.shape[2])
    acc = jnp.dot(both, block, preferred_element_type=jnp.float32) * SCALE
    out_ref[pl.ds(own * LINE + col, 1)] = acc[:rows][None]
    out_ref[pl.ds((1 - own) * LINE + col, 1)] = acc[rows:][None]


def near_kernel(place, x_ref, half_ref, out_ref):
    for i in range(LINE):
        part_block(place, x_ref, half_ref[i], out_ref, i)


def far_kernel(place, x_ref, w_ref, out_ref, buf_ref, sems):
    copies = halves(w_ref, buf_ref, sems, place[1])
    for copy in copies:
        copy.start()
    for i in range(LINE):
        copies[i].wait()
        part_block(place, x_ref, buf_ref[i], out_ref, i)


def part_sums(place, x, w, staged):
    rows, width = x.shape[1:]
    return pl.pallas_call(
        near_kernel if staged else far_kernel,
        out_shape=jax.ShapeDtypeStruct((CHIPS, rows, width), jnp.float32),
        in_specs=[SMEM_SPEC, VMEM_SPEC, VMEM_SPEC if staged else HBM_SPEC],
        out_specs=VMEM_SPEC,
        scratch_shapes=[] if staged else [pltpu.VMEM(half_shape(w), w.dtype), SEMS],
        compiler_params=pltpu.CompilerParams(vmem_limit_bytes=VMEM),
        cost_estimate=cost(2 * 2 * rows * width * width * LINE, width * width * LINE * 2),
    )(place, x, in_vmem(w) if staged else in_hbm(w))


def middle_kernel(r_ref, a_ref, b_ref, c_ref, adj_ref, g_ref, back_ref):
    pre = r_ref[...]
    rows = pre.shape[0]
    positive = jnp.maximum(pre, 0.0)
    negative = jnp.minimum(pre, 0.0)
    a, b, c = a_ref[...], b_ref[...], c_ref[...]
    cot = adj_ref[...].astype(jnp.float32)
    back_ref[0:rows] = (a * positive + b * negative).astype(jnp.bfloat16)
    grad = (cot * jnp.where(pre > 0.0, a, b)).astype(jnp.bfloat16)
    for k in range(CHIPS):
        g_ref[k, 0:rows] = grad
    width = pre.shape[1]
    line = lax.dot_general(
        jnp.ones((8, width), jnp.float32),
        negative * c,
        (((1,), (1,)), ((), ())),
        precision=lax.Precision.HIGHEST,
        preferred_element_type=jnp.float32,
    ) * (float(D) ** -0.5)
    high = line.astype(jnp.bfloat16).astype(jnp.float32)
    row = lax.broadcasted_iota(jnp.int32, line.shape, 0)
    tile = jnp.where(row == 0, high, jnp.where(row == 1, line - high, 0.0))
    tile = jnp.concatenate([tile, jnp.zeros((8, width - rows), jnp.float32)], axis=1).astype(jnp.bfloat16)
    for k in range(CHIPS):
        g_ref[k, rows : rows + 8] = tile
    boxes = rows // 4
    mine = lax.broadcasted_iota(jnp.int32, (boxes, rows), 1) // 4 == lax.broadcasted_iota(
        jnp.int32, (boxes, rows), 0
    )
    slope = jnp.dot(
        jnp.where(mine, 1.0, 0.0),
        jnp.where(c > 0.0, cot * positive, 0.0),
        precision=lax.Precision.HIGHEST,
        preferred_element_type=jnp.float32,
    )
    back_ref[rows : rows + boxes] = slope.astype(jnp.bfloat16)


def middle(r, a, b, c, adj):
    rows, width = r.shape
    return pl.pallas_call(
        middle_kernel,
        out_shape=(
            jax.ShapeDtypeStruct((CHIPS, rows + 8, width), jnp.bfloat16),
            jax.ShapeDtypeStruct((rows + rows // 4, width), jnp.bfloat16),
        ),
        compiler_params=pltpu.CompilerParams(vmem_limit_bytes=VMEM),
        cost_estimate=pl.CostEstimate(flops=30 * rows * width, bytes_accessed=8 * rows * width * 4, transcendentals=0),
    )(r, a, b, c, adj)


def back_block(g_ref, block, i):
    rows = g_ref.shape[2] - 8
    both = jnp.concatenate([g_ref[0, i, :rows], g_ref[1, i, :rows]], axis=0)
    return lax.dot_general(both, block, (((1,), (1,)), ((), ())), preferred_element_type=jnp.float32)


def near_back_kernel(place, g_ref, half_ref, w_ref, acc_ref, next_ref, sems):
    copies = halves(w_ref, next_ref, sems, place[2])
    for copy in copies:
        copy.start()
    acc = back_block(g_ref, half_ref[0], 0)
    for i in range(1, LINE):
        acc = acc + back_block(g_ref, half_ref[i], i)
    acc_ref[...] = acc
    for copy in copies:
        copy.wait()


def near_back(place, g, half, w):
    _, _, high, width = g.shape
    rows = high - 8
    return pl.pallas_call(
        near_back_kernel,
        out_shape=(pltpu.VMEM((2 * rows, width), jnp.float32), pltpu.VMEM(half_shape(w), w.dtype)),
        in_specs=[SMEM_SPEC, VMEM_SPEC, VMEM_SPEC, HBM_SPEC],
        out_specs=(VMEM_SPEC, VMEM_SPEC),
        scratch_shapes=[SEMS],
        compiler_params=pltpu.CompilerParams(vmem_limit_bytes=VMEM),
        cost_estimate=cost(2 * 2 * rows * width * width * LINE, width * width * LINE * 2),
    )(place, g, in_vmem(half), in_hbm(w))


def far_back_kernel(place, g_ref, near_ref, half_ref, acc_ref, back_ref, send_ref, keep_ref, bias_ref, sum_ref):
    rows, width = keep_ref.shape
    acc = acc_ref[...]
    for i in range(LINE):
        acc = acc + back_block(g_ref, half_ref[i], i)
    sum_ref[0] = acc[:rows]
    sum_ref[1] = acc[rows:]
    own = place[0]
    keep_ref[...] = sum_ref[own]
    send_ref[0:rows] = sum_ref[1 - own].astype(jnp.bfloat16)
    bias = []
    for k in range(2):
        lines = jnp.zeros((8, width), jnp.float32)
        for i in range(LINE):
            lines = lines + g_ref[k, i, rows : rows + 8].astype(jnp.float32)
            lines = lines + near_ref[k, i, rows : rows + 8].astype(jnp.float32)
        bias.append(jnp.sum(lines, axis=0, keepdims=True))
    first = own == 0
    bias_ref[...] = jnp.broadcast_to(jnp.where(first, bias[0], bias[1]), bias_ref.shape)
    send_ref[rows : rows + 8] = jnp.broadcast_to(jnp.where(first, bias[1], bias[0]), (8, width)).astype(jnp.bfloat16)
    send_ref[rows + 8 :] = back_ref[rows:]


def far_back(place, g, near, half, acc, back):
    _, _, high, width = g.shape
    rows = high - 8
    return pl.pallas_call(
        far_back_kernel,
        out_shape=(
            jax.ShapeDtypeStruct((back.shape[0] + 8, width), jnp.bfloat16),
            jax.ShapeDtypeStruct((rows, width), jnp.float32),
            jax.ShapeDtypeStruct((8, width), jnp.float32),
        ),
        in_specs=[SMEM_SPEC] + [VMEM_SPEC] * 5,
        out_specs=(VMEM_SPEC,) * 3,
        scratch_shapes=[pltpu.VMEM((2, rows, width), jnp.float32)],
        compiler_params=pltpu.CompilerParams(vmem_limit_bytes=VMEM),
        cost_estimate=cost(2 * 2 * rows * width * width * LINE, width * width * LINE * 2),
    )(place, in_vmem(g), in_vmem(near), in_vmem(half), in_vmem(acc), back)


def step(coeff, weight, upper_bound, lower_depth, slopes, state, adjoint):
    nboxes, nspecs, width = coeff.shape
    rows = nboxes * nspecs
    s = lax.axis_index("spec").astype(jnp.int32)
    core = lax.axis_index("neuron").astype(jnp.int32) % 2
    near = jnp.stack([s, core, 1 - core])
    far = jnp.stack([s, 1 - core, core])

    other = lax.ppermute(coeff, "spec", SPEC_SWAP)
    both = jnp.stack([coeff.reshape(rows, width), other.reshape(rows, width)])

    unstable = state == 2
    total = upper_bound + lower_depth
    one = jnp.where(state == 1, 1.0, 0.0)
    a = jnp.where(unstable, slopes, one)
    b = jnp.where(unstable, upper_bound / total, one)
    c = jnp.where(unstable, upper_bound * lower_depth / total, 0.0)
    abc = jnp.concatenate([a, b, c], axis=0)
    adj = adjoint.reshape(rows, width)

    half = stage(far, weight)
    away = part_sums(far, both, half, True).astype(jnp.float16)
    came = lax.ppermute(away, "neuron", CORE_SWAP)
    kept = part_sums(near, both, weight, False)
    chunks = (kept + came.astype(jnp.float32)).astype(jnp.float16)

    chunks, abc, adj = lax.optimization_barrier((chunks, abc, adj))
    sums = lax.all_to_all(chunks, "neuron", 0, 0, axis_index_groups=SAME_CORE, tiled=True)
    abc = lax.ppermute(abc, BOTH, MIDDLE_SWAP)
    adj = lax.ppermute(adj, BOTH, MIDDLE_SWAP)
    abc = jnp.broadcast_to(
        abc.reshape(3, nboxes, 1, width), (3, nboxes, nspecs, width)
    ).reshape(3, rows, width)

    pre = jnp.sum(sums.astype(jnp.float32), axis=0) * (1.0 / SCALE)
    grad, back = middle(pre, abc[0], abc[1], abc[2], adj)

    grads = lax.all_to_all(grad, "neuron", 0, 0, axis_index_groups=SAME_CORE, tiled=True)
    back = lax.ppermute(back, BOTH, MIDDLE_SWAP)
    half = stage(near, weight)
    grads, new_coeff = lax.optimization_barrier((grads, back[:rows].reshape(nboxes, nspecs, width)))

    far_grads = lax.ppermute(grads, "neuron", CORE_SWAP)
    grads = grads.reshape(2, LINE, rows + 8, width)
    near_part, other_half = near_back(near, grads, half, weight)
    send, mine, bias = far_back(near, far_grads.reshape(grads.shape), grads, other_half, near_part, back)
    recv = lax.ppermute(send, "spec", SPEC_SWAP)

    coeff_grad = (mine + recv[:rows].astype(jnp.float32)).astype(jnp.bfloat16)
    offset = bias[0, :rows] + recv[rows, :rows].astype(jnp.float32)
    slope_grad = back[rows:].astype(jnp.float32) + recv[rows + 8 :].astype(jnp.float32)
    return (
        new_coeff,
        offset.reshape(nboxes, nspecs),
        slope_grad,
        coeff_grad.reshape(nboxes, nspecs, width),
    )


def solution(mesh):
    return jax.shard_map(
        step,
        mesh=mesh,
        in_specs=(
            P("box", "spec", "neuron"),
            P("neuron", "spec"),
            P("box", "neuron"),
            P("box", "neuron"),
            P("box", "neuron"),
            P("box", "neuron"),
            P("box", "spec", "neuron"),
        ),
        out_specs=(
            P("box", "spec", "neuron"),
            P("box", "spec"),
            P("box", "neuron"),
            P("box", "spec", "neuron"),
        ),
        check_vma=False,
    )
```

profile of v0, /device:TPU:1, one launch (start us, length us, event | category | flops | bytes accessed | tf_op | source)
XLA Modules:
  0.0 77.9 jit_solution(3573067177879677838)
XLA Ops:
  0.6 5.6 %collective-permute-start = (bf16[24,4,512]{2,1,0:T(4,128)(2,1)}, bf16[24,4,512]{2,1,0:T(4,128)(2,1)S(1)}, u32[]{:S(2)}, u32[]{:S(2)}) collective-permute-start(bf16[24,4,512]{2,1,0:T(4,128)(2,1)} %param.7), channel_id=1, source_target_pairs={{0,1},{1,0},{2,3},{3,2},{4,5},{5,4},{6,7},{7,6},{8,9},{9,8},{10,11... | collective-permute-start | bytes 294920 | tf_op jit(solution)/shard_map/ppermute | solution.py:254
  6.3 0.9 %stack_reshape.6 = bf16[1,96,512]{2,1,0:T(8,128)(2,1)S(1)} reshape(bf16[24,4,512]{2,1,0:T(4,128)(2,1)} %param.7) | data formatting | bytes 196608 | tf_op jit(solution)/shard_map/stack;reshape | solution.py:255
  7.3 2.1 %shard_map.103.half_ref = bf16[4,512,512]{2,1,0:T(8,128)(2,1)S(1)} custom-call(s32[3]{0:T(128)S(1)} %pad_add_fusion.1.place, bf16[512,4096]{1,0:T(8,128)(2,1)} %w_ref.7), custom_call_target="tpu_custom_call" | custom-call | bytes 4194304 | tf_op jit(solution)/shard_map/pallas_call | solution.py:75
  9.5 1.1 %shard_map.104 = f32[8,96,512]{2,1,0:T(8,128)S(1)} custom-call(s32[3]{0:T(128)S(1)} %pad_add_fusion.1.place, bf16[2,96,512]{2,1,0:T(8,128)(2,1)S(1)} %constant_dynamic-update-slice_fusion.x_ref, bf16[4,512,512]{2,1,0:T(8,128)(2,1)S(1)} %shard_map.103.half_ref), custom_call_target="tpu_custom_call" | custom-call | flops 402653184 | bytes 2097152 | tf_op jit(solution)/shard_map/pallas_call | solution.py:111
  10.9 8.2 %collective-permute-start.1 = (f16[8,96,512]{2,1,0:T(8,128)(2,1)S(1)}, f16[8,96,512]{2,1,0:T(8,128)(2,1)S(1)}, u32[]{:S(2)}, u32[]{:S(2)}) collective-permute-start(f16[8,96,512]{2,1,0:T(8,128)(2,1)S(1)} %convert_element_type.29), channel_id=1, source_target_pairs={{0,32},{32,0},{64,96},{96,64},{128,160},{160,128},{192,224},{224,1... | collective-permute-start | bytes 2359304 | tf_op jit(solution)/shard_map/ppermute | solution.py:268
  19.3 2.7 %shard_map.102 = f32[8,96,512]{2,1,0:T(8,128)S(1)} custom-call(s32[3]{0:T(128)S(1)} %pad_add_fusion.place, bf16[2,96,512]{2,1,0:T(8,128)(2,1)S(1)} %constant_dynamic-update-slice_fusion.x_ref, bf16[512,4096]{1,0:T(8,128)(2,1)} %w_ref.7), custom_call_target="tpu_custom_call" | custom-call | flops 402653184 | bytes 2097152 | tf_op jit(solution)/shard_map/pallas_call | solution.py:111
  22.0 1.2 %add_convert_fusion = f16[8,96,512]{2,1,0:T(8,128)(2,1)} fusion(f32[8,96,512]{2,1,0:T(8,128)S(1)} %shard_map.102, f16[8,96,512]{2,1,0:T(8,128)(2,1)S(1)} %collective-permute-done.1), kind=kLoop, calls=%fused_computation.1 | loop fusion | flops 1179648 | bytes 3145728 | tf_op jit(solution)/shard_map/convert_element_type | solution.py:270
  23.2 3.5 %all-to-all-start = ((f16[8,96,512]{2,1,0:T(8,128)(2,1)}), f16[8,96,512]{2,1,0:T(8,128)(2,1)S(1)}, u32[]{:S(2)}, u32[]{:S(2)}) async-start(f16[8,96,512]{2,1,0:T(8,128)(2,1)} %add_convert_fusion), calls=%async_computation | async-start | bytes 1572864 | tf_op jit(solution)/shard_map/all_to_all | solution.py:273
  26.7 0.7 collective-permute-start.2
  27.4 0.7 collective-permute-start.3
  28.5 11.3 %all-to-all-done = f16[8,96,512]{2,1,0:T(8,128)(2,1)S(1)} async-done(((f16[8,96,512]{2,1,0:T(8,128)(2,1)}), f16[8,96,512]{2,1,0:T(8,128)(2,1)S(1)}, u32[]{:S(2)}, u32[]{:S(2)}) %all-to-all-start) | async-done | bytes 786464 | tf_op jit(solution)/shard_map/all_to_all | solution.py:273
  39.9 1.3 %shard_map.105 = (bf16[8,104,512]{2,1,0:T(8,128)(2,1)}, bf16[120,512]{1,0:T(8,128)(2,1)S(1)}) custom-call(f32[96,512]{1,0:T(8,128)S(1)} %broadcast_multiply_fusion.r_ref, f32[96,512]{1,0:T(8,128)S(1)} %broadcast_in_dim.28.a_ref, f32[96,512]{1,0:T(8,128)S(1)} %broadcast_in_dim.30.b_ref, f32[96,512]{1,0:T(8,128)S(1)} %broadcast_in_dim.32.c_ref, ...), custom_call_target="tpu_custom_call" | custom-call | flops 1474560 | bytes 1572864 | tf_op jit(solution)/shard_map/pallas_call | solution.py:162
  41.2 3.5 %all-to-all-start.1 = ((bf16[8,104,512]{2,1,0:T(8,128)(2,1)}), bf16[8,104,512]{2,1,0:T(8,128)(2,1)S(1)}, u32[]{:S(2)}, u32[]{:S(2)}) async-start(bf16[8,104,512]{2,1,0:T(8,128)(2,1)} %get-tuple-element.19), calls=%async_computation.1 | async-start | bytes 1703936 | tf_op jit(solution)/shard_map/all_to_all | solution.py:283
  44.8 0.7 collective-permute-start.4
  45.5 0.7 reshape.44
  46.1 12.3 %all-to-all-done.1 = bf16[8,104,512]{2,1,0:T(8,128)(2,1)S(1)} async-done(((bf16[8,104,512]{2,1,0:T(8,128)(2,1)}), bf16[8,104,512]{2,1,0:T(8,128)(2,1)S(1)}, u32[]{:S(2)}, u32[]{:S(2)}) %all-to-all-start.1) | async-done | bytes 852000 | tf_op jit(solution)/shard_map/all_to_all | solution.py:283
  58.5 2.7 %collective-permute-start.5 = (bf16[8,104,512]{2,1,0:T(8,128)(2,1)S(1)}, bf16[8,104,512]{2,1,0:T(8,128)(2,1)S(1)}, u32[]{:S(2)}, u32[]{:S(2)}) collective-permute-start(bf16[8,104,512]{2,1,0:T(8,128)(2,1)S(1)} %all-to-all-done.1), channel_id=1, source_target_pairs={{0,32},{32,0},{64,96},{96,64},{128,160},{160,128},{192,224},{224,1... | collective-permute-start | bytes 2555912 | tf_op jit(solution)/shard_map/ppermute | solution.py:288
  61.2 2.1 %shard_map.106.half_ref = bf16[4,512,512]{2,1,0:T(8,128)(2,1)S(1)} custom-call(s32[3]{0:T(128)S(1)} %pad_add_fusion.place, bf16[512,4096]{1,0:T(8,128)(2,1)} %w_ref.7), custom_call_target="tpu_custom_call" | custom-call | bytes 4194304 | tf_op jit(solution)/shard_map/pallas_call | solution.py:75
  63.3 2.7 %shard_map.107 = (f32[192,512]{1,0:T(8,128)S(1)}, bf16[4,512,512]{2,1,0:T(8,128)(2,1)S(1)}) custom-call(s32[3]{0:T(128)S(1)} %pad_add_fusion.place, bf16[2,4,104,512]{3,2,1,0:T(8,128)(2,1)S(1)} %bitcast.5, bf16[4,512,512]{2,1,0:T(8,128)(2,1)S(1)} %shard_map.106.half_ref, bf16[512,4096]{1,0:T(8,128)(2,1)} %w_ref.7), custom_call_target="tpu_custom_call" | custom-call | flops 402653184 | bytes 2097152 | tf_op jit(solution)/shard_map/pallas_call | solution.py:194
  66.0 1.4 %shard_map.108 = (bf16[128,512]{1,0:T(8,128)(2,1)S(1)}, f32[96,512]{1,0:T(8,128)S(1)}, f32[8,512]{1,0:T(8,128)S(1)}) custom-call(s32[3]{0:T(128)S(1)} %pad_add_fusion.place, bf16[2,4,104,512]{3,2,1,0:T(8,128)(2,1)S(1)} %bitcast.7, bf16[2,4,104,512]{3,2,1,0:T(8,128)(2,1)S(1)} %bitcast.6, bf16[4,512,512]{2,1,0:T(8,128)(2,1)S(1)} %get-tuple-element.23.half_ref, ...), custom_call_target="tpu_custom_call" | custom-call | flops 402653184 | bytes 2097152 | tf_op jit(solution)/shard_map/pallas_call | solution.py:231
  67.4 2.0 %collective-permute-start.6 = (bf16[128,512]{1,0:T(8,128)(2,1)S(1)}, bf16[128,512]{1,0:T(8,128)(2,1)S(1)}, u32[]{:S(2)}, u32[]{:S(2)}) collective-permute-start(bf16[128,512]{1,0:T(8,128)(2,1)S(1)} %get-tuple-element.26), channel_id=1, source_target_pairs={{0,1},{1,0},{2,3},{3,2},{4,5},{5,4},{6,7},{7,6},{8,9},{9,8},{10,11... | collective-permute-start | bytes 393224 | tf_op jit(solution)/shard_map/ppermute | solution.py:292
  69.4 6.4 %collective-permute-done.6 = bf16[128,512]{1,0:T(8,128)(2,1)S(1)} collective-permute-done((bf16[128,512]{1,0:T(8,128)(2,1)S(1)}, bf16[128,512]{1,0:T(8,128)(2,1)S(1)}, u32[]{:S(2)}, u32[]{:S(2)}) %collective-permute-start.6) | collective-permute-done | bytes 131104 | tf_op jit(solution)/shard_map/ppermute | solution.py:292
  75.9 0.7 reshape.47
  76.7 0.7 copy.12
  (40 shorter events, 1.7 us)
Async XLA Ops:
  0.6 8.8 %collective-permute-start = (bf16[24,4,512]{2,1,0:T(4,128)(2,1)}, bf16[24,4,512]{2,1,0:T(4,128)(2,1)S(1)}, u32[]{:S(2)}, u32[]{:S(2)}) collective-permute-start(bf16[24,4,512]{2,1,0:T(4,128)(2,1)} %param.7), channel_id=1, source_target_pairs={{0,1},{1,0},{2,3},{3,2},{4,5},{5,4},{6,7},{7,6},{8,9},{9,8},{10,11... | collective-permute-start | bytes 294920 | tf_op jit(solution)/shard_map/ppermute | solution.py:254
  10.6 8.4 %copy-start = (bf16[24,4,512]{2,1,0:T(4,128)(2,1)S(1)}, bf16[24,4,512]{2,1,0:T(4,128)(2,1)}, u32[]{:S(2)}) copy-start(bf16[24,4,512]{2,1,0:T(4,128)(2,1)} %param.13) | copy-start | bytes 294916
  10.6 8.5 %copy-start.3 = (f32[24,512]{1,0:T(8,128)S(1)}, f32[24,512]{1,0:T(8,128)}, u32[]{:S(2)}) copy-start(f32[24,512]{1,0:T(8,128)} %param.11) | copy-start | bytes 147460
  10.6 8.5 %copy-start.4 = (s32[24,512]{1,0:T(8,128)S(1)}, s32[24,512]{1,0:T(8,128)}, u32[]{:S(2)}) copy-start(s32[24,512]{1,0:T(8,128)} %param.12) | copy-start | bytes 147460
  10.7 8.5 %copy-start.1 = (f32[24,512]{1,0:T(8,128)S(1)}, f32[24,512]{1,0:T(8,128)}, u32[]{:S(2)}) copy-start(f32[24,512]{1,0:T(8,128)} %param.9) | copy-start | bytes 147460
  10.7 8.5 %copy-start.2 = (f32[24,512]{1,0:T(8,128)S(1)}, f32[24,512]{1,0:T(8,128)}, u32[]{:S(2)}) copy-start(f32[24,512]{1,0:T(8,128)} %param.10) | copy-start | bytes 147460
  10.9 11.1 %collective-permute-start.1 = (f16[8,96,512]{2,1,0:T(8,128)(2,1)S(1)}, f16[8,96,512]{2,1,0:T(8,128)(2,1)S(1)}, u32[]{:S(2)}, u32[]{:S(2)}) collective-permute-start(f16[8,96,512]{2,1,0:T(8,128)(2,1)S(1)} %convert_element_type.29), channel_id=1, source_target_pairs={{0,32},{32,0},{64,96},{96,64},{128,160},{160,128},{192,224},{224,1... | collective-permute-start | bytes 2359304 | tf_op jit(solution)/shard_map/ppermute | solution.py:268
  23.2 16.6 %all-to-all-start = ((f16[8,96,512]{2,1,0:T(8,128)(2,1)}), f16[8,96,512]{2,1,0:T(8,128)(2,1)S(1)}, u32[]{:S(2)}, u32[]{:S(2)}) async-start(f16[8,96,512]{2,1,0:T(8,128)(2,1)} %add_convert_fusion), calls=%async_computation | async-start | bytes 1572864 | tf_op jit(solution)/shard_map/all_to_all | solution.py:273
  26.7 1.4 %collective-permute-start.2 = (f32[72,512]{1,0:T(8,128)S(1)}, f32[72,512]{1,0:T(8,128)S(1)}, u32[]{:S(2)}, u32[]{:S(2)}) collective-permute-start(f32[72,512]{1,0:T(8,128)S(1)} %pad_maximum_fusion), channel_id=1, source_target_pairs={{0,0},{1,256},{32,32},{33,288},{64,64},{65,320},{96,96},{97,352},{... | collective-permute-start | bytes 442376 | tf_op jit(solution)/shard_map/ppermute | solution.py:274
  27.4 12.5 %collective-permute-start.3 = (bf16[96,512]{1,0:T(8,128)(2,1)S(1)}, bf16[96,512]{1,0:T(8,128)(2,1)S(1)}, u32[]{:S(2)}, u32[]{:S(2)}) collective-permute-start(bf16[96,512]{1,0:T(8,128)(2,1)S(1)} %reshape.43), channel_id=1, source_target_pairs={{0,0},{1,256},{32,32},{33,288},{64,64},{65,320},{96,96},{97,352},{... | collective-permute-start | bytes 294920 | tf_op jit(solution)/shard_map/ppermute | solution.py:275
  41.2 17.3 %all-to-all-start.1 = ((bf16[8,104,512]{2,1,0:T(8,128)(2,1)}), bf16[8,104,512]{2,1,0:T(8,128)(2,1)S(1)}, u32[]{:S(2)}, u32[]{:S(2)}) async-start(bf16[8,104,512]{2,1,0:T(8,128)(2,1)} %get-tuple-element.19), calls=%async_computation.1 | async-start | bytes 1703936 | tf_op jit(solution)/shard_map/all_to_all | solution.py:283
  44.8 0.7 collective-permute-start.4
  58.5 7.5 %collective-permute-start.5 = (bf16[8,104,512]{2,1,0:T(8,128)(2,1)S(1)}, bf16[8,104,512]{2,1,0:T(8,128)(2,1)S(1)}, u32[]{:S(2)}, u32[]{:S(2)}) collective-permute-start(bf16[8,104,512]{2,1,0:T(8,128)(2,1)S(1)} %all-to-all-done.1), channel_id=1, source_target_pairs={{0,32},{32,0},{64,96},{96,64},{128,160},{160,128},{192,224},{224,1... | collective-permute-start | bytes 2555912 | tf_op jit(solution)/shard_map/ppermute | solution.py:288
  67.4 8.4 %collective-permute-start.6 = (bf16[128,512]{1,0:T(8,128)(2,1)S(1)}, bf16[128,512]{1,0:T(8,128)(2,1)S(1)}, u32[]{:S(2)}, u32[]{:S(2)}) collective-permute-start(bf16[128,512]{1,0:T(8,128)(2,1)S(1)} %get-tuple-element.26), channel_id=1, source_target_pairs={{0,1},{1,0},{2,3},{3,2},{4,5},{5,4},{6,7},{7,6},{8,9},{9,8},{10,11... | collective-permute-start | bytes 393224 | tf_op jit(solution)/shard_map/ppermute | solution.py:292
where the time goes:
time: 78.5 us; the launch traced here: 77.9 us
  waiting for transfers between devices  30 us (38%)
  starting transfers between devices  27.6 us (35%)
  Pallas kernels  13.5 us (17%)
  local copies, waits for them, and re-layouts  3.45 us (4%)
  other arithmetic  2.41 us (3%)
  between operations  1.02 us (1%)
    all_to_all x1, waiting for transfers between devices, step(): lax.all_to_all(grad, 'neuron', 0, 0, axis_index_groups=SAME_CORE, tiled=T...  12.3 us
    all_to_all x1, waiting for transfers between devices, step(): lax.all_to_all(chunks, 'neuron', 0, 0, axis_index_groups=SAME_CORE, tiled...  11.3 us
    ppermute x1, starting transfers between devices, step(): came = lax.ppermute(away, 'neuron', CORE_SWAP)  8.16 us
    ppermute x1, waiting for transfers between devices, step(): recv = lax.ppermute(send, 'spec', SPEC_SWAP)  6.42 us
    ppermute x1, starting transfers between devices, step(): other = lax.ppermute(coeff, 'spec', SPEC_SWAP)  5.64 us
    pallas_call x2, Pallas kernels, stage(): pl.pallas_call(stage_kernel, out_shape=pltpu.VMEM(half_shape(w), w.dtype)...  4.21 us
    pallas_call x2, Pallas kernels, part_sums(): pl.pallas_call(near_kernel if staged else far_kernel, out_shape=jax.Shape...  3.82 us
    all_to_all x1, starting transfers between devices, step(): lax.all_to_all(grad, 'neuron', 0, 0, axis_index_groups=SAME_CORE, tiled=T...  3.55 us
  transfers between devices with their start and end apart: 9, of which 3 were waited for; matrix products, arithmetic and copies ran while one was open for 3% of the time, Pallas kernels for 12%

commit v1 on v0

--- a/solution.py
+++ b/solution.py
@@ -31,22 +31,53 @@
 MIDDLE_SWAP = middle_swap()
 
 
-def halves(w_ref, buf_ref, sems, core):
-    width = buf_ref.shape[2]
+PIECES = 2
+
+
+def halves(w_ref, buf_ref, sems, core, first=0):
+    count, _, width = buf_ref.shape
+    tall = width // PIECES
     return [
-        pltpu.make_async_copy(
-            w_ref.at[:, pl.ds(pl.multiple_of((2 * i + core) * width, width), width)], buf_ref.at[i], sems.at[i]
-        )
-        for i in range(LINE)
+        [
+            pltpu.make_async_copy(
+                columns(w_ref, first + i, core).at[pl.ds(p * tall, tall)],
+                buf_ref.at[i, pl.ds(p * tall, tall)],
+                sems.at[i, p],
+            )
+            for p in range(PIECES)
+        ]
+        for i in range(count)
     ]
+
+
+def columns(w_ref, i, core):
+    width = w_ref.shape[0]
+    return w_ref.at[:, pl.ds(pl.multiple_of((2 * i + core) * width, width), width)]
+
+
+def start(copies):
+    for pieces in copies:
+        for piece in pieces:
+            piece.start()
+
+
+def wait(pieces):
+    for piece in pieces:
+        piece.wait()
 
 
 def stage_kernel(place, w_ref, out_ref, sems):
     copies = halves(w_ref, out_ref, sems, place[1])
-    for copy in copies:
-        copy.start()
-    for copy in copies:
-        copy.wait()
+    start(copies)
+    for pieces in copies:
+        wait(pieces)
+
+
+def stage_more_kernel(place, w_ref, out_ref, more_ref, sems, more_sems):
+    copies = halves(w_ref, out_ref, sems, place[1]) + halves(w_ref, more_ref, more_sems, place[2])
+    start(copies)
+    for pieces in copies:
+        wait(pieces)
 
 
 def in_hbm(w):
@@ -60,7 +91,7 @@
 SMEM_SPEC = pl.BlockSpec(memory_space=pltpu.SMEM)
 VMEM_SPEC = pl.BlockSpec(memory_space=pltpu.VMEM)
 HBM_SPEC = pl.BlockSpec(memory_space=pltpu.HBM)
-SEMS = pltpu.SemaphoreType.DMA((LINE,))
+SEMS = pltpu.SemaphoreType.DMA((LINE, PIECES))
 
 
 def half_shape(w):
@@ -71,13 +102,15 @@
     return pl.CostEstimate(flops=flops, bytes_accessed=moved, transcendentals=0)
 
 
-def stage(place, w):
-    return pl.pallas_call(
-        stage_kernel,
-        out_shape=pltpu.VMEM(half_shape(w), w.dtype),
+def stage(place, w, more):
+    block = (1, w.shape[0], w.shape[0])
+    half = pltpu.VMEM(half_shape(w), w.dtype)
+    return pl.pallas_call(
+        stage_more_kernel if more else stage_kernel,
+        out_shape=(half, pltpu.VMEM(block, w.dtype)) if more else half,
         in_specs=[SMEM_SPEC, HBM_SPEC],
-        out_specs=VMEM_SPEC,
-        scratch_shapes=[SEMS],
+        out_specs=(VMEM_SPEC, VMEM_SPEC) if more else VMEM_SPEC,
+        scratch_shapes=[SEMS, SEMS] if more else [SEMS],
         compiler_params=pltpu.CompilerParams(vmem_limit_bytes=VMEM),
         cost_estimate=cost(0, w.size * 2),
     )(place, in_hbm(w))
@@ -97,26 +130,38 @@
         part_block(place, x_ref, half_ref[i], out_ref, i)
 
 
-def far_kernel(place, x_ref, w_ref, out_ref, buf_ref, sems):
-    copies = halves(w_ref, buf_ref, sems, place[1])
-    for copy in copies:
-        copy.start()
-    for i in range(LINE):
-        copies[i].wait()
-        part_block(place, x_ref, buf_ref[i], out_ref, i)
-
-
-def part_sums(place, x, w, staged):
+def near_sums(place, x, half):
     rows, width = x.shape[1:]
     return pl.pallas_call(
-        near_kernel if staged else far_kernel,
+        near_kernel,
         out_shape=jax.ShapeDtypeStruct((CHIPS, rows, width), jnp.float32),
-        in_specs=[SMEM_SPEC, VMEM_SPEC, VMEM_SPEC if staged else HBM_SPEC],
+        in_specs=[SMEM_SPEC, VMEM_SPEC, VMEM_SPEC],
         out_specs=VMEM_SPEC,
-        scratch_shapes=[] if staged else [pltpu.VMEM(half_shape(w), w.dtype), SEMS],
         compiler_params=pltpu.CompilerParams(vmem_limit_bytes=VMEM),
         cost_estimate=cost(2 * 2 * rows * width * width * LINE, width * width * LINE * 2),
-    )(place, x, in_vmem(w) if staged else in_hbm(w))
+    )(place, x, in_vmem(half))
+
+
+def far_kernel(place, x_ref, first_ref, w_ref, out_ref, buf_ref, sems):
+    copies = halves(w_ref, buf_ref, sems, place[1], 1)
+    start(copies)
+    part_block(place, x_ref, first_ref[0], out_ref, 0)
+    for i in range(1, LINE):
+        wait(copies[i - 1])
+        part_block(place, x_ref, buf_ref[i - 1], out_ref, i)
+
+
+def far_sums(place, x, first, w):
+    rows, width = x.shape[1:]
+    return pl.pallas_call(
+        far_kernel,
+        out_shape=jax.ShapeDtypeStruct((CHIPS, rows, width), jnp.float32),
+        in_specs=[SMEM_SPEC, VMEM_SPEC, VMEM_SPEC, HBM_SPEC],
+        out_specs=VMEM_SPEC,
+        scratch_shapes=[pltpu.VMEM((LINE - 1, width, width), w.dtype), SEMS],
+        compiler_params=pltpu.CompilerParams(vmem_limit_bytes=VMEM),
+        cost_estimate=cost(2 * 2 * rows * width * width * LINE, width * width * LINE * 2),
+    )(place, x, in_vmem(first), in_hbm(w))
 
 
 def middle_kernel(r_ref, a_ref, b_ref, c_ref, adj_ref, g_ref, back_ref):
@@ -170,22 +215,22 @@
     )(r, a, b, c, adj)
 
 
-def back_block(g_ref, block, i):
-    rows = g_ref.shape[2] - 8
-    both = jnp.concatenate([g_ref[0, i, :rows], g_ref[1, i, :rows]], axis=0)
-    return lax.dot_general(both, block, (((1,), (1,)), ((), ())), preferred_element_type=jnp.float32)
+def against(g, block):
+    return lax.dot_general(g, block, (((1,), (1,)), ((), ())), preferred_element_type=jnp.float32)
 
 
 def near_back_kernel(place, g_ref, half_ref, w_ref, acc_ref, next_ref, sems):
     copies = halves(w_ref, next_ref, sems, place[2])
-    for copy in copies:
-        copy.start()
-    acc = back_block(g_ref, half_ref[0], 0)
-    for i in range(1, LINE):
-        acc = acc + back_block(g_ref, half_ref[i], i)
-    acc_ref[...] = acc
-    for copy in copies:
-        copy.wait()
+    start(copies)
+    rows = acc_ref.shape[1]
+    acc = None
+    for i in range(LINE):
+        part = against(jnp.concatenate([g_ref[0, i, :rows], g_ref[1, i, :rows]], axis=0), half_ref[i])
+        acc = part if acc is None else acc + part
+    acc_ref[0] = acc[:rows]
+    acc_ref[1] = acc[rows:]
+    for pieces in copies:
+        wait(pieces)
 
 
 def near_back(place, g, half, w):
@@ -193,25 +238,27 @@
     rows = high - 8
     return pl.pallas_call(
         near_back_kernel,
-        out_shape=(pltpu.VMEM((2 * rows, width), jnp.float32), pltpu.VMEM(half_shape(w), w.dtype)),
+        out_shape=(pltpu.VMEM((2, rows, width), jnp.float32), pltpu.VMEM(half_shape(w), w.dtype)),
         in_specs=[SMEM_SPEC, VMEM_SPEC, VMEM_SPEC, HBM_SPEC],
         out_specs=(VMEM_SPEC, VMEM_SPEC),
         scratch_shapes=[SEMS],
         compiler_params=pltpu.CompilerParams(vmem_limit_bytes=VMEM),
         cost_estimate=cost(2 * 2 * rows * width * width * LINE, width * width * LINE * 2),
-    )(place, g, in_vmem(half), in_hbm(w))
-
-
-def far_back_kernel(place, g_ref, near_ref, half_ref, acc_ref, back_ref, send_ref, keep_ref, bias_ref, sum_ref):
-    rows, width = keep_ref.shape
-    acc = acc_ref[...]
+    )(place, in_vmem(g), in_vmem(half), in_hbm(w))
+
+
+def far_rows(which, g_ref, half_ref, acc_ref):
+    rows = acc_ref.shape[1]
+    acc = acc_ref[which]
     for i in range(LINE):
-        acc = acc + back_block(g_ref, half_ref[i], i)
-    sum_ref[0] = acc[:rows]
-    sum_ref[1] = acc[rows:]
-    own = place[0]
-    keep_ref[...] = sum_ref[own]
-    send_ref[0:rows] = sum_ref[1 - own].astype(jnp.bfloat16)
+        acc = acc + against(g_ref[which, i, :rows], half_ref[i])
+    return acc
+
+
+def send_kernel(place, g_ref, near_ref, w_ref, acc_ref, back_ref, send_ref, bias_ref):
+    rows, width = acc_ref.shape[1:]
+    other = 1 - place[0]
+    send_ref[0:rows] = far_rows(other, g_ref, w_ref, acc_ref).astype(jnp.bfloat16)
     bias = []
     for k in range(2):
         lines = jnp.zeros((8, width), jnp.float32)
@@ -219,28 +266,82 @@
             lines = lines + g_ref[k, i, rows : rows + 8].astype(jnp.float32)
             lines = lines + near_ref[k, i, rows : rows + 8].astype(jnp.float32)
         bias.append(jnp.sum(lines, axis=0, keepdims=True))
-    first = own == 0
+    first = other == 1
     bias_ref[...] = jnp.broadcast_to(jnp.where(first, bias[0], bias[1]), bias_ref.shape)
     send_ref[rows : rows + 8] = jnp.broadcast_to(jnp.where(first, bias[1], bias[0]), (8, width)).astype(jnp.bfloat16)
     send_ref[rows + 8 :] = back_ref[rows:]
 
 
-def far_back(place, g, near, half, acc, back):
-    _, _, high, width = g.shape
-    rows = high - 8
-    return pl.pallas_call(
-        far_back_kernel,
+def send_rows(place, g, near, w, acc, back):
+    _, rows, width = acc.shape
+    return pl.pallas_call(
+        send_kernel,
         out_shape=(
             jax.ShapeDtypeStruct((back.shape[0] + 8, width), jnp.bfloat16),
-            jax.ShapeDtypeStruct((rows, width), jnp.float32),
             jax.ShapeDtypeStruct((8, width), jnp.float32),
         ),
         in_specs=[SMEM_SPEC] + [VMEM_SPEC] * 5,
+        out_specs=(VMEM_SPEC,) * 2,
+        compiler_params=pltpu.CompilerParams(vmem_limit_bytes=VMEM),
+        cost_estimate=cost(2 * rows * width * width * LINE, width * width * LINE * 2),
+    )(place, in_vmem(g), in_vmem(near), in_vmem(w), in_vmem(acc), back)
+
+
+def as_boxes(rows, like):
+    return rows.astype(jnp.float32).reshape(like.shape).astype(like.dtype)
+
+
+def keep_kernel(place, g_ref, w_ref, acc_ref, back_ref, keep_ref, relaxed_ref):
+    keep_ref[...] = far_rows(place[0], g_ref, w_ref, acc_ref)
+    relaxed_ref[...] = as_boxes(back_ref[: keep_ref.shape[0]], relaxed_ref)
+
+
+def keep_rows(place, g, w, acc, back, shape):
+    _, rows, width = acc.shape
+    return pl.pallas_call(
+        keep_kernel,
+        out_shape=(jax.ShapeDtypeStruct((rows, width), jnp.float32), jax.ShapeDtypeStruct(shape, jnp.bfloat16)),
+        in_specs=[SMEM_SPEC] + [VMEM_SPEC] * 4,
+        out_specs=(VMEM_SPEC,) * 2,
+        compiler_params=pltpu.CompilerParams(vmem_limit_bytes=VMEM),
+        cost_estimate=cost(2 * rows * width * width * LINE, width * width * LINE * 2),
+    )(place, in_vmem(g), in_vmem(w), in_vmem(acc), back)
+
+
+def finish_kernel(keep_ref, recv_ref, bias_ref, back_ref, grad_ref, offset_ref, slope_ref):
+    rows = keep_ref.shape[0]
+    boxes, specs, _ = grad_ref.shape
+    grad_ref[...] = as_boxes(keep_ref[...] + recv_ref[0:rows].astype(jnp.float32), grad_ref)
+    slope_ref[...] = back_ref[rows:].astype(jnp.float32) + recv_ref[rows + 8 :].astype(jnp.float32)
+    line = bias_ref[...] + recv_ref[rows : rows + 8].astype(jnp.float32)
+    line = line[:specs, :rows]
+    index = lax.broadcasted_iota(jnp.int32, (specs, rows), 1)
+    spec = lax.broadcasted_iota(jnp.int32, (specs, rows), 0)
+    box = lax.broadcasted_iota(jnp.int32, (rows, boxes), 0) // specs == lax.broadcasted_iota(
+        jnp.int32, (rows, boxes), 1
+    )
+    offset_ref[...] = jnp.dot(
+        jnp.where(index % specs == spec, line, 0.0),
+        jnp.where(box, 1.0, 0.0),
+        precision=lax.Precision.HIGHEST,
+        preferred_element_type=jnp.float32,
+    )
+
+
+def finish(keep, recv, bias, back, boxes):
+    rows, width = keep.shape
+    return pl.pallas_call(
+        finish_kernel,
+        out_shape=(
+            jax.ShapeDtypeStruct((boxes, rows // boxes, width), jnp.bfloat16),
+            jax.ShapeDtypeStruct((rows // boxes, boxes), jnp.float32),
+            jax.ShapeDtypeStruct((boxes, width), jnp.float32),
+        ),
+        in_specs=[VMEM_SPEC] * 4,
         out_specs=(VMEM_SPEC,) * 3,
-        scratch_shapes=[pltpu.VMEM((2, rows, width), jnp.float32)],
-        compiler_params=pltpu.CompilerParams(vmem_limit_bytes=VMEM),
-        cost_estimate=cost(2 * 2 * rows * width * width * LINE, width * width * LINE * 2),
-    )(place, in_vmem(g), in_vmem(near), in_vmem(half), in_vmem(acc), back)
+        compiler_params=pltpu.CompilerParams(vmem_limit_bytes=VMEM),
+        cost_estimate=cost(0, rows * width * 4),
+    )(keep, recv, bias, back)
 
 
 def step(coeff, weight, upper_bound, lower_depth, slopes, state, adjoint):
@@ -263,10 +364,10 @@
     abc = jnp.concatenate([a, b, c], axis=0)
     adj = adjoint.reshape(rows, width)
 
-    half = stage(far, weight)
-    away = part_sums(far, both, half, True).astype(jnp.float16)
+    half, first = stage(far, weight, True)
+    away = near_sums(far, both, half).astype(jnp.float16)
     came = lax.ppermute(away, "neuron", CORE_SWAP)
-    kept = part_sums(near, both, weight, False)
+    kept = far_sums(near, both, first, weight)
     chunks = (kept + came.astype(jnp.float32)).astype(jnp.float16)
 
     chunks, abc, adj = lax.optimization_barrier((chunks, abc, adj))
@@ -282,24 +383,18 @@
 
     grads = lax.all_to_all(grad, "neuron", 0, 0, axis_index_groups=SAME_CORE, tiled=True)
     back = lax.ppermute(back, BOTH, MIDDLE_SWAP)
-    half = stage(near, weight)
-    grads, new_coeff = lax.optimization_barrier((grads, back[:rows].reshape(nboxes, nspecs, width)))
+    half = stage(near, weight, False)
+    grads, back = lax.optimization_barrier((grads, back))
 
     far_grads = lax.ppermute(grads, "neuron", CORE_SWAP)
-    grads = grads.reshape(2, LINE, rows + 8, width)
-    near_part, other_half = near_back(near, grads, half, weight)
-    send, mine, bias = far_back(near, far_grads.reshape(grads.shape), grads, other_half, near_part, back)
+    four = (2, LINE, rows + 8, width)
+    grads, far_grads = grads.reshape(four), far_grads.reshape(four)
+    acc, other_half = near_back(near, grads, half, weight)
+    send, bias = send_rows(near, far_grads, grads, other_half, acc, back)
     recv = lax.ppermute(send, "spec", SPEC_SWAP)
-
-    coeff_grad = (mine + recv[:rows].astype(jnp.float32)).astype(jnp.bfloat16)
-    offset = bias[0, :rows] + recv[rows, :rows].astype(jnp.float32)
-    slope_grad = back[rows:].astype(jnp.float32) + recv[rows + 8 :].astype(jnp.float32)
-    return (
-        new_coeff,
-        offset.reshape(nboxes, nspecs),
-        slope_grad,
-        coeff_grad.reshape(nboxes, nspecs, width),
-    )
+    keep, new_coeff = keep_rows(near, far_grads, other_half, acc, back, coeff.shape)
+    coeff_grad, offset, slope_grad = finish(keep, recv, bias, back, nboxes)
+    return new_coeff, offset.T, slope_grad, coeff_grad
 
 
 def solution(mesh):

time: 78.5 us -> 77 us (0.981)
  Pallas kernels: 13.5 us -> 16.1 us
  local copies, waits for them, and re-layouts: 3.45 us -> 1.36 us
  waiting for transfers between devices: 30 us -> 28.6 us
    pallas_call x6 -> x8, Pallas kernels: 12.1 us -> 14.8 us  [the longest x2 4.5 us: stage(): pl.pallas_call(stage_more_kernel if more else stage_kernel, out_shape=(ha...]
    ppermute x1, waiting for transfers between devices: 6.42 us -> 4.3 us  [step(): recv = lax.ppermute(send, 'spec', SPEC_SWAP)]
    reshape x2 -> x0, local copies, waits for them, and re-layouts: 1.34 us -> none  [the longest x1 0.67 us: step(): coeff_grad.reshape(nboxes, nspecs, width)]
  transfers between devices with their start and end apart: 9 -> 9, of which waited for: 3 -> 3; matrix products, arithmetic and copies ran while one was open for 3% -> 2% of each run, Pallas kernels for 12% -> 15%
where the time goes in v1:
time: 77 us; the launch traced here: 76.4 us
  waiting for transfers between devices  28.6 us (37%)
  starting transfers between devices  27.6 us (36%)
  Pallas kernels  16.1 us (21%)
  other arithmetic  1.72 us (2%)
  local copies, waits for them, and re-layouts  1.36 us (2%)
  between operations  0.99 us (1%)
    all_to_all x1, waiting for transfers between devices, step(): lax.all_to_all(grad, 'neuron', 0, 0, axis_index_groups=SAME_CORE, tiled=T...  13 us
    all_to_all x1, waiting for transfers between devices, step(): lax.all_to_all(chunks, 'neuron', 0, 0, axis_index_groups=SAME_CORE, tiled...  11.3 us
    ppermute x1, starting transfers between devices, step(): came = lax.ppermute(away, 'neuron', CORE_SWAP)  7.9 us
    ppermute x1, starting transfers between devices, step(): other = lax.ppermute(coeff, 'spec', SPEC_SWAP)  5.64 us
    pallas_call x2, Pallas kernels, stage(): pl.pallas_call(stage_more_kernel if more else stage_kernel, out_shape=(ha...  4.5 us
    ppermute x1, waiting for transfers between devices, step(): recv = lax.ppermute(send, 'spec', SPEC_SWAP)  4.3 us
    all_to_all x1, starting transfers between devices, step(): lax.all_to_all(grad, 'neuron', 0, 0, axis_index_groups=SAME_CORE, tiled=T...  3.55 us
    all_to_all x1, starting transfers between devices, step(): lax.all_to_all(chunks, 'neuron', 0, 0, axis_index_groups=SAME_CORE, tiled...  3.55 us
  transfers between devices with their start and end apart: 9, of which 3 were waited for; matrix products, arithmetic and copies ran while one was open for 2% of the time, Pallas kernels for 15%

profile of v1, /device:TPU:1, one launch (start us, length us, event | category | flops | bytes accessed | tf_op | source)
XLA Modules:
  0.0 76.4 jit_solution(11899529012965825873)
XLA Ops:
  0.6 5.6 %collective-permute-start = (bf16[24,4,512]{2,1,0:T(4,128)(2,1)}, bf16[24,4,512]{2,1,0:T(4,128)(2,1)S(1)}, u32[]{:S(2)}, u32[]{:S(2)}) collective-permute-start(bf16[24,4,512]{2,1,0:T(4,128)(2,1)} %param.7), channel_id=1, source_target_pairs={{0,1},{1,0},{2,3},{3,2},{4,5},{5,4},{6,7},{7,6},{8,9},{9,8},{10,11... | collective-permute-start | bytes 294920 | tf_op jit(solution)/shard_map/ppermute | solution.py:355
  6.3 0.9 %stack_reshape.6 = bf16[1,96,512]{2,1,0:T(8,128)(2,1)S(1)} reshape(bf16[24,4,512]{2,1,0:T(4,128)(2,1)} %param.7) | data formatting | bytes 196608 | tf_op jit(solution)/shard_map/stack;reshape | solution.py:356
  7.3 2.4 %shard_map.102 = (bf16[4,512,512]{2,1,0:T(8,128)(2,1)S(1)}, bf16[1,512,512]{2,1,0:T(8,128)(2,1)S(1)}) custom-call(s32[3]{0:T(128)S(1)} %pad_add_fusion.1.place, bf16[512,4096]{1,0:T(8,128)(2,1)} %w_ref.7), custom_call_target="tpu_custom_call" | custom-call | bytes 4194304 | tf_op jit(solution)/shard_map/pallas_call | solution.py:108
  9.7 1.1 %shard_map.104 = f32[8,96,512]{2,1,0:T(8,128)S(1)} custom-call(s32[3]{0:T(128)S(1)} %pad_add_fusion.1.place, bf16[2,96,512]{2,1,0:T(8,128)(2,1)S(1)} %constant_dynamic-update-slice_fusion.x_ref, bf16[4,512,512]{2,1,0:T(8,128)(2,1)S(1)} %get-tuple-element.23.half_ref), custom_call_target="tpu_custom_call" | custom-call | flops 402653184 | bytes 2097152 | tf_op jit(solution)/shard_map/pallas_call | solution.py:135
  10.9 0.2 convert_element_type.12
  11.1 7.9 %collective-permute-start.1 = (f16[8,96,512]{2,1,0:T(8,128)(2,1)S(1)}, f16[8,96,512]{2,1,0:T(8,128)(2,1)S(1)}, u32[]{:S(2)}, u32[]{:S(2)}) collective-permute-start(f16[8,96,512]{2,1,0:T(8,128)(2,1)S(1)} %convert_element_type.12), channel_id=1, source_target_pairs={{0,32},{32,0},{64,96},{96,64},{128,160},{160,128},{192,224},{224,1... | collective-permute-start | bytes 2359304 | tf_op jit(solution)/shard_map/ppermute | solution.py:369
  19.3 2.5 %shard_map.103 = f32[8,96,512]{2,1,0:T(8,128)S(1)} custom-call(s32[3]{0:T(128)S(1)} %pad_add_fusion.place, bf16[2,96,512]{2,1,0:T(8,128)(2,1)S(1)} %constant_dynamic-update-slice_fusion.x_ref, bf16[1,512,512]{2,1,0:T(8,128)(2,1)S(1)} %get-tuple-element.22.first_ref, bf16[512,4096]{1,0:T(8,128)(2,1)} %w_ref.7), custom_call_target="tpu_custom_call" | custom-call | flops 402653184 | bytes 2097152 | tf_op jit(solution)/shard_map/pallas_call | solution.py:156
  21.8 1.2 %add_convert_fusion = f16[8,96,512]{2,1,0:T(8,128)(2,1)} fusion(f32[8,96,512]{2,1,0:T(8,128)S(1)} %shard_map.103, f16[8,96,512]{2,1,0:T(8,128)(2,1)S(1)} %collective-permute-done.1), kind=kLoop, calls=%fused_computation.1 | loop fusion | flops 1179648 | bytes 3145728 | tf_op jit(solution)/shard_map/convert_element_type | solution.py:371
  23.0 3.5 %all-to-all-start = ((f16[8,96,512]{2,1,0:T(8,128)(2,1)}), f16[8,96,512]{2,1,0:T(8,128)(2,1)S(1)}, u32[]{:S(2)}, u32[]{:S(2)}) async-start(f16[8,96,512]{2,1,0:T(8,128)(2,1)} %add_convert_fusion), calls=%async_computation | async-start | bytes 1572864 | tf_op jit(solution)/shard_map/all_to_all | solution.py:374
  26.5 0.7 collective-permute-start.2
  27.2 0.7 collective-permute-start.3
  28.3 11.3 %all-to-all-done = f16[8,96,512]{2,1,0:T(8,128)(2,1)S(1)} async-done(((f16[8,96,512]{2,1,0:T(8,128)(2,1)}), f16[8,96,512]{2,1,0:T(8,128)(2,1)S(1)}, u32[]{:S(2)}, u32[]{:S(2)}) %all-to-all-start) | async-done | bytes 786464 | tf_op jit(solution)/shard_map/all_to_all | solution.py:374
  39.7 1.3 %shard_map.105 = (bf16[8,104,512]{2,1,0:T(8,128)(2,1)}, bf16[120,512]{1,0:T(8,128)(2,1)S(1)}) custom-call(f32[96,512]{1,0:T(8,128)S(1)} %broadcast_multiply_fusion.r_ref, f32[96,512]{1,0:T(8,128)S(1)} %broadcast_in_dim.28.a_ref, f32[96,512]{1,0:T(8,128)S(1)} %broadcast_in_dim.30.b_ref, f32[96,512]{1,0:T(8,128)S(1)} %broadcast_in_dim.32.c_ref, ...), custom_call_target="tpu_custom_call" | custom-call | flops 1474560 | bytes 1572864 | tf_op jit(solution)/shard_map/pallas_call | solution.py:207
  41.0 3.5 %all-to-all-start.1 = ((bf16[8,104,512]{2,1,0:T(8,128)(2,1)}), bf16[8,104,512]{2,1,0:T(8,128)(2,1)S(1)}, u32[]{:S(2)}, u32[]{:S(2)}) async-start(bf16[8,104,512]{2,1,0:T(8,128)(2,1)} %get-tuple-element.27), calls=%async_computation.1 | async-start | bytes 1703936 | tf_op jit(solution)/shard_map/all_to_all | solution.py:384
  44.6 0.7 collective-permute-start.4
  45.3 13.0 %all-to-all-done.1 = bf16[8,104,512]{2,1,0:T(8,128)(2,1)S(1)} async-done(((bf16[8,104,512]{2,1,0:T(8,128)(2,1)}), bf16[8,104,512]{2,1,0:T(8,128)(2,1)S(1)}, u32[]{:S(2)}, u32[]{:S(2)}) %all-to-all-start.1) | async-done | bytes 852000 | tf_op jit(solution)/shard_map/all_to_all | solution.py:384
  58.3 2.7 %collective-permute-start.5 = (bf16[8,104,512]{2,1,0:T(8,128)(2,1)S(1)}, bf16[8,104,512]{2,1,0:T(8,128)(2,1)S(1)}, u32[]{:S(2)}, u32[]{:S(2)}) collective-permute-start(bf16[8,104,512]{2,1,0:T(8,128)(2,1)S(1)} %all-to-all-done.1), channel_id=1, source_target_pairs={{0,32},{32,0},{64,96},{96,64},{128,160},{160,128},{192,224},{224,1... | collective-permute-start | bytes 2555912 | tf_op jit(solution)/shard_map/ppermute | solution.py:389
  61.0 2.1 %shard_map.106.half_ref = bf16[4,512,512]{2,1,0:T(8,128)(2,1)S(1)} custom-call(s32[3]{0:T(128)S(1)} %pad_add_fusion.place, bf16[512,4096]{1,0:T(8,128)(2,1)} %w_ref.7), custom_call_target="tpu_custom_call" | custom-call | bytes 4194304 | tf_op jit(solution)/shard_map/pallas_call | solution.py:108
  63.1 2.7 %shard_map.107 = (f32[2,96,512]{2,1,0:T(8,128)S(1)}, bf16[4,512,512]{2,1,0:T(8,128)(2,1)S(1)}) custom-call(s32[3]{0:T(128)S(1)} %pad_add_fusion.place, bf16[2,4,104,512]{3,2,1,0:T(8,128)(2,1)S(1)} %bitcast.6, bf16[4,512,512]{2,1,0:T(8,128)(2,1)S(1)} %shard_map.106.half_ref, bf16[512,4096]{1,0:T(8,128)(2,1)} %w_ref.7), custom_call_target="tpu_custom_call" | custom-call | flops 402653184 | bytes 2097152 | tf_op jit(solution)/shard_map/pallas_call | solution.py:239
  65.9 1.3 %shard_map.109 = (bf16[128,512]{1,0:T(8,128)(2,1)S(1)}, f32[8,512]{1,0:T(8,128)S(1)}) custom-call(s32[3]{0:T(128)S(1)} %pad_add_fusion.place, bf16[2,4,104,512]{3,2,1,0:T(8,128)(2,1)S(1)} %bitcast.8, bf16[2,4,104,512]{3,2,1,0:T(8,128)(2,1)S(1)} %bitcast.7, bf16[4,512,512]{2,1,0:T(8,128)(2,1)S(1)} %get-tuple-element.30.w_ref, ...), custom_call_target="tpu_custom_call" | custom-call | flops 201326592 | bytes 2097152 | tf_op jit(solution)/shard_map/pallas_call | solution.py:277
  67.2 2.3 %collective-permute-start.6 = (bf16[128,512]{1,0:T(8,128)(2,1)S(1)}, bf16[128,512]{1,0:T(8,128)(2,1)S(1)}, u32[]{:S(2)}, u32[]{:S(2)}) collective-permute-start(bf16[128,512]{1,0:T(8,128)(2,1)S(1)} %get-tuple-element.35), channel_id=1, source_target_pairs={{0,1},{1,0},{2,3},{3,2},{4,5},{5,4},{6,7},{7,6},{8,9},{9,8},{10,11... | collective-permute-start | bytes 393224 | tf_op jit(solution)/shard_map/ppermute | solution.py:394
  69.5 1.9 %shard_map.108 = (f32[96,512]{1,0:T(8,128)S(1)}, bf16[24,4,512]{2,1,0:T(4,128)(2,1)}) custom-call(s32[3]{0:T(128)S(1)} %pad_add_fusion.place, bf16[2,4,104,512]{3,2,1,0:T(8,128)(2,1)S(1)} %bitcast.9, bf16[4,512,512]{2,1,0:T(8,128)(2,1)S(1)} %get-tuple-element.30.w_ref, f32[2,96,512]{2,1,0:T(8,128)S(1)} %get-tuple-element.31.acc_ref, ...), custom_call_target="tpu_custom_call" | custom-call | flops 201326592 | bytes 2097152 | tf_op jit(solution)/shard_map/pallas_call | solution.py:301
  71.3 4.3 %collective-permute-done.6.recv_ref = bf16[128,512]{1,0:T(8,128)(2,1)S(1)} collective-permute-done((bf16[128,512]{1,0:T(8,128)(2,1)S(1)}, bf16[128,512]{1,0:T(8,128)(2,1)S(1)}, u32[]{:S(2)}, u32[]{:S(2)}) %collective-permute-start.6) | collective-permute-done | bytes 131104 | tf_op jit(solution)/shard_map/ppermute | solution.py:394
  75.6 0.8 %shard_map.110 = (bf16[24,4,512]{2,1,0:T(4,128)(2,1)}, f32[4,24]{1,0:T(4,128)}, f32[24,512]{1,0:T(8,128)}) custom-call(f32[96,512]{1,0:T(8,128)S(1)} %get-tuple-element.34.keep_ref, bf16[128,512]{1,0:T(8,128)(2,1)S(1)} %collective-permute-done.6.recv_ref, f32[8,512]{1,0:T(8,128)S(1)} %get-tuple-element.36.bias_ref, ...), custom_call_target="tpu_custom_call" | custom-call | bytes 196608 | tf_op jit(solution)/shard_map/pallas_call | solution.py:333
  (34 shorter events, 0.8 us)
Async XLA Ops:
  0.6 9.1 %collective-permute-start = (bf16[24,4,512]{2,1,0:T(4,128)(2,1)}, bf16[24,4,512]{2,1,0:T(4,128)(2,1)S(1)}, u32[]{:S(2)}, u32[]{:S(2)}) collective-permute-start(bf16[24,4,512]{2,1,0:T(4,128)(2,1)} %param.7), channel_id=1, source_target_pairs={{0,1},{1,0},{2,3},{3,2},{4,5},{5,4},{6,7},{7,6},{8,9},{9,8},{10,11... | collective-permute-start | bytes 294920 | tf_op jit(solution)/shard_map/ppermute | solution.py:355
  10.9 8.2 %copy-start = (bf16[24,4,512]{2,1,0:T(4,128)(2,1)S(1)}, bf16[24,4,512]{2,1,0:T(4,128)(2,1)}, u32[]{:S(2)}) copy-start(bf16[24,4,512]{2,1,0:T(4,128)(2,1)} %param.13) | copy-start | bytes 294916
  10.9 8.3 %copy-start.3 = (f32[24,512]{1,0:T(8,128)S(1)}, f32[24,512]{1,0:T(8,128)}, u32[]{:S(2)}) copy-start(f32[24,512]{1,0:T(8,128)} %param.11) | copy-start | bytes 147460
  10.9 8.3 %copy-start.4 = (s32[24,512]{1,0:T(8,128)S(1)}, s32[24,512]{1,0:T(8,128)}, u32[]{:S(2)}) copy-start(s32[24,512]{1,0:T(8,128)} %param.12) | copy-start | bytes 147460
  10.9 8.3 %copy-start.1 = (f32[24,512]{1,0:T(8,128)S(1)}, f32[24,512]{1,0:T(8,128)}, u32[]{:S(2)}) copy-start(f32[24,512]{1,0:T(8,128)} %param.9) | copy-start | bytes 147460
  10.9 8.3 %copy-start.2 = (f32[24,512]{1,0:T(8,128)S(1)}, f32[24,512]{1,0:T(8,128)}, u32[]{:S(2)}) copy-start(f32[24,512]{1,0:T(8,128)} %param.10) | copy-start | bytes 147460
  11.1 10.7 %collective-permute-start.1 = (f16[8,96,512]{2,1,0:T(8,128)(2,1)S(1)}, f16[8,96,512]{2,1,0:T(8,128)(2,1)S(1)}, u32[]{:S(2)}, u32[]{:S(2)}) collective-permute-start(f16[8,96,512]{2,1,0:T(8,128)(2,1)S(1)} %convert_element_type.12), channel_id=1, source_target_pairs={{0,32},{32,0},{64,96},{96,64},{128,160},{160,128},{192,224},{224,1... | collective-permute-start | bytes 2359304 | tf_op jit(solution)/shard_map/ppermute | solution.py:369
  23.0 16.6 %all-to-all-start = ((f16[8,96,512]{2,1,0:T(8,128)(2,1)}), f16[8,96,512]{2,1,0:T(8,128)(2,1)S(1)}, u32[]{:S(2)}, u32[]{:S(2)}) async-start(f16[8,96,512]{2,1,0:T(8,128)(2,1)} %add_convert_fusion), calls=%async_computation | async-start | bytes 1572864 | tf_op jit(solution)/shard_map/all_to_all | solution.py:374
  26.5 1.4 %collective-permute-start.2 = (f32[72,512]{1,0:T(8,128)S(1)}, f32[72,512]{1,0:T(8,128)S(1)}, u32[]{:S(2)}, u32[]{:S(2)}) collective-permute-start(f32[72,512]{1,0:T(8,128)S(1)} %pad_maximum_fusion), channel_id=1, source_target_pairs={{0,0},{1,256},{32,32},{33,288},{64,64},{65,320},{96,96},{97,352},{... | collective-permute-start | bytes 442376 | tf_op jit(solution)/shard_map/ppermute | solution.py:375
  27.2 12.5 %collective-permute-start.3 = (bf16[96,512]{1,0:T(8,128)(2,1)S(1)}, bf16[96,512]{1,0:T(8,128)(2,1)S(1)}, u32[]{:S(2)}, u32[]{:S(2)}) collective-permute-start(bf16[96,512]{1,0:T(8,128)(2,1)S(1)} %reshape.32), channel_id=1, source_target_pairs={{0,0},{1,256},{32,32},{33,288},{64,64},{65,320},{96,96},{97,352},{... | collective-permute-start | bytes 294920 | tf_op jit(solution)/shard_map/ppermute | solution.py:376
  41.0 17.3 %all-to-all-start.1 = ((bf16[8,104,512]{2,1,0:T(8,128)(2,1)}), bf16[8,104,512]{2,1,0:T(8,128)(2,1)S(1)}, u32[]{:S(2)}, u32[]{:S(2)}) async-start(bf16[8,104,512]{2,1,0:T(8,128)(2,1)} %get-tuple-element.27), calls=%async_computation.1 | async-start | bytes 1703936 | tf_op jit(solution)/shard_map/all_to_all | solution.py:384
  44.6 0.7 collective-permute-start.4
  58.3 7.6 %collective-permute-start.5 = (bf16[8,104,512]{2,1,0:T(8,128)(2,1)S(1)}, bf16[8,104,512]{2,1,0:T(8,128)(2,1)S(1)}, u32[]{:S(2)}, u32[]{:S(2)}) collective-permute-start(bf16[8,104,512]{2,1,0:T(8,128)(2,1)S(1)} %all-to-all-done.1), channel_id=1, source_target_pairs={{0,32},{32,0},{64,96},{96,64},{128,160},{160,128},{192,224},{224,1... | collective-permute-start | bytes 2555912 | tf_op jit(solution)/shard_map/ppermute | solution.py:389
  67.2 8.4 %collective-permute-start.6 = (bf16[128,512]{1,0:T(8,128)(2,1)S(1)}, bf16[128,512]{1,0:T(8,128)(2,1)S(1)}, u32[]{:S(2)}, u32[]{:S(2)}) collective-permute-start(bf16[128,512]{1,0:T(8,128)(2,1)S(1)} %get-tuple-element.35), channel_id=1, source_target_pairs={{0,1},{1,0},{2,3},{3,2},{4,5},{5,4},{6,7},{7,6},{8,9},{9,8},{10,11... | collective-permute-start | bytes 393224 | tf_op jit(solution)/shard_map/ppermute | solution.py:394

commit v2 on v1

--- a/solution.py
+++ b/solution.py
@@ -164,18 +164,65 @@
     )(place, x, in_vmem(first), in_hbm(w))
 
 
-def middle_kernel(r_ref, a_ref, b_ref, c_ref, adj_ref, g_ref, back_ref):
+def operand_kernel(*refs):
+    given, out_ref, held, sems = refs[:5], refs[5], refs[6:11], refs[11]
+    copies = [pltpu.make_async_copy(given[k], held[k], sems.at[k]) for k in range(5)]
+    for copy in copies:
+        copy.start()
+    for copy in copies:
+        copy.wait()
+    ub_ref, ld_ref, slopes_ref, state_ref, adj_ref = held
+    boxes, specs, width = adj_ref.shape
+    rows = boxes * specs
+    out_ref[0:rows] = adj_ref[...].astype(jnp.float32).reshape(rows, width).astype(jnp.bfloat16)
+    upper, depth, state = ub_ref[...], ld_ref[...], state_ref[...]
+    unstable = state == 2
+    total = upper + depth
+    one = jnp.where(state == 1, 1.0, 0.0)
+    values = (
+        jnp.where(unstable, slopes_ref[...], one),
+        jnp.where(unstable, upper / total, one),
+        jnp.where(unstable, upper * depth / total, 0.0),
+    )
+    for value in values:
+        high = value.astype(jnp.bfloat16)
+        out_ref[rows : rows + boxes] = high
+        out_ref[rows + boxes : rows + 2 * boxes] = (value - high.astype(jnp.float32)).astype(jnp.bfloat16)
+        rows += 2 * boxes
+
+
+def operands(*given):
+    boxes, specs, width = given[4].shape
+    return pl.pallas_call(
+        operand_kernel,
+        out_shape=jax.ShapeDtypeStruct((boxes * (specs + 6), width), jnp.bfloat16),
+        in_specs=[HBM_SPEC] * 5,
+        out_specs=VMEM_SPEC,
+        scratch_shapes=[pltpu.VMEM(x.shape, x.dtype) for x in given] + [pltpu.SemaphoreType.DMA((5,))],
+        compiler_params=pltpu.CompilerParams(vmem_limit_bytes=VMEM),
+        cost_estimate=cost(0, boxes * width * 4 * 8),
+    )(*map(in_hbm, given))
+
+
+def middle_kernel(r_ref, ops_ref, g_ref, back_ref):
     pre = r_ref[...]
-    rows = pre.shape[0]
+    rows, width = pre.shape
+    boxes = (ops_ref.shape[0] - rows) // 6
+    specs = rows // boxes
+
+    def operand(k):
+        at = rows + 2 * k * boxes
+        value = ops_ref[at : at + boxes].astype(jnp.float32) + ops_ref[at + boxes : at + 2 * boxes].astype(jnp.float32)
+        return jnp.broadcast_to(value[:, None, :], (boxes, specs, width)).reshape(rows, width)
+
+    a, b, c = operand(0), operand(1), operand(2)
     positive = jnp.maximum(pre, 0.0)
     negative = jnp.minimum(pre, 0.0)
-    a, b, c = a_ref[...], b_ref[...], c_ref[...]
-    cot = adj_ref[...].astype(jnp.float32)
+    cot = ops_ref[0:rows].astype(jnp.float32)
     back_ref[0:rows] = (a * positive + b * negative).astype(jnp.bfloat16)
     grad = (cot * jnp.where(pre > 0.0, a, b)).astype(jnp.bfloat16)
     for k in range(CHIPS):
         g_ref[k, 0:rows] = grad
-    width = pre.shape[1]
     line = lax.dot_general(
         jnp.ones((8, width), jnp.float32),
         negative * c,
@@ -189,20 +236,11 @@
     tile = jnp.concatenate([tile, jnp.zeros((8, width - rows), jnp.float32)], axis=1).astype(jnp.bfloat16)
     for k in range(CHIPS):
         g_ref[k, rows : rows + 8] = tile
-    boxes = rows // 4
-    mine = lax.broadcasted_iota(jnp.int32, (boxes, rows), 1) // 4 == lax.broadcasted_iota(
-        jnp.int32, (boxes, rows), 0
-    )
-    slope = jnp.dot(
-        jnp.where(mine, 1.0, 0.0),
-        jnp.where(c > 0.0, cot * positive, 0.0),
-        precision=lax.Precision.HIGHEST,
-        preferred_element_type=jnp.float32,
-    )
-    back_ref[rows : rows + boxes] = slope.astype(jnp.bfloat16)
-
-
-def middle(r, a, b, c, adj):
+    slope = jnp.where(c > 0.0, cot * positive, 0.0).reshape(boxes, specs, width)
+    back_ref[rows : rows + boxes] = jnp.sum(slope, axis=1).astype(jnp.bfloat16)
+
+
+def middle(r, ops):
     rows, width = r.shape
     return pl.pallas_call(
         middle_kernel,
@@ -210,9 +248,11 @@
             jax.ShapeDtypeStruct((CHIPS, rows + 8, width), jnp.bfloat16),
             jax.ShapeDtypeStruct((rows + rows // 4, width), jnp.bfloat16),
         ),
-        compiler_params=pltpu.CompilerParams(vmem_limit_bytes=VMEM),
-        cost_estimate=pl.CostEstimate(flops=30 * rows * width, bytes_accessed=8 * rows * width * 4, transcendentals=0),
-    )(r, a, b, c, adj)
+        in_specs=[VMEM_SPEC] * 2,
+        out_specs=(VMEM_SPEC,) * 2,
+        compiler_params=pltpu.CompilerParams(vmem_limit_bytes=VMEM),
+        cost_estimate=cost(30 * rows * width, 8 * rows * width * 4),
+    )(r, ops)
 
 
 def against(g, block):
@@ -355,31 +395,19 @@
     other = lax.ppermute(coeff, "spec", SPEC_SWAP)
     both = jnp.stack([coeff.reshape(rows, width), other.reshape(rows, width)])
 
-    unstable = state == 2
-    total = upper_bound + lower_depth
-    one = jnp.where(state == 1, 1.0, 0.0)
-    a = jnp.where(unstable, slopes, one)
-    b = jnp.where(unstable, upper_bound / total, one)
-    c = jnp.where(unstable, upper_bound * lower_depth / total, 0.0)
-    abc = jnp.concatenate([a, b, c], axis=0)
-    adj = adjoint.reshape(rows, width)
+    ops = operands(upper_bound, lower_depth, slopes, state, adjoint)
+    ops = lax.ppermute(ops, BOTH, MIDDLE_SWAP)
 
     half, first = stage(far, weight, True)
-    away = near_sums(far, both, half).astype(jnp.float16)
+    away = near_sums(far, both, half)
+    away = away.astype(jnp.float16)
     came = lax.ppermute(away, "neuron", CORE_SWAP)
     kept = far_sums(near, both, first, weight)
     chunks = (kept + came.astype(jnp.float32)).astype(jnp.float16)
 
-    chunks, abc, adj = lax.optimization_barrier((chunks, abc, adj))
     sums = lax.all_to_all(chunks, "neuron", 0, 0, axis_index_groups=SAME_CORE, tiled=True)
-    abc = lax.ppermute(abc, BOTH, MIDDLE_SWAP)
-    adj = lax.ppermute(adj, BOTH, MIDDLE_SWAP)
-    abc = jnp.broadcast_to(
-        abc.reshape(3, nboxes, 1, width), (3, nboxes, nspecs, width)
-    ).reshape(3, rows, width)
-
     pre = jnp.sum(sums.astype(jnp.float32), axis=0) * (1.0 / SCALE)
-    grad, back = middle(pre, abc[0], abc[1], abc[2], adj)
+    grad, back = middle(pre, ops)
 
     grads = lax.all_to_all(grad, "neuron", 0, 0, axis_index_groups=SAME_CORE, tiled=True)
     back = lax.ppermute(back, BOTH, MIDDLE_SWAP)

time: 77 us -> 77 us (level)
  Pallas kernels: 16.1 us -> 17.5 us
    pallas_call x0 -> x1, Pallas kernels: none -> 1.11 us  [operands(): pl.pallas_call(operand_kernel, out_shape=jax.ShapeDtypeStruct((boxes * (s...]
  transfers between devices with their start and end apart: 9 -> 8, of which waited for: 3 -> 3; matrix products, arithmetic and copies ran while one was open for 2% -> 2% of each run, Pallas kernels for 15% -> 17%
where the time goes in v2:
time: 77 us; the launch traced here: 76.4 us
  waiting for transfers between devices  28.5 us (37%)
  starting transfers between devices  26.9 us (35%)
  Pallas kernels  17.5 us (23%)
  other arithmetic  1.64 us (2%)
  local copies, waits for them, and re-layouts  0.97 us (1%)
  between operations  0.85 us (1%)
    all_to_all x1, waiting for transfers between devices, step(): lax.all_to_all(grad, 'neuron', 0, 0, axis_index_groups=SAME_CORE, tiled=T...  13 us
    all_to_all x1, waiting for transfers between devices, step(): lax.all_to_all(chunks, 'neuron', 0, 0, axis_index_groups=SAME_CORE, tiled...  11.2 us
    ppermute x1, starting transfers between devices, step(): came = lax.ppermute(away, 'neuron', CORE_SWAP)  7.9 us
    ppermute x1, starting transfers between devices, step(): other = lax.ppermute(coeff, 'spec', SPEC_SWAP)  5.64 us
    pallas_call x2, Pallas kernels, stage(): pl.pallas_call(stage_more_kernel if more else stage_kernel, out_shape=(ha...  4.5 us
    ppermute x1, waiting for transfers between devices, step(): recv = lax.ppermute(send, 'spec', SPEC_SWAP)  4.31 us
    all_to_all x1, starting transfers between devices, step(): lax.all_to_all(grad, 'neuron', 0, 0, axis_index_groups=SAME_CORE, tiled=T...  3.55 us
    all_to_all x1, starting transfers between devices, step(): lax.all_to_all(chunks, 'neuron', 0, 0, axis_index_groups=SAME_CORE, tiled...  3.55 us
  transfers between devices with their start and end apart: 8, of which 3 were waited for; matrix products, arithmetic and copies ran while one was open for 2% of the time, Pallas kernels for 17%

profile of v2, /device:TPU:1, one launch (start us, length us, event | category | flops | bytes accessed | tf_op | source)
XLA Modules:
  0.0 76.4 jit_solution(11043076167000592322)
XLA Ops:
  0.6 5.6 %collective-permute-start = (bf16[24,4,512]{2,1,0:T(4,128)(2,1)}, bf16[24,4,512]{2,1,0:T(4,128)(2,1)S(1)}, u32[]{:S(2)}, u32[]{:S(2)}) collective-permute-start(bf16[24,4,512]{2,1,0:T(4,128)(2,1)} %param.7), channel_id=1, source_target_pairs={{0,1},{1,0},{2,3},{3,2},{4,5},{5,4},{6,7},{7,6},{8,9},{9,8},{10,11... | collective-permute-start | bytes 294920 | tf_op jit(solution)/shard_map/ppermute | solution.py:395
  6.3 0.9 %stack_reshape.6 = bf16[1,96,512]{2,1,0:T(8,128)(2,1)S(1)} reshape(bf16[24,4,512]{2,1,0:T(4,128)(2,1)} %param.7) | data formatting | bytes 196608 | tf_op jit(solution)/shard_map/stack;reshape | solution.py:396
  7.3 2.4 %shard_map.102 = (bf16[4,512,512]{2,1,0:T(8,128)(2,1)S(1)}, bf16[1,512,512]{2,1,0:T(8,128)(2,1)S(1)}) custom-call(s32[3]{0:T(128)S(1)} %pad_add_fusion.1.place, bf16[512,4096]{1,0:T(8,128)(2,1)} %w_ref.7), custom_call_target="tpu_custom_call" | custom-call | bytes 4194304 | tf_op jit(solution)/shard_map/pallas_call | solution.py:108
  9.7 1.1 %shard_map.104 = f32[8,96,512]{2,1,0:T(8,128)S(1)} custom-call(s32[3]{0:T(128)S(1)} %pad_add_fusion.1.place, bf16[2,96,512]{2,1,0:T(8,128)(2,1)S(1)} %constant_dynamic-update-slice_fusion.x_ref, bf16[4,512,512]{2,1,0:T(8,128)(2,1)S(1)} %get-tuple-element.20.half_ref), custom_call_target="tpu_custom_call" | custom-call | flops 402653184 | bytes 2097152 | tf_op jit(solution)/shard_map/pallas_call | solution.py:135
  10.9 0.2 convert_element_type.12
  11.1 7.9 %collective-permute-start.1 = (f16[8,96,512]{2,1,0:T(8,128)(2,1)S(1)}, f16[8,96,512]{2,1,0:T(8,128)(2,1)S(1)}, u32[]{:S(2)}, u32[]{:S(2)}) collective-permute-start(f16[8,96,512]{2,1,0:T(8,128)(2,1)S(1)} %convert_element_type.12), channel_id=1, source_target_pairs={{0,32},{32,0},{64,96},{96,64},{128,160},{160,128},{192,224},{224,1... | collective-permute-start | bytes 2359304 | tf_op jit(solution)/shard_map/ppermute | solution.py:404
  19.1 2.5 %shard_map.103 = f32[8,96,512]{2,1,0:T(8,128)S(1)} custom-call(s32[3]{0:T(128)S(1)} %pad_add_fusion.place, bf16[2,96,512]{2,1,0:T(8,128)(2,1)S(1)} %constant_dynamic-update-slice_fusion.x_ref, bf16[1,512,512]{2,1,0:T(8,128)(2,1)S(1)} %get-tuple-element.19.first_ref, bf16[512,4096]{1,0:T(8,128)(2,1)} %w_ref.7), custom_call_target="tpu_custom_call" | custom-call | flops 402653184 | bytes 2097152 | tf_op jit(solution)/shard_map/pallas_call | solution.py:156
  21.6 1.2 %add_convert_fusion = f16[8,96,512]{2,1,0:T(8,128)(2,1)} fusion(f32[8,96,512]{2,1,0:T(8,128)S(1)} %shard_map.103, f16[8,96,512]{2,1,0:T(8,128)(2,1)S(1)} %collective-permute-done.1), kind=kLoop, calls=%fused_computation.1 | loop fusion | flops 1179648 | bytes 3145728 | tf_op jit(solution)/shard_map/convert_element_type | solution.py:406
  22.8 3.5 %all-to-all-start = ((f16[8,96,512]{2,1,0:T(8,128)(2,1)}), f16[8,96,512]{2,1,0:T(8,128)(2,1)S(1)}, u32[]{:S(2)}, u32[]{:S(2)}) async-start(f16[8,96,512]{2,1,0:T(8,128)(2,1)} %add_convert_fusion), calls=%async_computation | async-start | bytes 1572864 | tf_op jit(solution)/shard_map/all_to_all | solution.py:408
  26.3 1.1 %shard_map.105 = bf16[240,512]{1,0:T(8,128)(2,1)S(1)} custom-call(f32[24,512]{1,0:T(8,128)} %refs_0_.1, f32[24,512]{1,0:T(8,128)} %refs_1_.1, f32[24,512]{1,0:T(8,128)} %refs_2_.1, s32[24,512]{1,0:T(8,128)} %refs_3_.1, bf16[24,4,512]{2,1,0:T(4,128)(2,1)} %refs_4_.1), custom_call_target="tpu_custom_call" | custom-call | bytes 393216 | tf_op jit(solution)/shard_map/pallas_call | solution.py:196
  27.4 0.7 collective-permute-start.2
  28.1 11.2 %all-to-all-done = f16[8,96,512]{2,1,0:T(8,128)(2,1)S(1)} async-done(((f16[8,96,512]{2,1,0:T(8,128)(2,1)}), f16[8,96,512]{2,1,0:T(8,128)(2,1)S(1)}, u32[]{:S(2)}, u32[]{:S(2)}) %all-to-all-start) | async-done | bytes 786464 | tf_op jit(solution)/shard_map/all_to_all | solution.py:408
  39.5 1.6 %shard_map.106 = (bf16[8,104,512]{2,1,0:T(8,128)(2,1)}, bf16[120,512]{1,0:T(8,128)(2,1)S(1)}) custom-call(f32[96,512]{1,0:T(8,128)S(1)} %broadcast_multiply_fusion.r_ref, bf16[240,512]{1,0:T(8,128)(2,1)S(1)} %collective-permute-done.2.ops_ref), custom_call_target="tpu_custom_call" | custom-call | flops 1474560 | bytes 1572864 | tf_op jit(solution)/shard_map/pallas_call | solution.py:245
  41.0 3.5 %all-to-all-start.1 = ((bf16[8,104,512]{2,1,0:T(8,128)(2,1)}), bf16[8,104,512]{2,1,0:T(8,128)(2,1)S(1)}, u32[]{:S(2)}, u32[]{:S(2)}) async-start(bf16[8,104,512]{2,1,0:T(8,128)(2,1)} %get-tuple-element.21), calls=%async_computation.1 | async-start | bytes 1703936 | tf_op jit(solution)/shard_map/all_to_all | solution.py:412
  44.6 0.7 collective-permute-start.3
  45.3 13.0 %all-to-all-done.1 = bf16[8,104,512]{2,1,0:T(8,128)(2,1)S(1)} async-done(((bf16[8,104,512]{2,1,0:T(8,128)(2,1)}), bf16[8,104,512]{2,1,0:T(8,128)(2,1)S(1)}, u32[]{:S(2)}, u32[]{:S(2)}) %all-to-all-start.1) | async-done | bytes 852000 | tf_op jit(solution)/shard_map/all_to_all | solution.py:412
  58.3 2.7 %collective-permute-start.4 = (bf16[8,104,512]{2,1,0:T(8,128)(2,1)S(1)}, bf16[8,104,512]{2,1,0:T(8,128)(2,1)S(1)}, u32[]{:S(2)}, u32[]{:S(2)}) collective-permute-start(bf16[8,104,512]{2,1,0:T(8,128)(2,1)S(1)} %all-to-all-done.1), channel_id=1, source_target_pairs={{0,32},{32,0},{64,96},{96,64},{128,160},{160,128},{192,224},{224,1... | collective-permute-start | bytes 2555912 | tf_op jit(solution)/shard_map/ppermute | solution.py:417
  61.0 2.1 %shard_map.107.half_ref = bf16[4,512,512]{2,1,0:T(8,128)(2,1)S(1)} custom-call(s32[3]{0:T(128)S(1)} %pad_add_fusion.place, bf16[512,4096]{1,0:T(8,128)(2,1)} %w_ref.7), custom_call_target="tpu_custom_call" | custom-call | bytes 4194304 | tf_op jit(solution)/shard_map/pallas_call | solution.py:108
  63.1 2.7 %shard_map.108 = (f32[2,96,512]{2,1,0:T(8,128)S(1)}, bf16[4,512,512]{2,1,0:T(8,128)(2,1)S(1)}) custom-call(s32[3]{0:T(128)S(1)} %pad_add_fusion.place, bf16[2,4,104,512]{3,2,1,0:T(8,128)(2,1)S(1)} %bitcast.6, bf16[4,512,512]{2,1,0:T(8,128)(2,1)S(1)} %shard_map.107.half_ref, bf16[512,4096]{1,0:T(8,128)(2,1)} %w_ref.7), custom_call_target="tpu_custom_call" | custom-call | flops 402653184 | bytes 2097152 | tf_op jit(solution)/shard_map/pallas_call | solution.py:279
  65.9 1.3 %shard_map.110 = (bf16[128,512]{1,0:T(8,128)(2,1)S(1)}, f32[8,512]{1,0:T(8,128)S(1)}) custom-call(s32[3]{0:T(128)S(1)} %pad_add_fusion.place, bf16[2,4,104,512]{3,2,1,0:T(8,128)(2,1)S(1)} %bitcast.8, bf16[2,4,104,512]{3,2,1,0:T(8,128)(2,1)S(1)} %bitcast.7, bf16[4,512,512]{2,1,0:T(8,128)(2,1)S(1)} %get-tuple-element.24.w_ref, ...), custom_call_target="tpu_custom_call" | custom-call | flops 201326592 | bytes 2097152 | tf_op jit(solution)/shard_map/pallas_call | solution.py:317
  67.2 2.3 %collective-permute-start.5 = (bf16[128,512]{1,0:T(8,128)(2,1)S(1)}, bf16[128,512]{1,0:T(8,128)(2,1)S(1)}, u32[]{:S(2)}, u32[]{:S(2)}) collective-permute-start(bf16[128,512]{1,0:T(8,128)(2,1)S(1)} %get-tuple-element.29), channel_id=1, source_target_pairs={{0,1},{1,0},{2,3},{3,2},{4,5},{5,4},{6,7},{7,6},{8,9},{9,8},{10,11... | collective-permute-start | bytes 393224 | tf_op jit(solution)/shard_map/ppermute | solution.py:422
  69.5 1.9 %shard_map.109 = (f32[96,512]{1,0:T(8,128)S(1)}, bf16[24,4,512]{2,1,0:T(4,128)(2,1)}) custom-call(s32[3]{0:T(128)S(1)} %pad_add_fusion.place, bf16[2,4,104,512]{3,2,1,0:T(8,128)(2,1)S(1)} %bitcast.9, bf16[4,512,512]{2,1,0:T(8,128)(2,1)S(1)} %get-tuple-element.24.w_ref, f32[2,96,512]{2,1,0:T(8,128)S(1)} %get-tuple-element.25.acc_ref, ...), custom_call_target="tpu_custom_call" | custom-call | flops 201326592 | bytes 2097152 | tf_op jit(solution)/shard_map/pallas_call | solution.py:341
  71.3 4.3 %collective-permute-done.5.recv_ref = bf16[128,512]{1,0:T(8,128)(2,1)S(1)} collective-permute-done((bf16[128,512]{1,0:T(8,128)(2,1)S(1)}, bf16[128,512]{1,0:T(8,128)(2,1)S(1)}, u32[]{:S(2)}, u32[]{:S(2)}) %collective-permute-start.5) | collective-permute-done | bytes 131104 | tf_op jit(solution)/shard_map/ppermute | solution.py:422
  75.7 0.8 %shard_map.111 = (bf16[24,4,512]{2,1,0:T(4,128)(2,1)}, f32[4,24]{1,0:T(4,128)}, f32[24,512]{1,0:T(8,128)}) custom-call(f32[96,512]{1,0:T(8,128)S(1)} %get-tuple-element.28.keep_ref, bf16[128,512]{1,0:T(8,128)(2,1)S(1)} %collective-permute-done.5.recv_ref, f32[8,512]{1,0:T(8,128)S(1)} %get-tuple-element.30.bias_ref, ...), custom_call_target="tpu_custom_call" | custom-call | bytes 196608 | tf_op jit(solution)/shard_map/pallas_call | solution.py:373
  (12 shorter events, 0.3 us)
Async XLA Ops:
  0.6 9.1 %collective-permute-start = (bf16[24,4,512]{2,1,0:T(4,128)(2,1)}, bf16[24,4,512]{2,1,0:T(4,128)(2,1)S(1)}, u32[]{:S(2)}, u32[]{:S(2)}) collective-permute-start(bf16[24,4,512]{2,1,0:T(4,128)(2,1)} %param.7), channel_id=1, source_target_pairs={{0,1},{1,0},{2,3},{3,2},{4,5},{5,4},{6,7},{7,6},{8,9},{9,8},{10,11... | collective-permute-start | bytes 294920 | tf_op jit(solution)/shard_map/ppermute | solution.py:395
  11.1 10.5 %collective-permute-start.1 = (f16[8,96,512]{2,1,0:T(8,128)(2,1)S(1)}, f16[8,96,512]{2,1,0:T(8,128)(2,1)S(1)}, u32[]{:S(2)}, u32[]{:S(2)}) collective-permute-start(f16[8,96,512]{2,1,0:T(8,128)(2,1)S(1)} %convert_element_type.12), channel_id=1, source_target_pairs={{0,32},{32,0},{64,96},{96,64},{128,160},{160,128},{192,224},{224,1... | collective-permute-start | bytes 2359304 | tf_op jit(solution)/shard_map/ppermute | solution.py:404
  22.8 16.6 %all-to-all-start = ((f16[8,96,512]{2,1,0:T(8,128)(2,1)}), f16[8,96,512]{2,1,0:T(8,128)(2,1)S(1)}, u32[]{:S(2)}, u32[]{:S(2)}) async-start(f16[8,96,512]{2,1,0:T(8,128)(2,1)} %add_convert_fusion), calls=%async_computation | async-start | bytes 1572864 | tf_op jit(solution)/shard_map/all_to_all | solution.py:408
  27.4 12.0 %collective-permute-start.2 = (bf16[240,512]{1,0:T(8,128)(2,1)S(1)}, bf16[240,512]{1,0:T(8,128)(2,1)S(1)}, u32[]{:S(2)}, u32[]{:S(2)}) collective-permute-start(bf16[240,512]{1,0:T(8,128)(2,1)S(1)} %shard_map.105), channel_id=1, source_target_pairs={{0,0},{1,256},{32,32},{33,288},{64,64},{65,320},{96,96},{97,352},{... | collective-permute-start | bytes 737288 | tf_op jit(solution)/shard_map/ppermute | solution.py:399
  41.0 17.3 %all-to-all-start.1 = ((bf16[8,104,512]{2,1,0:T(8,128)(2,1)}), bf16[8,104,512]{2,1,0:T(8,128)(2,1)S(1)}, u32[]{:S(2)}, u32[]{:S(2)}) async-start(bf16[8,104,512]{2,1,0:T(8,128)(2,1)} %get-tuple-element.21), calls=%async_computation.1 | async-start | bytes 1703936 | tf_op jit(solution)/shard_map/all_to_all | solution.py:412
  44.6 0.7 collective-permute-start.3
  58.3 7.6 %collective-permute-start.4 = (bf16[8,104,512]{2,1,0:T(8,128)(2,1)S(1)}, bf16[8,104,512]{2,1,0:T(8,128)(2,1)S(1)}, u32[]{:S(2)}, u32[]{:S(2)}) collective-permute-start(bf16[8,104,512]{2,1,0:T(8,128)(2,1)S(1)} %all-to-all-done.1), channel_id=1, source_target_pairs={{0,32},{32,0},{64,96},{96,64},{128,160},{160,128},{192,224},{224,1... | collective-permute-start | bytes 2555912 | tf_op jit(solution)/shard_map/ppermute | solution.py:417
  67.2 8.4 %collective-permute-start.5 = (bf16[128,512]{1,0:T(8,128)(2,1)S(1)}, bf16[128,512]{1,0:T(8,128)(2,1)S(1)}, u32[]{:S(2)}, u32[]{:S(2)}) collective-permute-start(bf16[128,512]{1,0:T(8,128)(2,1)S(1)} %get-tuple-element.29), channel_id=1, source_target_pairs={{0,1},{1,0},{2,3},{3,2},{4,5},{5,4},{6,7},{7,6},{8,9},{9,8},{10,11... | collective-permute-start | bytes 393224 | tf_op jit(solution)/shard_map/ppermute | solution.py:422

commit v3 on v2

--- a/solution.py
+++ b/solution.py
@@ -73,13 +73,6 @@
         wait(pieces)
 
 
-def stage_more_kernel(place, w_ref, out_ref, more_ref, sems, more_sems):
-    copies = halves(w_ref, out_ref, sems, place[1]) + halves(w_ref, more_ref, more_sems, place[2])
-    start(copies)
-    for pieces in copies:
-        wait(pieces)
-
-
 def in_hbm(w):
     return pltpu.with_memory_space_constraint(w, pltpu.HBM)
 
@@ -102,85 +95,88 @@
     return pl.CostEstimate(flops=flops, bytes_accessed=moved, transcendentals=0)
 
 
-def stage(place, w, more):
-    block = (1, w.shape[0], w.shape[0])
-    half = pltpu.VMEM(half_shape(w), w.dtype)
-    return pl.pallas_call(
-        stage_more_kernel if more else stage_kernel,
-        out_shape=(half, pltpu.VMEM(block, w.dtype)) if more else half,
+def stage(place, w):
+    return pl.pallas_call(
+        stage_kernel,
+        out_shape=pltpu.VMEM(half_shape(w), w.dtype),
         in_specs=[SMEM_SPEC, HBM_SPEC],
-        out_specs=(VMEM_SPEC, VMEM_SPEC) if more else VMEM_SPEC,
-        scratch_shapes=[SEMS, SEMS] if more else [SEMS],
+        out_specs=VMEM_SPEC,
+        scratch_shapes=[SEMS],
         compiler_params=pltpu.CompilerParams(vmem_limit_bytes=VMEM),
         cost_estimate=cost(0, w.size * 2),
     )(place, in_hbm(w))
 
 
-def part_block(place, x_ref, block, out_ref, col):
+def part_block(place, both, block, out_ref, col):
     own = place[0]
-    rows = x_ref.shape[1]
-    both = x_ref[...].reshape(2 * rows, x_ref.shape[2])
+    rows = both.shape[0] // 2
     acc = jnp.dot(both, block, preferred_element_type=jnp.float32) * SCALE
     out_ref[pl.ds(own * LINE + col, 1)] = acc[:rows][None]
     out_ref[pl.ds((1 - own) * LINE + col, 1)] = acc[rows:][None]
 
 
-def near_kernel(place, x_ref, half_ref, out_ref):
+def near_kernel(place, own_ref, other_ref, half_ref, out_ref):
+    both = jnp.concatenate([own_ref[...], other_ref[...]], axis=0)
     for i in range(LINE):
-        part_block(place, x_ref, half_ref[i], out_ref, i)
-
-
-def near_sums(place, x, half):
-    rows, width = x.shape[1:]
+        part_block(place, both, half_ref[i], out_ref, i)
+
+
+def near_sums(place, own, other, half):
+    rows, width = own.shape
     return pl.pallas_call(
         near_kernel,
         out_shape=jax.ShapeDtypeStruct((CHIPS, rows, width), jnp.float32),
-        in_specs=[SMEM_SPEC, VMEM_SPEC, VMEM_SPEC],
+        in_specs=[SMEM_SPEC] + [VMEM_SPEC] * 3,
         out_specs=VMEM_SPEC,
         compiler_params=pltpu.CompilerParams(vmem_limit_bytes=VMEM),
         cost_estimate=cost(2 * 2 * rows * width * width * LINE, width * width * LINE * 2),
-    )(place, x, in_vmem(half))
-
-
-def far_kernel(place, x_ref, first_ref, w_ref, out_ref, buf_ref, sems):
+    )(place, in_vmem(own), other, in_vmem(half))
+
+
+def far_kernel(place, own_ref, other_ref, first_ref, w_ref, out_ref, buf_ref, sems):
     copies = halves(w_ref, buf_ref, sems, place[1], 1)
     start(copies)
-    part_block(place, x_ref, first_ref[0], out_ref, 0)
+    both = jnp.concatenate([own_ref[...], other_ref[...]], axis=0)
+    part_block(place, both, first_ref[0], out_ref, 0)
     for i in range(1, LINE):
         wait(copies[i - 1])
-        part_block(place, x_ref, buf_ref[i - 1], out_ref, i)
-
-
-def far_sums(place, x, first, w):
-    rows, width = x.shape[1:]
+        part_block(place, both, buf_ref[i - 1], out_ref, i)
+
+
+def far_sums(place, own, other, first, w):
+    rows, width = own.shape
     return pl.pallas_call(
         far_kernel,
         out_shape=jax.ShapeDtypeStruct((CHIPS, rows, width), jnp.float32),
-        in_specs=[SMEM_SPEC, VMEM_SPEC, VMEM_SPEC, HBM_SPEC],
+        in_specs=[SMEM_SPEC] + [VMEM_SPEC] * 3 + [HBM_SPEC],
         out_specs=VMEM_SPEC,
         scratch_shapes=[pltpu.VMEM((LINE - 1, width, width), w.dtype), SEMS],
         compiler_params=pltpu.CompilerParams(vmem_limit_bytes=VMEM),
         cost_estimate=cost(2 * 2 * rows * width * width * LINE, width * width * LINE * 2),
-    )(place, x, in_vmem(first), in_hbm(w))
-
-
-def operand_kernel(*refs):
-    given, out_ref, held, sems = refs[:5], refs[5], refs[6:11], refs[11]
-    copies = [pltpu.make_async_copy(given[k], held[k], sems.at[k]) for k in range(5)]
+    )(place, in_vmem(own), other, in_vmem(first), in_hbm(w))
+
+
+def prepare_kernel(place, w_ref, *refs):
+    given, (out_ref, own_ref, half_ref, more_ref) = refs[:6], refs[6:10]
+    held, sems, half_sems, more_sems = refs[10:16], refs[16], refs[17], refs[18]
+    copies = [pltpu.make_async_copy(given[k], held[k], sems.at[k]) for k in range(6)]
     for copy in copies:
         copy.start()
+    weights = halves(w_ref, half_ref, half_sems, place[1]) + halves(w_ref, more_ref, more_sems, place[2])
+    start(weights)
     for copy in copies:
         copy.wait()
-    ub_ref, ld_ref, slopes_ref, state_ref, adj_ref = held
+    upper, depth, slopes, state = (held[k][...] for k in range(4))
+    adj_ref, coeff_ref = held[4:]
     boxes, specs, width = adj_ref.shape
     rows = boxes * specs
     out_ref[0:rows] = adj_ref[...].astype(jnp.float32).reshape(rows, width).astype(jnp.bfloat16)
-    upper, depth, state = ub_ref[...], ld_ref[...], state_ref[...]
+    own_ref[...] = coeff_ref[...].astype(jnp.float32).reshape(rows, width).astype(jnp.bfloat16)
     unstable = state == 2
     total = upper + depth
     one = jnp.where(state == 1, 1.0, 0.0)
     values = (
-        jnp.where(unstable, slopes_ref[...], one),
+        jnp.where(unstable, slopes, one),
         jnp.where(unstable, upper / total, one),
         jnp.where(unstable, upper * depth / total, 0.0),
     )
@@ -189,19 +185,26 @@
         out_ref[rows : rows + boxes] = high
         out_ref[rows + boxes : rows + 2 * boxes] = (value - high.astype(jnp.float32)).astype(jnp.bfloat16)
         rows += 2 * boxes
-
-
-def operands(*given):
+    for pieces in weights:
+        wait(pieces)
+
+
+def prepare(place, w, *given):
     boxes, specs, width = given[4].shape
     return pl.pallas_call(
-        operand_kernel,
-        out_shape=jax.ShapeDtypeStruct((boxes * (specs + 6), width), jnp.bfloat16),
-        in_specs=[HBM_SPEC] * 5,
-        out_specs=VMEM_SPEC,
-        scratch_shapes=[pltpu.VMEM(x.shape, x.dtype) for x in given] + [pltpu.SemaphoreType.DMA((5,))],
-        compiler_params=pltpu.CompilerParams(vmem_limit_bytes=VMEM),
-        cost_estimate=cost(0, boxes * width * 4 * 8),
-    )(*map(in_hbm, given))
+        prepare_kernel,
+        out_shape=(
+            pltpu.VMEM((boxes * (specs + 6), width), jnp.bfloat16),
+            pltpu.VMEM((boxes * specs, width), jnp.bfloat16),
+            pltpu.VMEM(half_shape(w), w.dtype),
+            pltpu.VMEM((1, width, width), w.dtype),
+        ),
+        in_specs=[SMEM_SPEC] + [HBM_SPEC] * 7,
+        out_specs=(VMEM_SPEC,) * 4,
+        scratch_shapes=[pltpu.VMEM(x.shape, x.dtype) for x in given] + [pltpu.SemaphoreType.DMA((6,)), SEMS, SEMS],
+        compiler_params=pltpu.CompilerParams(vmem_limit_bytes=VMEM),
+        cost_estimate=cost(0, w.size * 2),
+    )(place, *map(in_hbm, (w, *given)))
 
 
 def middle_kernel(r_ref, ops_ref, g_ref, back_ref):
@@ -393,16 +396,14 @@
     far = jnp.stack([s, 1 - core, core])
 
     other = lax.ppermute(coeff, "spec", SPEC_SWAP)
-    both = jnp.stack([coeff.reshape(rows, width), other.reshape(rows, width)])
-
-    ops = operands(upper_bound, lower_depth, slopes, state, adjoint)
+    other = other.reshape(rows, width)
+    ops, own, half, first = prepare(far, weight, upper_bound, lower_depth, slopes, state, adjoint, coeff)
     ops = lax.ppermute(ops, BOTH, MIDDLE_SWAP)
 
-    half, first = stage(far, weight, True)
-    away = near_sums(far, both, half)
+    away = near_sums(far, own, other, half)
     away = away.astype(jnp.float16)
     came = lax.ppermute(away, "neuron", CORE_SWAP)
-    kept = far_sums(near, both, first, weight)
+    kept = far_sums(near, own, other, first, weight)
     chunks = (kept + came.astype(jnp.float32)).astype(jnp.float16)
 
     sums = lax.all_to_all(chunks, "neuron", 0, 0, axis_index_groups=SAME_CORE, tiled=True)
@@ -411,7 +412,7 @@
 
     grads = lax.all_to_all(grad, "neuron", 0, 0, axis_index_groups=SAME_CORE, tiled=True)
     back = lax.ppermute(back, BOTH, MIDDLE_SWAP)
-    half = stage(near, weight, False)
+    half = stage(near, weight)
     grads, back = lax.optimization_barrier((grads, back))
 
     far_grads = lax.ppermute(grads, "neuron", CORE_SWAP)

time: 77 us -> 76.9 us (level)
  waiting for transfers between devices: 28.5 us -> 30 us
  local copies, waits for them, and re-layouts: 0.97 us -> 0.03 us
  Pallas kernels: 17.5 us -> 16.6 us
    all_to_all x1, waiting for transfers between devices: 11.2 us -> 12.3 us  [step(): lax.all_to_all(chunks, 'neuron', 0, 0, axis_index_groups=SAME_CORE, tiled...]
    another operation x3 -> x0, local copies, waits for them, and re-layouts: 0.96 us -> none  [step(): both = jnp.stack([coeff.reshape(rows, width), other.reshape(rows, width)])]
    pallas_call x3 -> x2, Pallas kernels: 5.61 us -> 4.68 us  [the longest x1 2.55 us: prepare(): pl.pallas_call(prepare_kernel, out_shape=(pltpu.VMEM((boxes * (specs + 6)...]
    ppermute x1, starting transfers between devices: 7.9 us -> 8.67 us  [step(): came = lax.ppermute(away, 'neuron', CORE_SWAP)]
  transfers between devices with their start and end apart: 8 -> 8, of which waited for: 3 -> 3; matrix products, arithmetic and copies ran while one was open for 2% -> 0% of each run, Pallas kernels for 17% -> 15%
where the time goes in v3:
time: 76.9 us; the launch traced here: 76.4 us
  waiting for transfers between devices  30 us (39%)
  starting transfers between devices  27.4 us (36%)
  Pallas kernels  16.6 us (22%)
  other arithmetic  1.64 us (2%)
  between operations  0.81 us (1%)
    all_to_all x1, waiting for transfers between devices, step(): lax.all_to_all(grad, 'neuron', 0, 0, axis_index_groups=SAME_CORE, tiled=T...  13 us
    all_to_all x1, waiting for transfers between devices, step(): lax.all_to_all(chunks, 'neuron', 0, 0, axis_index_groups=SAME_CORE, tiled...  12.3 us
    ppermute x1, starting transfers between devices, step(): came = lax.ppermute(away, 'neuron', CORE_SWAP)  8.67 us
    ppermute x1, starting transfers between devices, step(): other = lax.ppermute(coeff, 'spec', SPEC_SWAP)  5.64 us
    ppermute x1, waiting for transfers between devices, step(): recv = lax.ppermute(send, 'spec', SPEC_SWAP)  4.65 us
    all_to_all x1, starting transfers between devices, step(): lax.all_to_all(grad, 'neuron', 0, 0, axis_index_groups=SAME_CORE, tiled=T...  3.55 us
    all_to_all x1, starting transfers between devices, step(): lax.all_to_all(chunks, 'neuron', 0, 0, axis_index_groups=SAME_CORE, tiled...  3.55 us
    pallas_call x1, Pallas kernels, near_back(): pl.pallas_call(near_back_kernel, out_shape=(pltpu.VMEM((2, rows, width),...  2.74 us
  transfers between devices with their start and end apart: 8, of which 3 were waited for; matrix products, arithmetic and copies ran while one was open for 0% of the time, Pallas kernels for 15%

profile of v3, /device:TPU:1, one launch (start us, length us, event | category | flops | bytes accessed | tf_op | source)
XLA Modules:
  0.0 76.4 jit_solution(3913298538773907271)
XLA Ops:
  0.6 5.6 %collective-permute-start = (bf16[24,4,512]{2,1,0:T(4,128)(2,1)}, bf16[24,4,512]{2,1,0:T(4,128)(2,1)S(1)}, u32[]{:S(2)}, u32[]{:S(2)}) collective-permute-start(bf16[24,4,512]{2,1,0:T(4,128)(2,1)} %refs_5_.1), channel_id=1, source_target_pairs={{0,1},{1,0},{2,3},{3,2},{4,5},{5,4},{6,7},{7,6},{8,9},{9,8},{10,11... | collective-permute-start | bytes 294920 | tf_op jit(solution)/shard_map/ppermute | solution.py:398
  6.4 2.5 %shard_map.102 = (bf16[240,512]{1,0:T(8,128)(2,1)S(1)}, bf16[96,512]{1,0:T(8,128)(2,1)S(1)}, bf16[4,512,512]{2,1,0:T(8,128)(2,1)S(1)}, bf16[1,512,512]{2,1,0:T(8,128)(2,1)S(1)}) custom-call(s32[3]{0:T(128)S(1)} %pad_add_fusion.1.place, bf16[512,4096]{1,0:T(8,128)(2,1)} %w_ref.7, f32[24,512]{1,0:T(8,128)} %refs_0_.1, f32[24,512]{1,0:T(8,128)} %refs_1_.1, ...), custom_call_target="tpu_custom_call" | custom-call | bytes 4194304 | tf_op jit(solution)/shard_map/pallas_call | solution.py:194
  9.0 1.1 %shard_map.104 = f32[8,96,512]{2,1,0:T(8,128)S(1)} custom-call(s32[3]{0:T(128)S(1)} %pad_add_fusion.1.place, bf16[96,512]{1,0:T(8,128)(2,1)S(1)} %get-tuple-element.21.own_ref, bf16[96,512]{1,0:T(8,128)(2,1)S(1)} %reshape.17.other_ref, bf16[4,512,512]{2,1,0:T(8,128)(2,1)S(1)} %get-tuple-element.23.half_ref), custom_call_target="tpu_custom_call" | custom-call | flops 402653184 | bytes 2097152 | tf_op jit(solution)/shard_map/pallas_call | solution.py:126
  10.1 0.2 convert_element_type.12
  10.3 8.7 %collective-permute-start.1 = (f16[8,96,512]{2,1,0:T(8,128)(2,1)S(1)}, f16[8,96,512]{2,1,0:T(8,128)(2,1)S(1)}, u32[]{:S(2)}, u32[]{:S(2)}) collective-permute-start(f16[8,96,512]{2,1,0:T(8,128)(2,1)S(1)} %convert_element_type.12), channel_id=1, source_target_pairs={{0,32},{32,0},{64,96},{96,64},{128,160},{160,128},{192,224},{224,1... | collective-permute-start | bytes 2359304 | tf_op jit(solution)/shard_map/ppermute | solution.py:405
  19.0 0.1 pad_add_fusion.place
  19.0 2.5 %shard_map.103 = f32[8,96,512]{2,1,0:T(8,128)S(1)} custom-call(s32[3]{0:T(128)S(1)} %pad_add_fusion.place, bf16[96,512]{1,0:T(8,128)(2,1)S(1)} %get-tuple-element.21.own_ref, bf16[96,512]{1,0:T(8,128)(2,1)S(1)} %reshape.17.other_ref, bf16[1,512,512]{2,1,0:T(8,128)(2,1)S(1)} %get-tuple-element.22.first_ref, bf16[512,4096]{1,0:T(8,128)(2,1)} %w_ref.7), custom_call_target="tpu_custom_call" | custom-call | flops 402653184 | bytes 2097152 | tf_op jit(solution)/shard_map/pallas_call | solution.py:148
  21.5 1.2 %add_convert_fusion = f16[8,96,512]{2,1,0:T(8,128)(2,1)} fusion(f32[8,96,512]{2,1,0:T(8,128)S(1)} %shard_map.103, f16[8,96,512]{2,1,0:T(8,128)(2,1)S(1)} %collective-permute-done.1), kind=kLoop, calls=%fused_computation.1 | loop fusion | flops 1179648 | bytes 3145728 | tf_op jit(solution)/shard_map/convert_element_type | solution.py:407
  22.7 3.5 %all-to-all-start = ((f16[8,96,512]{2,1,0:T(8,128)(2,1)}), f16[8,96,512]{2,1,0:T(8,128)(2,1)S(1)}, u32[]{:S(2)}, u32[]{:S(2)}) async-start(f16[8,96,512]{2,1,0:T(8,128)(2,1)} %add_convert_fusion), calls=%async_computation | async-start | bytes 1572864 | tf_op jit(solution)/shard_map/all_to_all | solution.py:409
  26.3 0.7 collective-permute-start.2
  27.0 12.3 %all-to-all-done = f16[8,96,512]{2,1,0:T(8,128)(2,1)S(1)} async-done(((f16[8,96,512]{2,1,0:T(8,128)(2,1)}), f16[8,96,512]{2,1,0:T(8,128)(2,1)S(1)}, u32[]{:S(2)}, u32[]{:S(2)}) %all-to-all-start) | async-done | bytes 786464 | tf_op jit(solution)/shard_map/all_to_all | solution.py:409
  39.3 0.1 convert_reduce_fusion
  39.4 1.6 %shard_map.105 = (bf16[8,104,512]{2,1,0:T(8,128)(2,1)}, bf16[120,512]{1,0:T(8,128)(2,1)S(1)}) custom-call(f32[96,512]{1,0:T(8,128)S(1)} %broadcast_multiply_fusion.r_ref, bf16[240,512]{1,0:T(8,128)(2,1)S(1)} %collective-permute-done.2.ops_ref), custom_call_target="tpu_custom_call" | custom-call | flops 1474560 | bytes 1572864 | tf_op jit(solution)/shard_map/pallas_call | solution.py:248
  41.0 3.5 %all-to-all-start.1 = ((bf16[8,104,512]{2,1,0:T(8,128)(2,1)}), bf16[8,104,512]{2,1,0:T(8,128)(2,1)S(1)}, u32[]{:S(2)}, u32[]{:S(2)}) async-start(bf16[8,104,512]{2,1,0:T(8,128)(2,1)} %get-tuple-element.25), calls=%async_computation.1 | async-start | bytes 1703936 | tf_op jit(solution)/shard_map/all_to_all | solution.py:413
  44.6 0.7 collective-permute-start.3
  45.2 13.0 %all-to-all-done.1 = bf16[8,104,512]{2,1,0:T(8,128)(2,1)S(1)} async-done(((bf16[8,104,512]{2,1,0:T(8,128)(2,1)}), bf16[8,104,512]{2,1,0:T(8,128)(2,1)S(1)}, u32[]{:S(2)}, u32[]{:S(2)}) %all-to-all-start.1) | async-done | bytes 852000 | tf_op jit(solution)/shard_map/all_to_all | solution.py:413
  58.3 2.7 %collective-permute-start.4 = (bf16[8,104,512]{2,1,0:T(8,128)(2,1)S(1)}, bf16[8,104,512]{2,1,0:T(8,128)(2,1)S(1)}, u32[]{:S(2)}, u32[]{:S(2)}) collective-permute-start(bf16[8,104,512]{2,1,0:T(8,128)(2,1)S(1)} %all-to-all-done.1), channel_id=1, source_target_pairs={{0,32},{32,0},{64,96},{96,64},{128,160},{160,128},{192,224},{224,1... | collective-permute-start | bytes 2555912 | tf_op jit(solution)/shard_map/ppermute | solution.py:418
  61.0 2.1 %shard_map.106.half_ref = bf16[4,512,512]{2,1,0:T(8,128)(2,1)S(1)} custom-call(s32[3]{0:T(128)S(1)} %pad_add_fusion.place, bf16[512,4096]{1,0:T(8,128)(2,1)} %w_ref.7), custom_call_target="tpu_custom_call" | custom-call | bytes 4194304 | tf_op jit(solution)/shard_map/pallas_call | solution.py:99
  63.1 2.7 %shard_map.107 = (f32[2,96,512]{2,1,0:T(8,128)S(1)}, bf16[4,512,512]{2,1,0:T(8,128)(2,1)S(1)}) custom-call(s32[3]{0:T(128)S(1)} %pad_add_fusion.place, bf16[2,4,104,512]{3,2,1,0:T(8,128)(2,1)S(1)} %bitcast.6, bf16[4,512,512]{2,1,0:T(8,128)(2,1)S(1)} %shard_map.106.half_ref, bf16[512,4096]{1,0:T(8,128)(2,1)} %w_ref.7), custom_call_target="tpu_custom_call" | custom-call | flops 402653184 | bytes 2097152 | tf_op jit(solution)/shard_map/pallas_call | solution.py:282
  65.9 1.3 %shard_map.109 = (bf16[128,512]{1,0:T(8,128)(2,1)S(1)}, f32[8,512]{1,0:T(8,128)S(1)}) custom-call(s32[3]{0:T(128)S(1)} %pad_add_fusion.place, bf16[2,4,104,512]{3,2,1,0:T(8,128)(2,1)S(1)} %bitcast.8, bf16[2,4,104,512]{3,2,1,0:T(8,128)(2,1)S(1)} %bitcast.7, bf16[4,512,512]{2,1,0:T(8,128)(2,1)S(1)} %get-tuple-element.28.w_ref, ...), custom_call_target="tpu_custom_call" | custom-call | flops 201326592 | bytes 2097152 | tf_op jit(solution)/shard_map/pallas_call | solution.py:320
  67.2 1.9 %collective-permute-start.5 = (bf16[128,512]{1,0:T(8,128)(2,1)S(1)}, bf16[128,512]{1,0:T(8,128)(2,1)S(1)}, u32[]{:S(2)}, u32[]{:S(2)}) collective-permute-start(bf16[128,512]{1,0:T(8,128)(2,1)S(1)} %get-tuple-element.33), channel_id=1, source_target_pairs={{0,1},{1,0},{2,3},{3,2},{4,5},{5,4},{6,7},{7,6},{8,9},{9,8},{10,11... | collective-permute-start | bytes 393224 | tf_op jit(solution)/shard_map/ppermute | solution.py:423
  69.1 1.9 %shard_map.108 = (f32[96,512]{1,0:T(8,128)S(1)}, bf16[24,4,512]{2,1,0:T(4,128)(2,1)}) custom-call(s32[3]{0:T(128)S(1)} %pad_add_fusion.place, bf16[2,4,104,512]{3,2,1,0:T(8,128)(2,1)S(1)} %bitcast.9, bf16[4,512,512]{2,1,0:T(8,128)(2,1)S(1)} %get-tuple-element.28.w_ref, f32[2,96,512]{2,1,0:T(8,128)S(1)} %get-tuple-element.29.acc_ref, ...), custom_call_target="tpu_custom_call" | custom-call | flops 201326592 | bytes 2097152 | tf_op jit(solution)/shard_map/pallas_call | solution.py:344
  71.0 4.7 %collective-permute-done.5.recv_ref = bf16[128,512]{1,0:T(8,128)(2,1)S(1)} collective-permute-done((bf16[128,512]{1,0:T(8,128)(2,1)S(1)}, bf16[128,512]{1,0:T(8,128)(2,1)S(1)}, u32[]{:S(2)}, u32[]{:S(2)}) %collective-permute-start.5) | collective-permute-done | bytes 131104 | tf_op jit(solution)/shard_map/ppermute | solution.py:423
  75.6 0.8 %shard_map.110 = (bf16[24,4,512]{2,1,0:T(4,128)(2,1)}, f32[4,24]{1,0:T(4,128)}, f32[24,512]{1,0:T(8,128)}) custom-call(f32[96,512]{1,0:T(8,128)S(1)} %get-tuple-element.32.keep_ref, bf16[128,512]{1,0:T(8,128)(2,1)S(1)} %collective-permute-done.5.recv_ref, f32[8,512]{1,0:T(8,128)S(1)} %get-tuple-element.34.bias_ref, ...), custom_call_target="tpu_custom_call" | custom-call | bytes 196608 | tf_op jit(solution)/shard_map/pallas_call | solution.py:376
  (8 shorter events, 0.1 us)
Async XLA Ops:
  0.6 8.3 %collective-permute-start = (bf16[24,4,512]{2,1,0:T(4,128)(2,1)}, bf16[24,4,512]{2,1,0:T(4,128)(2,1)S(1)}, u32[]{:S(2)}, u32[]{:S(2)}) collective-permute-start(bf16[24,4,512]{2,1,0:T(4,128)(2,1)} %refs_5_.1), channel_id=1, source_target_pairs={{0,1},{1,0},{2,3},{3,2},{4,5},{5,4},{6,7},{7,6},{8,9},{9,8},{10,11... | collective-permute-start | bytes 294920 | tf_op jit(solution)/shard_map/ppermute | solution.py:398
  10.3 11.3 %collective-permute-start.1 = (f16[8,96,512]{2,1,0:T(8,128)(2,1)S(1)}, f16[8,96,512]{2,1,0:T(8,128)(2,1)S(1)}, u32[]{:S(2)}, u32[]{:S(2)}) collective-permute-start(f16[8,96,512]{2,1,0:T(8,128)(2,1)S(1)} %convert_element_type.12), channel_id=1, source_target_pairs={{0,32},{32,0},{64,96},{96,64},{128,160},{160,128},{192,224},{224,1... | collective-permute-start | bytes 2359304 | tf_op jit(solution)/shard_map/ppermute | solution.py:405
  22.7 16.6 %all-to-all-start = ((f16[8,96,512]{2,1,0:T(8,128)(2,1)}), f16[8,96,512]{2,1,0:T(8,128)(2,1)S(1)}, u32[]{:S(2)}, u32[]{:S(2)}) async-start(f16[8,96,512]{2,1,0:T(8,128)(2,1)} %add_convert_fusion), calls=%async_computation | async-start | bytes 1572864 | tf_op jit(solution)/shard_map/all_to_all | solution.py:409
  26.3 13.1 %collective-permute-start.2 = (bf16[240,512]{1,0:T(8,128)(2,1)S(1)}, bf16[240,512]{1,0:T(8,128)(2,1)S(1)}, u32[]{:S(2)}, u32[]{:S(2)}) collective-permute-start(bf16[240,512]{1,0:T(8,128)(2,1)S(1)} %get-tuple-element.24), channel_id=1, source_target_pairs={{0,0},{1,256},{32,32},{33,288},{64,64},{65,320},{96,96},{97,352},{... | collective-permute-start | bytes 737288 | tf_op jit(solution)/shard_map/ppermute | solution.py:401
  41.0 17.3 %all-to-all-start.1 = ((bf16[8,104,512]{2,1,0:T(8,128)(2,1)}), bf16[8,104,512]{2,1,0:T(8,128)(2,1)S(1)}, u32[]{:S(2)}, u32[]{:S(2)}) async-start(bf16[8,104,512]{2,1,0:T(8,128)(2,1)} %get-tuple-element.25), calls=%async_computation.1 | async-start | bytes 1703936 | tf_op jit(solution)/shard_map/all_to_all | solution.py:413
  44.6 0.7 collective-permute-start.3
  58.3 7.6 %collective-permute-start.4 = (bf16[8,104,512]{2,1,0:T(8,128)(2,1)S(1)}, bf16[8,104,512]{2,1,0:T(8,128)(2,1)S(1)}, u32[]{:S(2)}, u32[]{:S(2)}) collective-permute-start(bf16[8,104,512]{2,1,0:T(8,128)(2,1)S(1)} %all-to-all-done.1), channel_id=1, source_target_pairs={{0,32},{32,0},{64,96},{96,64},{128,160},{160,128},{192,224},{224,1... | collective-permute-start | bytes 2555912 | tf_op jit(solution)/shard_map/ppermute | solution.py:418
  67.2 8.4 %collective-permute-start.5 = (bf16[128,512]{1,0:T(8,128)(2,1)S(1)}, bf16[128,512]{1,0:T(8,128)(2,1)S(1)}, u32[]{:S(2)}, u32[]{:S(2)}) collective-permute-start(bf16[128,512]{1,0:T(8,128)(2,1)S(1)} %get-tuple-element.33), channel_id=1, source_target_pairs={{0,1},{1,0},{2,3},{3,2},{4,5},{5,4},{6,7},{7,6},{8,9},{9,8},{10,11... | collective-permute-start | bytes 393224 | tf_op jit(solution)/shard_map/ppermute | solution.py:423

commit v4 on v3

--- a/solution.py
+++ b/solution.py
@@ -66,8 +66,8 @@
         piece.wait()
 
 
-def stage_kernel(place, w_ref, out_ref, sems):
-    copies = halves(w_ref, out_ref, sems, place[1])
+def stage_kernel(place, w_ref, half_ref, more_ref, sems, more_sems):
+    copies = halves(w_ref, half_ref, sems, place[1]) + halves(w_ref, more_ref, more_sems, place[2])
     start(copies)
     for pieces in copies:
         wait(pieces)
@@ -96,12 +96,13 @@
 
 
 def stage(place, w):
+    block = (1, w.shape[0], w.shape[0])
     return pl.pallas_call(
         stage_kernel,
-        out_shape=pltpu.VMEM(half_shape(w), w.dtype),
+        out_shape=(pltpu.VMEM(half_shape(w), w.dtype), pltpu.VMEM(block, w.dtype)),
         in_specs=[SMEM_SPEC, HBM_SPEC],
-        out_specs=VMEM_SPEC,
-        scratch_shapes=[SEMS],
+        out_specs=(VMEM_SPEC, VMEM_SPEC),
+        scratch_shapes=[SEMS, SEMS],
         compiler_params=pltpu.CompilerParams(vmem_limit_bytes=VMEM),
         cost_estimate=cost(0, w.size * 2),
     )(place, in_hbm(w))
@@ -207,7 +208,7 @@
     )(place, *map(in_hbm, (w, *given)))
 
 
-def middle_kernel(r_ref, ops_ref, g_ref, back_ref):
+def middle_kernel(r_ref, ops_ref, g_ref, back_ref, tile_ref, sems):
     pre = r_ref[...]
     rows, width = pre.shape
     boxes = (ops_ref.shape[0] - rows) // 6
@@ -219,13 +220,9 @@
         return jnp.broadcast_to(value[:, None, :], (boxes, specs, width)).reshape(rows, width)
 
     a, b, c = operand(0), operand(1), operand(2)
-    positive = jnp.maximum(pre, 0.0)
     negative = jnp.minimum(pre, 0.0)
     cot = ops_ref[0:rows].astype(jnp.float32)
-    back_ref[0:rows] = (a * positive + b * negative).astype(jnp.bfloat16)
-    grad = (cot * jnp.where(pre > 0.0, a, b)).astype(jnp.bfloat16)
-    for k in range(CHIPS):
-        g_ref[k, 0:rows] = grad
+    tile_ref[0:rows] = (cot * jnp.where(pre > 0.0, a, b)).astype(jnp.bfloat16)
     line = lax.dot_general(
         jnp.ones((8, width), jnp.float32),
         negative * c,
@@ -236,11 +233,17 @@
     high = line.astype(jnp.bfloat16).astype(jnp.float32)
     row = lax.broadcasted_iota(jnp.int32, line.shape, 0)
     tile = jnp.where(row == 0, high, jnp.where(row == 1, line - high, 0.0))
-    tile = jnp.concatenate([tile, jnp.zeros((8, width - rows), jnp.float32)], axis=1).astype(jnp.bfloat16)
-    for k in range(CHIPS):
-        g_ref[k, rows : rows + 8] = tile
+    tile = jnp.concatenate([tile, jnp.zeros((8, width - rows), jnp.float32)], axis=1)
+    tile_ref[rows : rows + 8] = tile.astype(jnp.bfloat16)
+    copies = [pltpu.make_async_copy(tile_ref, g_ref.at[k], sems.at[k]) for k in range(CHIPS)]
+    for copy in copies:
+        copy.start()
+    positive = jnp.maximum(pre, 0.0)
+    back_ref[0:rows] = (a * positive + b * negative).astype(jnp.bfloat16)
     slope = jnp.where(c > 0.0, cot * positive, 0.0).reshape(boxes, specs, width)
     back_ref[rows : rows + boxes] = jnp.sum(slope, axis=1).astype(jnp.bfloat16)
+    for copy in copies:
+        copy.wait()
 
 
 def middle(r, ops):
@@ -248,11 +251,12 @@
     return pl.pallas_call(
         middle_kernel,
         out_shape=(
-            jax.ShapeDtypeStruct((CHIPS, rows + 8, width), jnp.bfloat16),
+            pltpu.HBM((CHIPS, rows + 8, width), jnp.bfloat16),
             jax.ShapeDtypeStruct((rows + rows // 4, width), jnp.bfloat16),
         ),
         in_specs=[VMEM_SPEC] * 2,
-        out_specs=(VMEM_SPEC,) * 2,
+        out_specs=(HBM_SPEC, VMEM_SPEC),
+        scratch_shapes=[pltpu.VMEM((rows + 8, width), jnp.bfloat16), pltpu.SemaphoreType.DMA((CHIPS,))],
         compiler_params=pltpu.CompilerParams(vmem_limit_bytes=VMEM),
         cost_estimate=cost(30 * rows * width, 8 * rows * width * 4),
     )(r, ops)
@@ -263,7 +267,7 @@
 
 
 def near_back_kernel(place, g_ref, half_ref, w_ref, acc_ref, next_ref, sems):
-    copies = halves(w_ref, next_ref, sems, place[2])
+    copies = halves(w_ref, next_ref, sems, place[2], 1)
     start(copies)
     rows = acc_ref.shape[1]
     acc = None
@@ -281,7 +285,10 @@
     rows = high - 8
     return pl.pallas_call(
         near_back_kernel,
-        out_shape=(pltpu.VMEM((2, rows, width), jnp.float32), pltpu.VMEM(half_shape(w), w.dtype)),
+        out_shape=(
+            pltpu.VMEM((2, rows, width), jnp.float32),
+            pltpu.VMEM((LINE - 1, w.shape[0], w.shape[0]), w.dtype),
+        ),
         in_specs=[SMEM_SPEC, VMEM_SPEC, VMEM_SPEC, HBM_SPEC],
         out_specs=(VMEM_SPEC, VMEM_SPEC),
         scratch_shapes=[SEMS],
@@ -290,18 +297,18 @@
     )(place, in_vmem(g), in_vmem(half), in_hbm(w))
 
 
-def far_rows(which, g_ref, half_ref, acc_ref):
+def far_rows(which, g_ref, first_ref, rest_ref, acc_ref):
     rows = acc_ref.shape[1]
-    acc = acc_ref[which]
-    for i in range(LINE):
-        acc = acc + against(g_ref[which, i, :rows], half_ref[i])
+    acc = acc_ref[which] + against(g_ref[which, 0, :rows], first_ref[0])
+    for i in range(1, LINE):
+        acc = acc + against(g_ref[which, i, :rows], rest_ref[i - 1])
     return acc
 
 
-def send_kernel(place, g_ref, near_ref, w_ref, acc_ref, back_ref, send_ref, bias_ref):
+def send_kernel(place, g_ref, near_ref, first_ref, rest_ref, acc_ref, back_ref, send_ref, bias_ref):
     rows, width = acc_ref.shape[1:]
     other = 1 - place[0]
-    send_ref[0:rows] = far_rows(other, g_ref, w_ref, acc_ref).astype(jnp.bfloat16)
+    send_ref[0:rows] = far_rows(other, g_ref, first_ref, rest_ref, acc_ref).astype(jnp.bfloat16)
     bias = []
     for k in range(2):
         lines = jnp.zeros((8, width), jnp.float32)
@@ -315,7 +322,7 @@
     send_ref[rows + 8 :] = back_ref[rows:]
 
 
-def send_rows(place, g, near, w, acc, back):
+def send_rows(place, g, near, first, rest, acc, back):
     _, rows, width = acc.shape
     return pl.pallas_call(
         send_kernel,
@@ -323,32 +330,32 @@
             jax.ShapeDtypeStruct((back.shape[0] + 8, width), jnp.bfloat16),
             jax.ShapeDtypeStruct((8, width), jnp.float32),
         ),
+        in_specs=[SMEM_SPEC] + [VMEM_SPEC] * 6,
+        out_specs=(VMEM_SPEC,) * 2,
+        compiler_params=pltpu.CompilerParams(vmem_limit_bytes=VMEM),
+        cost_estimate=cost(2 * rows * width * width * LINE, width * width * LINE * 2),
+    )(place, *map(in_vmem, (g, near, first, rest, acc)), back)
+
+
+def as_boxes(rows, like):
+    return rows.astype(jnp.float32).reshape(like.shape).astype(like.dtype)
+
+
+def keep_kernel(place, g_ref, first_ref, rest_ref, acc_ref, back_ref, keep_ref, relaxed_ref):
+    keep_ref[...] = far_rows(place[0], g_ref, first_ref, rest_ref, acc_ref)
+    relaxed_ref[...] = as_boxes(back_ref[: keep_ref.shape[0]], relaxed_ref)
+
+
+def keep_rows(place, g, first, rest, acc, back, shape):
+    _, rows, width = acc.shape
+    return pl.pallas_call(
+        keep_kernel,
+        out_shape=(jax.ShapeDtypeStruct((rows, width), jnp.float32), jax.ShapeDtypeStruct(shape, jnp.bfloat16)),
         in_specs=[SMEM_SPEC] + [VMEM_SPEC] * 5,
         out_specs=(VMEM_SPEC,) * 2,
         compiler_params=pltpu.CompilerParams(vmem_limit_bytes=VMEM),
         cost_estimate=cost(2 * rows * width * width * LINE, width * width * LINE * 2),
-    )(place, in_vmem(g), in_vmem(near), in_vmem(w), in_vmem(acc), back)
-
-
-def as_boxes(rows, like):
-    return rows.astype(jnp.float32).reshape(like.shape).astype(like.dtype)
-
-
-def keep_kernel(place, g_ref, w_ref, acc_ref, back_ref, keep_ref, relaxed_ref):
-    keep_ref[...] = far_rows(place[0], g_ref, w_ref, acc_ref)
-    relaxed_ref[...] = as_boxes(back_ref[: keep_ref.shape[0]], relaxed_ref)
-
-
-def keep_rows(place, g, w, acc, back, shape):
-    _, rows, width = acc.shape
-    return pl.pallas_call(
-        keep_kernel,
-        out_shape=(jax.ShapeDtypeStruct((rows, width), jnp.float32), jax.ShapeDtypeStruct(shape, jnp.bfloat16)),
-        in_specs=[SMEM_SPEC] + [VMEM_SPEC] * 4,
-        out_specs=(VMEM_SPEC,) * 2,
-        compiler_params=pltpu.CompilerParams(vmem_limit_bytes=VMEM),
-        cost_estimate=cost(2 * rows * width * width * LINE, width * width * LINE * 2),
-    )(place, in_vmem(g), in_vmem(w), in_vmem(acc), back)
+    )(place, *map(in_vmem, (g, first, rest, acc)), back)
 
 
 def finish_kernel(keep_ref, recv_ref, bias_ref, back_ref, grad_ref, offset_ref, slope_ref):
@@ -412,16 +419,16 @@
 
     grads = lax.all_to_all(grad, "neuron", 0, 0, axis_index_groups=SAME_CORE, tiled=True)
     back = lax.ppermute(back, BOTH, MIDDLE_SWAP)
-    half = stage(near, weight)
+    half, first = stage(near, weight)
     grads, back = lax.optimization_barrier((grads, back))
 
     far_grads = lax.ppermute(grads, "neuron", CORE_SWAP)
     four = (2, LINE, rows + 8, width)
     grads, far_grads = grads.reshape(four), far_grads.reshape(four)
-    acc, other_half = near_back(near, grads, half, weight)
-    send, bias = send_rows(near, far_grads, grads, other_half, acc, back)
+    acc, rest = near_back(near, grads, half, weight)
+    send, bias = send_rows(near, far_grads, grads, first, rest, acc, back)
     recv = lax.ppermute(send, "spec", SPEC_SWAP)
-    keep, new_coeff = keep_rows(near, far_grads, other_half, acc, back, coeff.shape)
+    keep, new_coeff = keep_rows(near, far_grads, first, rest, acc, back, coeff.shape)
     coeff_grad, offset, slope_grad = finish(keep, recv, bias, back, nboxes)
     return new_coeff, offset.T, slope_grad, coeff_grad
 

time: 76.9 us -> 77 us (level)
  no operation moved by 1% of the time
where the time goes in v4:
time: 77 us; the launch traced here: 76.5 us
  waiting for transfers between devices  30 us (39%)
  starting transfers between devices  27.4 us (36%)
  Pallas kernels  16.7 us (22%)
  other arithmetic  1.63 us (2%)
  between operations  0.82 us (1%)
    all_to_all x1, waiting for transfers between devices, step(): lax.all_to_all(grad, 'neuron', 0, 0, axis_index_groups=SAME_CORE, tiled=T...  13 us
    all_to_all x1, waiting for transfers between devices, step(): lax.all_to_all(chunks, 'neuron', 0, 0, axis_index_groups=SAME_CORE, tiled...  12.3 us
    ppermute x1, starting transfers between devices, step(): came = lax.ppermute(away, 'neuron', CORE_SWAP)  8.67 us
    ppermute x1, starting transfers between devices, step(): other = lax.ppermute(coeff, 'spec', SPEC_SWAP)  5.64 us
    ppermute x1, waiting for transfers between devices, step(): recv = lax.ppermute(send, 'spec', SPEC_SWAP)  4.65 us
    all_to_all x1, starting transfers between devices, step(): lax.all_to_all(grad, 'neuron', 0, 0, axis_index_groups=SAME_CORE, tiled=T...  3.56 us
    all_to_all x1, starting transfers between devices, step(): lax.all_to_all(chunks, 'neuron', 0, 0, axis_index_groups=SAME_CORE, tiled...  3.55 us
    ppermute x1, starting transfers between devices, step(): far_grads = lax.ppermute(grads, 'neuron', CORE_SWAP)  2.68 us
  transfers between devices with their start and end apart: 8, of which 3 were waited for; matrix products, arithmetic and copies ran while one was open for 0% of the time, Pallas kernels for 15%

profile of v4, /device:TPU:1, one launch (start us, length us, event | category | flops | bytes accessed | tf_op | source)
XLA Modules:
  0.0 76.5 jit_solution(17933743988371657572)
XLA Ops:
  0.6 5.6 %collective-permute-start = (bf16[24,4,512]{2,1,0:T(4,128)(2,1)}, bf16[24,4,512]{2,1,0:T(4,128)(2,1)S(1)}, u32[]{:S(2)}, u32[]{:S(2)}) collective-permute-start(bf16[24,4,512]{2,1,0:T(4,128)(2,1)} %refs_5_.1), channel_id=1, source_target_pairs={{0,1},{1,0},{2,3},{3,2},{4,5},{5,4},{6,7},{7,6},{8,9},{9,8},{10,11... | collective-permute-start | bytes 294920 | tf_op jit(solution)/shard_map/ppermute | solution.py:405
  6.4 2.5 %shard_map.102 = (bf16[240,512]{1,0:T(8,128)(2,1)S(1)}, bf16[96,512]{1,0:T(8,128)(2,1)S(1)}, bf16[4,512,512]{2,1,0:T(8,128)(2,1)S(1)}, bf16[1,512,512]{2,1,0:T(8,128)(2,1)S(1)}) custom-call(s32[3]{0:T(128)S(1)} %pad_add_fusion.1.place, bf16[512,4096]{1,0:T(8,128)(2,1)} %w_ref.7, f32[24,512]{1,0:T(8,128)} %refs_0_.1, f32[24,512]{1,0:T(8,128)} %refs_1_.1, ...), custom_call_target="tpu_custom_call" | custom-call | bytes 4194304 | tf_op jit(solution)/shard_map/pallas_call | solution.py:195
  9.0 1.1 %shard_map.104 = f32[8,96,512]{2,1,0:T(8,128)S(1)} custom-call(s32[3]{0:T(128)S(1)} %pad_add_fusion.1.place, bf16[96,512]{1,0:T(8,128)(2,1)S(1)} %get-tuple-element.23.own_ref, bf16[96,512]{1,0:T(8,128)(2,1)S(1)} %reshape.17.other_ref, bf16[4,512,512]{2,1,0:T(8,128)(2,1)S(1)} %get-tuple-element.25.half_ref), custom_call_target="tpu_custom_call" | custom-call | flops 402653184 | bytes 2097152 | tf_op jit(solution)/shard_map/pallas_call | solution.py:127
  10.1 0.2 convert_element_type.12
  10.3 8.7 %collective-permute-start.1 = (f16[8,96,512]{2,1,0:T(8,128)(2,1)S(1)}, f16[8,96,512]{2,1,0:T(8,128)(2,1)S(1)}, u32[]{:S(2)}, u32[]{:S(2)}) collective-permute-start(f16[8,96,512]{2,1,0:T(8,128)(2,1)S(1)} %convert_element_type.12), channel_id=1, source_target_pairs={{0,32},{32,0},{64,96},{96,64},{128,160},{160,128},{192,224},{224,1... | collective-permute-start | bytes 2359304 | tf_op jit(solution)/shard_map/ppermute | solution.py:412
  19.0 0.1 pad_add_fusion.place
  19.0 2.5 %shard_map.103 = f32[8,96,512]{2,1,0:T(8,128)S(1)} custom-call(s32[3]{0:T(128)S(1)} %pad_add_fusion.place, bf16[96,512]{1,0:T(8,128)(2,1)S(1)} %get-tuple-element.23.own_ref, bf16[96,512]{1,0:T(8,128)(2,1)S(1)} %reshape.17.other_ref, bf16[1,512,512]{2,1,0:T(8,128)(2,1)S(1)} %get-tuple-element.24.first_ref, bf16[512,4096]{1,0:T(8,128)(2,1)} %w_ref.7), custom_call_target="tpu_custom_call" | custom-call | flops 402653184 | bytes 2097152 | tf_op jit(solution)/shard_map/pallas_call | solution.py:149
  21.5 1.2 %add_convert_fusion = f16[8,96,512]{2,1,0:T(8,128)(2,1)} fusion(f32[8,96,512]{2,1,0:T(8,128)S(1)} %shard_map.103, f16[8,96,512]{2,1,0:T(8,128)(2,1)S(1)} %collective-permute-done.1), kind=kLoop, calls=%fused_computation.1 | loop fusion | flops 1179648 | bytes 3145728 | tf_op jit(solution)/shard_map/convert_element_type | solution.py:414
  22.7 3.5 %all-to-all-start = ((f16[8,96,512]{2,1,0:T(8,128)(2,1)}), f16[8,96,512]{2,1,0:T(8,128)(2,1)S(1)}, u32[]{:S(2)}, u32[]{:S(2)}) async-start(f16[8,96,512]{2,1,0:T(8,128)(2,1)} %add_convert_fusion), calls=%async_computation | async-start | bytes 1572864 | tf_op jit(solution)/shard_map/all_to_all | solution.py:416
  26.3 0.7 collective-permute-start.2
  27.0 12.3 %all-to-all-done = f16[8,96,512]{2,1,0:T(8,128)(2,1)S(1)} async-done(((f16[8,96,512]{2,1,0:T(8,128)(2,1)}), f16[8,96,512]{2,1,0:T(8,128)(2,1)S(1)}, u32[]{:S(2)}, u32[]{:S(2)}) %all-to-all-start) | async-done | bytes 786464 | tf_op jit(solution)/shard_map/all_to_all | solution.py:416
  39.3 0.1 convert_reduce_fusion
  39.4 1.6 %shard_map.105 = (bf16[8,104,512]{2,1,0:T(8,128)(2,1)}, bf16[120,512]{1,0:T(8,128)(2,1)S(1)}) custom-call(f32[96,512]{1,0:T(8,128)S(1)} %broadcast_multiply_fusion.r_ref, bf16[240,512]{1,0:T(8,128)(2,1)S(1)} %collective-permute-done.2.ops_ref), custom_call_target="tpu_custom_call" | custom-call | flops 1474560 | bytes 1572864 | tf_op jit(solution)/shard_map/pallas_call | solution.py:251
  41.1 3.6 %all-to-all-start.1 = ((bf16[8,104,512]{2,1,0:T(8,128)(2,1)}), bf16[8,104,512]{2,1,0:T(8,128)(2,1)S(1)}, u32[]{:S(2)}, u32[]{:S(2)}) async-start(bf16[8,104,512]{2,1,0:T(8,128)(2,1)} %get-tuple-element.27), calls=%async_computation.1 | async-start | bytes 1703936 | tf_op jit(solution)/shard_map/all_to_all | solution.py:420
  44.6 0.7 collective-permute-start.3
  45.3 13.0 %all-to-all-done.1 = bf16[8,104,512]{2,1,0:T(8,128)(2,1)S(1)} async-done(((bf16[8,104,512]{2,1,0:T(8,128)(2,1)}), bf16[8,104,512]{2,1,0:T(8,128)(2,1)S(1)}, u32[]{:S(2)}, u32[]{:S(2)}) %all-to-all-start.1) | async-done | bytes 852000 | tf_op jit(solution)/shard_map/all_to_all | solution.py:420
  58.3 2.7 %collective-permute-start.4 = (bf16[8,104,512]{2,1,0:T(8,128)(2,1)S(1)}, bf16[8,104,512]{2,1,0:T(8,128)(2,1)S(1)}, u32[]{:S(2)}, u32[]{:S(2)}) collective-permute-start(bf16[8,104,512]{2,1,0:T(8,128)(2,1)S(1)} %all-to-all-done.1), channel_id=1, source_target_pairs={{0,32},{32,0},{64,96},{96,64},{128,160},{160,128},{192,224},{224,1... | collective-permute-start | bytes 2555912 | tf_op jit(solution)/shard_map/ppermute | solution.py:425
  61.0 2.4 %shard_map.106 = (bf16[4,512,512]{2,1,0:T(8,128)(2,1)S(1)}, bf16[1,512,512]{2,1,0:T(8,128)(2,1)S(1)}) custom-call(s32[3]{0:T(128)S(1)} %pad_add_fusion.place, bf16[512,4096]{1,0:T(8,128)(2,1)} %w_ref.7), custom_call_target="tpu_custom_call" | custom-call | bytes 4194304 | tf_op jit(solution)/shard_map/pallas_call | solution.py:100
  63.4 2.6 %shard_map.107 = (f32[2,96,512]{2,1,0:T(8,128)S(1)}, bf16[3,512,512]{2,1,0:T(8,128)(2,1)S(1)}) custom-call(s32[3]{0:T(128)S(1)} %pad_add_fusion.place, bf16[2,4,104,512]{3,2,1,0:T(8,128)(2,1)S(1)} %bitcast.6, bf16[4,512,512]{2,1,0:T(8,128)(2,1)S(1)} %get-tuple-element.31.half_ref, bf16[512,4096]{1,0:T(8,128)(2,1)} %w_ref.7), custom_call_target="tpu_custom_call" | custom-call | flops 402653184 | bytes 2097152 | tf_op jit(solution)/shard_map/pallas_call | solution.py:286
  66.0 1.3 %shard_map.109 = (bf16[128,512]{1,0:T(8,128)(2,1)S(1)}, f32[8,512]{1,0:T(8,128)S(1)}) custom-call(s32[3]{0:T(128)S(1)} %pad_add_fusion.place, bf16[2,4,104,512]{3,2,1,0:T(8,128)(2,1)S(1)} %bitcast.8, bf16[2,4,104,512]{3,2,1,0:T(8,128)(2,1)S(1)} %bitcast.7, bf16[1,512,512]{2,1,0:T(8,128)(2,1)S(1)} %get-tuple-element.30.first_ref, ...), custom_call_target="tpu_custom_call" | custom-call | flops 201326592 | bytes 2097152 | tf_op jit(solution)/shard_map/pallas_call | solution.py:327
  67.3 1.9 %collective-permute-start.5 = (bf16[128,512]{1,0:T(8,128)(2,1)S(1)}, bf16[128,512]{1,0:T(8,128)(2,1)S(1)}, u32[]{:S(2)}, u32[]{:S(2)}) collective-permute-start(bf16[128,512]{1,0:T(8,128)(2,1)S(1)} %get-tuple-element.37), channel_id=1, source_target_pairs={{0,1},{1,0},{2,3},{3,2},{4,5},{5,4},{6,7},{7,6},{8,9},{9,8},{10,11... | collective-permute-start | bytes 393224 | tf_op jit(solution)/shard_map/ppermute | solution.py:430
  69.2 1.9 %shard_map.108 = (f32[96,512]{1,0:T(8,128)S(1)}, bf16[24,4,512]{2,1,0:T(4,128)(2,1)}) custom-call(s32[3]{0:T(128)S(1)} %pad_add_fusion.place, bf16[2,4,104,512]{3,2,1,0:T(8,128)(2,1)S(1)} %bitcast.9, bf16[1,512,512]{2,1,0:T(8,128)(2,1)S(1)} %get-tuple-element.30.first_ref, bf16[3,512,512]{2,1,0:T(8,128)(2,1)S(1)} %get-tuple-element.32.rest_ref, ...), custom_call_target="tpu_custom_call" | custom-call | flops 201326592 | bytes 2097152 | tf_op jit(solution)/shard_map/pallas_call | solution.py:351
  71.1 4.7 %collective-permute-done.5.recv_ref = bf16[128,512]{1,0:T(8,128)(2,1)S(1)} collective-permute-done((bf16[128,512]{1,0:T(8,128)(2,1)S(1)}, bf16[128,512]{1,0:T(8,128)(2,1)S(1)}, u32[]{:S(2)}, u32[]{:S(2)}) %collective-permute-start.5) | collective-permute-done | bytes 131104 | tf_op jit(solution)/shard_map/ppermute | solution.py:430
  75.7 0.8 %shard_map.110 = (bf16[24,4,512]{2,1,0:T(4,128)(2,1)}, f32[4,24]{1,0:T(4,128)}, f32[24,512]{1,0:T(8,128)}) custom-call(f32[96,512]{1,0:T(8,128)S(1)} %get-tuple-element.36.keep_ref, bf16[128,512]{1,0:T(8,128)(2,1)S(1)} %collective-permute-done.5.recv_ref, f32[8,512]{1,0:T(8,128)S(1)} %get-tuple-element.38.bias_ref, ...), custom_call_target="tpu_custom_call" | custom-call | bytes 196608 | tf_op jit(solution)/shard_map/pallas_call | solution.py:383
  (8 shorter events, 0.1 us)
Async XLA Ops:
  0.6 8.3 %collective-permute-start = (bf16[24,4,512]{2,1,0:T(4,128)(2,1)}, bf16[24,4,512]{2,1,0:T(4,128)(2,1)S(1)}, u32[]{:S(2)}, u32[]{:S(2)}) collective-permute-start(bf16[24,4,512]{2,1,0:T(4,128)(2,1)} %refs_5_.1), channel_id=1, source_target_pairs={{0,1},{1,0},{2,3},{3,2},{4,5},{5,4},{6,7},{7,6},{8,9},{9,8},{10,11... | collective-permute-start | bytes 294920 | tf_op jit(solution)/shard_map/ppermute | solution.py:405
  10.3 11.3 %collective-permute-start.1 = (f16[8,96,512]{2,1,0:T(8,128)(2,1)S(1)}, f16[8,96,512]{2,1,0:T(8,128)(2,1)S(1)}, u32[]{:S(2)}, u32[]{:S(2)}) collective-permute-start(f16[8,96,512]{2,1,0:T(8,128)(2,1)S(1)} %convert_element_type.12), channel_id=1, source_target_pairs={{0,32},{32,0},{64,96},{96,64},{128,160},{160,128},{192,224},{224,1... | collective-permute-start | bytes 2359304 | tf_op jit(solution)/shard_map/ppermute | solution.py:412
  22.7 16.6 %all-to-all-start = ((f16[8,96,512]{2,1,0:T(8,128)(2,1)}), f16[8,96,512]{2,1,0:T(8,128)(2,1)S(1)}, u32[]{:S(2)}, u32[]{:S(2)}) async-start(f16[8,96,512]{2,1,0:T(8,128)(2,1)} %add_convert_fusion), calls=%async_computation | async-start | bytes 1572864 | tf_op jit(solution)/shard_map/all_to_all | solution.py:416
  26.3 13.1 %collective-permute-start.2 = (bf16[240,512]{1,0:T(8,128)(2,1)S(1)}, bf16[240,512]{1,0:T(8,128)(2,1)S(1)}, u32[]{:S(2)}, u32[]{:S(2)}) collective-permute-start(bf16[240,512]{1,0:T(8,128)(2,1)S(1)} %get-tuple-element.26), channel_id=1, source_target_pairs={{0,0},{1,256},{32,32},{33,288},{64,64},{65,320},{96,96},{97,352},{... | collective-permute-start | bytes 737288 | tf_op jit(solution)/shard_map/ppermute | solution.py:408
  41.1 17.3 %all-to-all-start.1 = ((bf16[8,104,512]{2,1,0:T(8,128)(2,1)}), bf16[8,104,512]{2,1,0:T(8,128)(2,1)S(1)}, u32[]{:S(2)}, u32[]{:S(2)}) async-start(bf16[8,104,512]{2,1,0:T(8,128)(2,1)} %get-tuple-element.27), calls=%async_computation.1 | async-start | bytes 1703936 | tf_op jit(solution)/shard_map/all_to_all | solution.py:420
  44.6 0.7 collective-permute-start.3
  58.3 7.7 %collective-permute-start.4 = (bf16[8,104,512]{2,1,0:T(8,128)(2,1)S(1)}, bf16[8,104,512]{2,1,0:T(8,128)(2,1)S(1)}, u32[]{:S(2)}, u32[]{:S(2)}) collective-permute-start(bf16[8,104,512]{2,1,0:T(8,128)(2,1)S(1)} %all-to-all-done.1), channel_id=1, source_target_pairs={{0,32},{32,0},{64,96},{96,64},{128,160},{160,128},{192,224},{224,1... | collective-permute-start | bytes 2555912 | tf_op jit(solution)/shard_map/ppermute | solution.py:425
  67.3 8.4 %collective-permute-start.5 = (bf16[128,512]{1,0:T(8,128)(2,1)S(1)}, bf16[128,512]{1,0:T(8,128)(2,1)S(1)}, u32[]{:S(2)}, u32[]{:S(2)}) collective-permute-start(bf16[128,512]{1,0:T(8,128)(2,1)S(1)} %get-tuple-element.37), channel_id=1, source_target_pairs={{0,1},{1,0},{2,3},{3,2},{4,5},{5,4},{6,7},{7,6},{8,9},{9,8},{10,11... | collective-permute-start | bytes 393224 | tf_op jit(solution)/shard_map/ppermute | solution.py:430

commit v5 on v3

v5 whole, which is shorter than its diff:
```python
import functools

import jax
import jax.numpy as jnp
from jax import lax
from jax.experimental import pallas as pl
from jax.experimental.pallas import tpu as pltpu
from jax.sharding import PartitionSpec as P


D = 8192

CHIPS = 8
LINE = 4
VMEM = 24 * 1024 * 1024
SCALE = 64.0

BOTH = ("neuron", "spec")
CORE_SWAP = [(n, n ^ 1) for n in range(16)]
SPEC_SWAP = [(0, 1), (1, 0)]
SAME_CORE = [[n for n in range(16) if n % 2 == core] for core in range(2)]


def middle_swap():
    pairs = []
    for n in range(16):
        for s in range(2):
            y_lo, rest = n // 8, n % 8
            pairs.append((n * 2 + s, (s * 8 + rest) * 2 + y_lo))
    return pairs


MIDDLE_SWAP = middle_swap()


def columns(w_ref, i, core):
    width = w_ref.shape[0]
    return w_ref[:, pl.ds(pl.multiple_of((2 * i + core) * width, width), width)]


def in_hbm(w):
    return pltpu.with_memory_space_constraint(w, pltpu.HBM)


def in_vmem(w):
    return pltpu.with_memory_space_constraint(w, pltpu.VMEM)


VMEM_SPEC = pl.BlockSpec(memory_space=pltpu.VMEM)
HBM_SPEC = pl.BlockSpec(memory_space=pltpu.HBM)


def cost(flops, moved):
    return pl.CostEstimate(flops=flops, bytes_accessed=moved, transcendentals=0)


def spec_and_core():
    return lax.axis_index("spec"), lax.rem(lax.axis_index("neuron"), 2)


def part_kernel(partner, own_ref, other_ref, w_ref, out_ref):
    rows, width = own_ref.shape
    other = other_ref[...].astype(jnp.float32).reshape(rows, width).astype(jnp.bfloat16)
    both = jnp.concatenate([own_ref[...], other], axis=0)
    own, core = spec_and_core()
    core = 1 - core if partner else core
    for i in range(LINE):
        acc = jnp.dot(both, columns(w_ref, i, core), preferred_element_type=jnp.float32) * SCALE
        out_ref[pl.ds(own * LINE + i, 1)] = acc[:rows][None]
        out_ref[pl.ds((1 - own) * LINE + i, 1)] = acc[rows:][None]


def part_sums(partner, own, other, w):
    rows, width = own.shape
    return pl.pallas_call(
        functools.partial(part_kernel, partner),
        out_shape=jax.ShapeDtypeStruct((CHIPS, rows, width), jnp.float32),
        in_specs=[VMEM_SPEC] * 3,
        out_specs=VMEM_SPEC,
        compiler_params=pltpu.CompilerParams(vmem_limit_bytes=VMEM),
        cost_estimate=cost(2 * 2 * rows * width * width * LINE, width * width * LINE * 2),
    )(in_vmem(own), other, in_vmem(w))


def prepare_kernel(*refs):
    w_ref, given, (whole_ref, out_ref, own_ref) = refs[0], refs[1:7], refs[7:10]
    held, sems, w_sems = refs[10:16], refs[16], refs[17]
    copies = [pltpu.make_async_copy(given[k], held[k], sems.at[k]) for k in range(6)]
    for copy in copies:
        copy.start()
    tall = w_ref.shape[0] // LINE
    fetches = [
        pltpu.make_async_copy(w_ref.at[pl.ds(i * tall, tall)], whole_ref.at[pl.ds(i * tall, tall)], w_sems.at[i])
        for i in range(LINE)
    ]
    for fetch in fetches:
        fetch.start()
    for copy in copies:
        copy.wait()
    upper, depth, slopes, state = (held[k][...] for k in range(4))
    adj_ref, coeff_ref = held[4:]
    boxes, specs, width = adj_ref.shape
    rows = boxes * specs
    out_ref[0:rows] = adj_ref[...].astype(jnp.float32).reshape(rows, width).astype(jnp.bfloat16)
    own_ref[...] = coeff_ref[...].astype(jnp.float32).reshape(rows, width).astype(jnp.bfloat16)
    unstable = state == 2
    total = upper + depth
    one = jnp.where(state == 1, 1.0, 0.0)
    values = (
        jnp.where(unstable, slopes, one),
        jnp.where(unstable, upper / total, one),
        jnp.where(unstable, upper * depth / total, 0.0),
    )
    for value in values:
        high = value.astype(jnp.bfloat16)
        out_ref[rows : rows + boxes] = high
        out_ref[rows + boxes : rows + 2 * boxes] = (value - high.astype(jnp.float32)).astype(jnp.bfloat16)
        rows += 2 * boxes
    for fetch in fetches:
        fetch.wait()


def prepare(w, *given):
    boxes, specs, width = given[4].shape
    return pl.pallas_call(
        prepare_kernel,
        out_shape=(
            pltpu.VMEM(w.shape, w.dtype),
            pltpu.VMEM((boxes * (specs + 6), width), jnp.bfloat16),
            pltpu.VMEM((boxes * specs, width), jnp.bfloat16),
        ),
        in_specs=[HBM_SPEC] * 7,
        out_specs=(VMEM_SPEC,) * 3,
        scratch_shapes=[pltpu.VMEM(x.shape, x.dtype) for x in given] + [pltpu.SemaphoreType.DMA((6,)), pltpu.SemaphoreType.DMA((LINE,))],
        compiler_params=pltpu.CompilerParams(vmem_limit_bytes=VMEM),
        cost_estimate=cost(0, w.size * 2),
    )(*map(in_hbm, (w, *given)))


def middle_kernel(r_ref, ops_ref, g_ref, back_ref):
    pre = r_ref[...]
    rows, width = pre.shape
    boxes = (ops_ref.shape[0] - rows) // 6
    specs = rows // boxes

    def operand(k):
        at = rows + 2 * k * boxes
        value = ops_ref[at : at + boxes].astype(jnp.float32) + ops_ref[at + boxes : at + 2 * boxes].astype(jnp.float32)
        return jnp.broadcast_to(value[:, None, :], (boxes, specs, width)).reshape(rows, width)

    a, b, c = operand(0), operand(1), operand(2)
    positive = jnp.maximum(pre, 0.0)
    negative = jnp.minimum(pre, 0.0)
    cot = ops_ref[0:rows].astype(jnp.float32)
    back_ref[0:rows] = (a * positive + b * negative).astype(jnp.bfloat16)
    grad = (cot * jnp.where(pre > 0.0, a, b)).astype(jnp.bfloat16)
    for k in range(CHIPS):
        g_ref[k, 0:rows] = grad
    line = lax.dot_general(
        jnp.ones((8, width), jnp.float32),
        negative * c,
        (((1,), (1,)), ((), ())),
        precision=lax.Precision.HIGHEST,
        preferred_element_type=jnp.float32,
    ) * (float(D) ** -0.5)
    high = line.astype(jnp.bfloat16).astype(jnp.float32)
    row = lax.broadcasted_iota(jnp.int32, line.shape, 0)
    tile = jnp.where(row == 0, high, jnp.where(row == 1, line - high, 0.0))
    tile = jnp.concatenate([tile, jnp.zeros((8, width - rows), jnp.float32)], axis=1).astype(jnp.bfloat16)
    for k in range(CHIPS):
        g_ref[k, rows : rows + 8] = tile
    slope = jnp.where(c > 0.0, cot * positive, 0.0).reshape(boxes, specs, width)
    back_ref[rows : rows + boxes] = jnp.sum(slope, axis=1).astype(jnp.bfloat16)


def middle(r, ops):
    rows, width = r.shape
    return pl.pallas_call(
        middle_kernel,
        out_shape=(
            jax.ShapeDtypeStruct((CHIPS, rows + 8, width), jnp.bfloat16),
            jax.ShapeDtypeStruct((rows + rows // 4, width), jnp.bfloat16),
        ),
        in_specs=[VMEM_SPEC] * 2,
        out_specs=(VMEM_SPEC,) * 2,
        compiler_params=pltpu.CompilerParams(vmem_limit_bytes=VMEM),
        cost_estimate=cost(30 * rows * width, 8 * rows * width * 4),
    )(r, ops)


def against(g, block):
    return lax.dot_general(g, block, (((1,), (1,)), ((), ())), preferred_element_type=jnp.float32)


def near_back_kernel(g_ref, w_ref, acc_ref):
    rows = acc_ref.shape[1]
    _, core = spec_and_core()
    acc = None
    for i in range(LINE):
        both = jnp.concatenate([g_ref[0, i, :rows], g_ref[1, i, :rows]], axis=0)
        part = against(both, columns(w_ref, i, core))
        acc = part if acc is None else acc + part
    acc_ref[0] = acc[:rows]
    acc_ref[1] = acc[rows:]


def near_back(g, w):
    _, _, high, width = g.shape
    rows = high - 8
    return pl.pallas_call(
        near_back_kernel,
        out_shape=pltpu.VMEM((2, rows, width), jnp.float32),
        in_specs=[VMEM_SPEC, VMEM_SPEC],
        out_specs=VMEM_SPEC,
        compiler_params=pltpu.CompilerParams(vmem_limit_bytes=VMEM),
        cost_estimate=cost(2 * 2 * rows * width * width * LINE, width * width * LINE * 2),
    )(in_vmem(g), in_vmem(w))


def far_rows(which, core, g_ref, w_ref, acc_ref):
    rows = acc_ref.shape[1]
    acc = acc_ref[which]
    for i in range(LINE):
        acc = acc + against(g_ref[which, i, :rows], columns(w_ref, i, 1 - core))
    return acc


def send_kernel(g_ref, near_ref, w_ref, acc_ref, back_ref, send_ref, bias_ref):
    rows, width = acc_ref.shape[1:]
    own, core = spec_and_core()
    other = 1 - own
    send_ref[0:rows] = far_rows(other, core, g_ref, w_ref, acc_ref).astype(jnp.bfloat16)
    bias = []
    for k in range(2):
        lines = jnp.zeros((8, width), jnp.float32)
        for i in range(LINE):
            lines = lines + g_ref[k, i, rows : rows + 8].astype(jnp.float32)
            lines = lines + near_ref[k, i, rows : rows + 8].astype(jnp.float32)
        bias.append(jnp.sum(lines, axis=0, keepdims=True))
    first = other == 1
    bias_ref[...] = jnp.broadcast_to(jnp.where(first, bias[0], bias[1]), bias_ref.shape)
    send_ref[rows : rows + 8] = jnp.broadcast_to(jnp.where(first, bias[1], bias[0]), (8, width)).astype(jnp.bfloat16)
    send_ref[rows + 8 :] = back_ref[rows:]


def send_rows(g, near, w, acc, back):
    _, rows, width = acc.shape
    return pl.pallas_call(
        send_kernel,
        out_shape=(
            jax.ShapeDtypeStruct((back.shape[0] + 8, width), jnp.bfloat16),
            jax.ShapeDtypeStruct((8, width), jnp.float32),
        ),
        in_specs=[VMEM_SPEC] * 5,
        out_specs=(VMEM_SPEC,) * 2,
        compiler_params=pltpu.CompilerParams(vmem_limit_bytes=VMEM),
        cost_estimate=cost(2 * rows * width * width * LINE, width * width * LINE * 2),
    )(in_vmem(g), in_vmem(near), in_vmem(w), in_vmem(acc), back)


def as_boxes(rows, like):
    return rows.astype(jnp.float32).reshape(like.shape).astype(like.dtype)


def keep_kernel(g_ref, w_ref, acc_ref, back_ref, keep_ref, relaxed_ref):
    own, core = spec_and_core()
    keep_ref[...] = far_rows(own, core, g_ref, w_ref, acc_ref)
    relaxed_ref[...] = as_boxes(back_ref[: keep_ref.shape[0]], relaxed_ref)


def keep_rows(g, w, acc, back, shape):
    _, rows, width = acc.shape
    return pl.pallas_call(
        keep_kernel,
        out_shape=(jax.ShapeDtypeStruct((rows, width), jnp.float32), jax.ShapeDtypeStruct(shape, jnp.bfloat16)),
        in_specs=[VMEM_SPEC] * 4,
        out_specs=(VMEM_SPEC,) * 2,
        compiler_params=pltpu.CompilerParams(vmem_limit_bytes=VMEM),
        cost_estimate=cost(2 * rows * width * width * LINE, width * width * LINE * 2),
    )(in_vmem(g), in_vmem(w), in_vmem(acc), back)


def finish_kernel(keep_ref, recv_ref, bias_ref, back_ref, grad_ref, offset_ref, slope_ref):
    rows = keep_ref.shape[0]
    boxes, specs, _ = grad_ref.shape
    grad_ref[...] = as_boxes(keep_ref[...] + recv_ref[0:rows].astype(jnp.float32), grad_ref)
    slope_ref[...] = back_ref[rows:].astype(jnp.float32) + recv_ref[rows + 8 :].astype(jnp.float32)
    line = bias_ref[...] + recv_ref[rows : rows + 8].astype(jnp.float32)
    line = line[:specs, :rows]
    index = lax.broadcasted_iota(jnp.int32, (specs, rows), 1)
    spec = lax.broadcasted_iota(jnp.int32, (specs, rows), 0)
    box = lax.broadcasted_iota(jnp.int32, (rows, boxes), 0) // specs == lax.broadcasted_iota(
        jnp.int32, (rows, boxes), 1
    )
    offset_ref[...] = jnp.dot(
        jnp.where(index % specs == spec, line, 0.0),
        jnp.where(box, 1.0, 0.0),
        precision=lax.Precision.HIGHEST,
        preferred_element_type=jnp.float32,
    )


def finish(keep, recv, bias, back, boxes):
    rows, width = keep.shape
    return pl.pallas_call(
        finish_kernel,
        out_shape=(
            jax.ShapeDtypeStruct((boxes, rows // boxes, width), jnp.bfloat16),
            jax.ShapeDtypeStruct((rows // boxes, boxes), jnp.float32),
            jax.ShapeDtypeStruct((boxes, width), jnp.float32),
        ),
        in_specs=[VMEM_SPEC] * 4,
        out_specs=(VMEM_SPEC,) * 3,
        compiler_params=pltpu.CompilerParams(vmem_limit_bytes=VMEM),
        cost_estimate=cost(0, rows * width * 4),
    )(keep, recv, bias, back)


def step(coeff, weight, upper_bound, lower_depth, slopes, state, adjoint):
    nboxes, nspecs, width = coeff.shape
    rows = nboxes * nspecs
    other = lax.ppermute(coeff, "spec", SPEC_SWAP)
    whole, ops, own = prepare(weight, upper_bound, lower_depth, slopes, state, adjoint, coeff)
    ops = lax.ppermute(ops, BOTH, MIDDLE_SWAP)

    away = part_sums(True, own, other, whole)
    away = away.astype(jnp.float16)
    came = lax.ppermute(away, "neuron", CORE_SWAP)
    kept = part_sums(False, own, other, whole)
    chunks = (kept + came.astype(jnp.float32)).astype(jnp.float16)

    sums = lax.all_to_all(chunks, "neuron", 0, 0, axis_index_groups=SAME_CORE, tiled=True)
    pre = jnp.sum(sums.astype(jnp.float32), axis=0) * (1.0 / SCALE)
    grad, back = middle(pre, ops)

    grads = lax.all_to_all(grad, "neuron", 0, 0, axis_index_groups=SAME_CORE, tiled=True)
    grads, back = lax.optimization_barrier((grads, back))
    far_grads = lax.ppermute(grads, "neuron", CORE_SWAP)
    back = lax.ppermute(back, BOTH, MIDDLE_SWAP)
    four = (2, LINE, rows + 8, width)
    grads, far_grads = grads.reshape(four), far_grads.reshape(four)
    acc = near_back(grads, weight)
    send, bias = send_rows(far_grads, grads, weight, acc, back)
    recv = lax.ppermute(send, "spec", SPEC_SWAP)
    keep, new_coeff = keep_rows(far_grads, weight, acc, back, coeff.shape)
    coeff_grad, offset, slope_grad = finish(keep, recv, bias, back, nboxes)
    return new_coeff, offset.T, slope_grad, coeff_grad


def solution(mesh):
    return jax.shard_map(
        step,
        mesh=mesh,
        in_specs=(
            P("box", "spec", "neuron"),
            P("neuron", "spec"),
            P("box", "neuron"),
            P("box", "neuron"),
            P("box", "neuron"),
            P("box", "neuron"),
            P("box", "spec", "neuron"),
        ),
        out_specs=(
            P("box", "spec", "neuron"),
            P("box", "spec"),
            P("box", "neuron"),
            P("box", "spec", "neuron"),
        ),
        check_vma=False,
    )
```

time: 76.9 us -> 73.3 us (0.953)
  the two profiles are of different devices: /device:TPU:1 before, /device:TPU:8 now
where the time goes in v5:
time: 73.3 us; the launch traced here: 72.9 us
  starting transfers between devices  23 us (31%)
  waiting for transfers between devices  21.1 us (29%)
  blocking collectives  16.3 us (22%)
  Pallas kernels  7.98 us (11%)
  local copies, waits for them, and re-layouts  2.18 us (3%)
  other arithmetic  1.45 us (2%)
  between operations  0.75 us (1%)
    all_to_all x1, blocking collectives, step(): lax.all_to_all(grad, 'neuron', 0, 0, axis_index_groups=SAME_CORE, tiled=T...  16.3 us
    all_to_all x1, waiting for transfers between devices, step(): lax.all_to_all(chunks, 'neuron', 0, 0, axis_index_groups=SAME_CORE, tiled...  10.1 us
    all_to_all x1, starting transfers between devices, step(): lax.all_to_all(chunks, 'neuron', 0, 0, axis_index_groups=SAME_CORE, tiled...  9.26 us
    ppermute x1, waiting for transfers between devices, step(): recv = lax.ppermute(send, 'spec', SPEC_SWAP)  5.17 us
    ppermute x1, starting transfers between devices, step(): other = lax.ppermute(coeff, 'spec', SPEC_SWAP)  4.2 us
    ppermute x1, waiting for transfers between devices, step(): back = lax.ppermute(back, BOTH, MIDDLE_SWAP)  2.65 us
    pallas_call x1, Pallas kernels, prepare(): pl.pallas_call(prepare_kernel, out_shape=(pltpu.VMEM(w.shape, w.dtype), p...  2.42 us
    unnamed x2, local copies, waits for them, and re-layouts  2.18 us
  transfers between devices with their start and end apart: 7, of which 5 were waited for; matrix products, arithmetic and copies ran while one was open for 0% of the time, Pallas kernels for 7%

profile of v5, /device:TPU:8, one launch (start us, length us, event | category | flops | bytes accessed | tf_op | source)
XLA Modules:
  0.0 72.9 jit_solution(7889495439984389602)
XLA Ops:
  0.6 4.2 %collective-permute-start = (bf16[24,4,512]{2,1,0:T(4,128)(2,1)}, bf16[24,4,512]{2,1,0:T(4,128)(2,1)S(1)}, u32[]{:S(2)}, u32[]{:S(2)}) collective-permute-start(bf16[24,4,512]{2,1,0:T(4,128)(2,1)} %refs_6_.1), channel_id=1, source_target_pairs={{0,1},{1,0},{2,3},{3,2},{4,5},{5,4},{6,7},{7,6},{8,9},{9,8},{10,11... | collective-permute-start | bytes 294920 | tf_op jit(solution)/shard_map/ppermute | solution.py:322
  4.8 2.4 %shard_map.102 = (bf16[512,4096]{1,0:T(8,128)(2,1)S(1)}, bf16[240,512]{1,0:T(8,128)(2,1)S(1)}, bf16[96,512]{1,0:T(8,128)(2,1)S(1)}) custom-call(bf16[512,4096]{1,0:T(8,128)(2,1)} %w_ref.5, f32[24,512]{1,0:T(8,128)} %refs_1_.1, f32[24,512]{1,0:T(8,128)} %refs_2_.1, f32[24,512]{1,0:T(8,128)} %refs_3_.1, s32[24,512]{1,0:T(8,128)} %refs_4_.1, ...), custom_call_target="tpu_custom_call" | custom-call | bytes 4194304 | tf_op jit(solution)/shard_map/pallas_call | solution.py:125
  7.3 1.6 %collective-permute-done.other_ref = bf16[24,4,512]{2,1,0:T(4,128)(2,1)S(1)} collective-permute-done((bf16[24,4,512]{2,1,0:T(4,128)(2,1)}, bf16[24,4,512]{2,1,0:T(4,128)(2,1)S(1)}, u32[]{:S(2)}, u32[]{:S(2)}) %collective-permute-start) | collective-permute-done | bytes 98336 | tf_op jit(solution)/shard_map/ppermute | solution.py:322
  8.9 0.6 shard_map.104
  9.4 0.2 convert_element_type.12
  9.6 1.9 %collective-permute-start.1 = (f16[8,96,512]{2,1,0:T(8,128)(2,1)S(1)}, f16[8,96,512]{2,1,0:T(8,128)(2,1)S(1)}, u32[]{:S(2)}, u32[]{:S(2)}) collective-permute-start(f16[8,96,512]{2,1,0:T(8,128)(2,1)S(1)} %convert_element_type.12), channel_id=1, source_target_pairs={{0,32},{32,0},{64,96},{96,64},{128,160},{160,128},{192,224},{224,1... | collective-permute-start | bytes 2359304 | tf_op jit(solution)/shard_map/ppermute | solution.py:328
  11.6 0.6 shard_map.103
  12.2 1.6 %collective-permute-done.1 = f16[8,96,512]{2,1,0:T(8,128)(2,1)S(1)} collective-permute-done((f16[8,96,512]{2,1,0:T(8,128)(2,1)S(1)}, f16[8,96,512]{2,1,0:T(8,128)(2,1)S(1)}, u32[]{:S(2)}, u32[]{:S(2)}) %collective-permute-start.1) | collective-permute-done | bytes 786464 | tf_op jit(solution)/shard_map/ppermute | solution.py:328
  13.8 1.2 %add_convert_fusion = f16[8,96,512]{2,1,0:T(8,128)(2,1)} fusion(f32[8,96,512]{2,1,0:T(8,128)S(1)} %shard_map.103, f16[8,96,512]{2,1,0:T(8,128)(2,1)S(1)} %collective-permute-done.1), kind=kLoop, calls=%fused_computation.1 | loop fusion | flops 1179648 | bytes 3145728 | tf_op jit(solution)/shard_map/convert_element_type | solution.py:330
  15.0 9.3 %all-to-all-start = ((f16[8,96,512]{2,1,0:T(8,128)(2,1)}), f16[8,96,512]{2,1,0:T(8,128)(2,1)S(1)}, u32[]{:S(2)}, u32[]{:S(2)}) async-start(f16[8,96,512]{2,1,0:T(8,128)(2,1)} %add_convert_fusion), calls=%async_computation | async-start | bytes 1572864 | tf_op jit(solution)/shard_map/all_to_all | solution.py:332
  24.2 1.9 %collective-permute-start.2 = (bf16[240,512]{1,0:T(8,128)(2,1)S(1)}, bf16[240,512]{1,0:T(8,128)(2,1)S(1)}, u32[]{:S(2)}, u32[]{:S(2)}) collective-permute-start(bf16[240,512]{1,0:T(8,128)(2,1)S(1)} %get-tuple-element.20), channel_id=1, source_target_pairs={{0,0},{1,256},{32,32},{33,288},{64,64},{65,320},{96,96},{97,352},{... | collective-permute-start | bytes 737288 | tf_op jit(solution)/shard_map/ppermute | solution.py:324
  26.1 10.1 %all-to-all-done = f16[8,96,512]{2,1,0:T(8,128)(2,1)S(1)} async-done(((f16[8,96,512]{2,1,0:T(8,128)(2,1)}), f16[8,96,512]{2,1,0:T(8,128)(2,1)S(1)}, u32[]{:S(2)}, u32[]{:S(2)}) %all-to-all-start) | async-done | bytes 786464 | tf_op jit(solution)/shard_map/all_to_all | solution.py:332
  36.4 0.7 shard_map.105
  37.0 16.3 %all_to_all.10 = bf16[8,104,512]{2,1,0:T(8,128)(2,1)S(1)} all-to-all(bf16[8,104,512]{2,1,0:T(8,128)(2,1)S(1)} %get-tuple-element.21), channel_id=1, replica_groups={{0,64,128,192,256,320,384,448},{32,96,160,224,288,352,416,480},{1,65,12..., dimensions={0} | all-to-all | bytes 1703936 | tf_op jit(solution)/shard_map/all_to_all | solution.py:336
  53.4 1.9 %collective-permute-start.3 = (bf16[8,104,512]{2,1,0:T(8,128)(2,1)S(1)}, bf16[8,104,512]{2,1,0:T(8,128)(2,1)S(1)}, u32[]{:S(2)}, u32[]{:S(2)}) collective-permute-start(bf16[8,104,512]{2,1,0:T(8,128)(2,1)S(1)} %all_to_all.10), channel_id=1, source_target_pairs={{0,32},{32,0},{64,96},{96,64},{128,160},{160,128},{192,224},{224,1... | collective-permute-start | bytes 2555912 | tf_op jit(solution)/shard_map/ppermute | solution.py:338
  55.3 1.9 %collective-permute-start.4 = (bf16[120,512]{1,0:T(8,128)(2,1)S(1)}, bf16[120,512]{1,0:T(8,128)(2,1)S(1)}, u32[]{:S(2)}, u32[]{:S(2)}) collective-permute-start(bf16[120,512]{1,0:T(8,128)(2,1)S(1)} %get-tuple-element.24), channel_id=1, source_target_pairs={{0,0},{1,256},{32,32},{33,288},{64,64},{65,320},{96,96},{97,352},{... | collective-permute-start | bytes 368648 | tf_op jit(solution)/shard_map/ppermute | solution.py:339
  57.2 2.2 %copy-done = bf16[512,4096]{1,0:T(8,128)(2,1)S(1)} copy-done((bf16[512,4096]{1,0:T(8,128)(2,1)S(1)}, bf16[512,4096]{1,0:T(8,128)(2,1)}, u32[]{:S(2)}) %copy-start) | copy-done | bytes 4194328
  59.4 0.8 %shard_map.106.acc_ref = f32[2,96,512]{2,1,0:T(8,128)S(1)} custom-call(bf16[2,4,104,512]{3,2,1,0:T(8,128)(2,1)S(1)} %bitcast.3, bf16[512,4096]{1,0:T(8,128)(2,1)S(1)} %copy-done), custom_call_target="tpu_custom_call" | custom-call | flops 402653184 | bytes 2097152 | tf_op jit(solution)/shard_map/pallas_call | solution.py:210
  60.2 2.7 %collective-permute-done.4.back_ref = bf16[120,512]{1,0:T(8,128)(2,1)S(1)} collective-permute-done((bf16[120,512]{1,0:T(8,128)(2,1)S(1)}, bf16[120,512]{1,0:T(8,128)(2,1)S(1)}, u32[]{:S(2)}, u32[]{:S(2)}) %collective-permute-start.4) | collective-permute-done | bytes 122912 | tf_op jit(solution)/shard_map/ppermute | solution.py:339
  62.9 0.8 %shard_map.108 = (bf16[128,512]{1,0:T(8,128)(2,1)S(1)}, f32[8,512]{1,0:T(8,128)S(1)}) custom-call(bf16[2,4,104,512]{3,2,1,0:T(8,128)(2,1)S(1)} %bitcast.5, bf16[2,4,104,512]{3,2,1,0:T(8,128)(2,1)S(1)} %bitcast.4, bf16[512,4096]{1,0:T(8,128)(2,1)S(1)} %copy-done, f32[2,96,512]{2,1,0:T(8,128)S(1)} %shard_map.106.acc_ref, ...), custom_call_target="tpu_custom_call" | custom-call | flops 201326592 | bytes 2097152 | tf_op jit(solution)/shard_map/pallas_call | solution.py:248
  63.7 1.9 %collective-permute-start.5 = (bf16[128,512]{1,0:T(8,128)(2,1)S(1)}, bf16[128,512]{1,0:T(8,128)(2,1)S(1)}, u32[]{:S(2)}, u32[]{:S(2)}) collective-permute-start(bf16[128,512]{1,0:T(8,128)(2,1)S(1)} %get-tuple-element.27), channel_id=1, source_target_pairs={{0,1},{1,0},{2,3},{3,2},{4,5},{5,4},{6,7},{7,6},{8,9},{9,8},{10,11... | collective-permute-start | bytes 393224 | tf_op jit(solution)/shard_map/ppermute | solution.py:344
  65.6 1.3 %shard_map.107 = (f32[96,512]{1,0:T(8,128)S(1)}, bf16[24,4,512]{2,1,0:T(4,128)(2,1)}) custom-call(bf16[2,4,104,512]{3,2,1,0:T(8,128)(2,1)S(1)} %bitcast.6, bf16[512,4096]{1,0:T(8,128)(2,1)S(1)} %copy-done, f32[2,96,512]{2,1,0:T(8,128)S(1)} %shard_map.106.acc_ref, bf16[120,512]{1,0:T(8,128)(2,1)S(1)} %collective-permute-done.4.back_ref), custom_call_target="tpu_custom_call" | custom-call | flops 201326592 | bytes 2097152 | tf_op jit(solution)/shard_map/pallas_call | solution.py:273
  66.9 5.2 %collective-permute-done.5.recv_ref = bf16[128,512]{1,0:T(8,128)(2,1)S(1)} collective-permute-done((bf16[128,512]{1,0:T(8,128)(2,1)S(1)}, bf16[128,512]{1,0:T(8,128)(2,1)S(1)}, u32[]{:S(2)}, u32[]{:S(2)}) %collective-permute-start.5) | collective-permute-done | bytes 131104 | tf_op jit(solution)/shard_map/ppermute | solution.py:344
  72.1 0.8 %shard_map.109 = (bf16[24,4,512]{2,1,0:T(4,128)(2,1)}, f32[4,24]{1,0:T(4,128)}, f32[24,512]{1,0:T(8,128)}) custom-call(f32[96,512]{1,0:T(8,128)S(1)} %get-tuple-element.26.keep_ref, bf16[128,512]{1,0:T(8,128)(2,1)S(1)} %collective-permute-done.5.recv_ref, f32[8,512]{1,0:T(8,128)S(1)} %get-tuple-element.28.bias_ref, ...), custom_call_target="tpu_custom_call" | custom-call | bytes 196608 | tf_op jit(solution)/shard_map/pallas_call | solution.py:305
  (5 shorter events, 0.1 us)
Async XLA Ops:
  0.6 8.2 %collective-permute-start = (bf16[24,4,512]{2,1,0:T(4,128)(2,1)}, bf16[24,4,512]{2,1,0:T(4,128)(2,1)S(1)}, u32[]{:S(2)}, u32[]{:S(2)}) collective-permute-start(bf16[24,4,512]{2,1,0:T(4,128)(2,1)} %refs_6_.1), channel_id=1, source_target_pairs={{0,1},{1,0},{2,3},{3,2},{4,5},{5,4},{6,7},{7,6},{8,9},{9,8},{10,11... | collective-permute-start | bytes 294920 | tf_op jit(solution)/shard_map/ppermute | solution.py:322
  9.6 4.2 %collective-permute-start.1 = (f16[8,96,512]{2,1,0:T(8,128)(2,1)S(1)}, f16[8,96,512]{2,1,0:T(8,128)(2,1)S(1)}, u32[]{:S(2)}, u32[]{:S(2)}) collective-permute-start(f16[8,96,512]{2,1,0:T(8,128)(2,1)S(1)} %convert_element_type.12), channel_id=1, source_target_pairs={{0,32},{32,0},{64,96},{96,64},{128,160},{160,128},{192,224},{224,1... | collective-permute-start | bytes 2359304 | tf_op jit(solution)/shard_map/ppermute | solution.py:328
  15.0 21.3 %all-to-all-start = ((f16[8,96,512]{2,1,0:T(8,128)(2,1)}), f16[8,96,512]{2,1,0:T(8,128)(2,1)S(1)}, u32[]{:S(2)}, u32[]{:S(2)}) async-start(f16[8,96,512]{2,1,0:T(8,128)(2,1)} %add_convert_fusion), calls=%async_computation | async-start | bytes 1572864 | tf_op jit(solution)/shard_map/all_to_all | solution.py:332
  24.2 12.1 %collective-permute-start.2 = (bf16[240,512]{1,0:T(8,128)(2,1)S(1)}, bf16[240,512]{1,0:T(8,128)(2,1)S(1)}, u32[]{:S(2)}, u32[]{:S(2)}) collective-permute-start(bf16[240,512]{1,0:T(8,128)(2,1)S(1)} %get-tuple-element.20), channel_id=1, source_target_pairs={{0,0},{1,256},{32,32},{33,288},{64,64},{65,320},{96,96},{97,352},{... | collective-permute-start | bytes 737288 | tf_op jit(solution)/shard_map/ppermute | solution.py:324
  53.4 9.5 %collective-permute-start.3 = (bf16[8,104,512]{2,1,0:T(8,128)(2,1)S(1)}, bf16[8,104,512]{2,1,0:T(8,128)(2,1)S(1)}, u32[]{:S(2)}, u32[]{:S(2)}) collective-permute-start(bf16[8,104,512]{2,1,0:T(8,128)(2,1)S(1)} %all_to_all.10), channel_id=1, source_target_pairs={{0,32},{32,0},{64,96},{96,64},{128,160},{160,128},{192,224},{224,1... | collective-permute-start | bytes 2555912 | tf_op jit(solution)/shard_map/ppermute | solution.py:338
  55.3 7.6 %collective-permute-start.4 = (bf16[120,512]{1,0:T(8,128)(2,1)S(1)}, bf16[120,512]{1,0:T(8,128)(2,1)S(1)}, u32[]{:S(2)}, u32[]{:S(2)}) collective-permute-start(bf16[120,512]{1,0:T(8,128)(2,1)S(1)} %get-tuple-element.24), channel_id=1, source_target_pairs={{0,0},{1,256},{32,32},{33,288},{64,64},{65,320},{96,96},{97,352},{... | collective-permute-start | bytes 368648 | tf_op jit(solution)/shard_map/ppermute | solution.py:339
  57.2 2.2 %copy-start = (bf16[512,4096]{1,0:T(8,128)(2,1)S(1)}, bf16[512,4096]{1,0:T(8,128)(2,1)}, u32[]{:S(2)}) copy-start(bf16[512,4096]{1,0:T(8,128)(2,1)} %w_ref.5) | copy-start | bytes 12582916
  63.7 8.4 %collective-permute-start.5 = (bf16[128,512]{1,0:T(8,128)(2,1)S(1)}, bf16[128,512]{1,0:T(8,128)(2,1)S(1)}, u32[]{:S(2)}, u32[]{:S(2)}) collective-permute-start(bf16[128,512]{1,0:T(8,128)(2,1)S(1)} %get-tuple-element.27), channel_id=1, source_target_pairs={{0,1},{1,0},{2,3},{3,2},{4,5},{5,4},{6,7},{7,6},{8,9},{9,8},{10,11... | collective-permute-start | bytes 393224 | tf_op jit(solution)/shard_map/ppermute | solution.py:344

commit v6 on v5

--- a/solution.py
+++ b/solution.py
@@ -192,44 +192,81 @@
     return lax.dot_general(g, block, (((1,), (1,)), ((), ())), preferred_element_type=jnp.float32)
 
 
-def near_back_kernel(g_ref, w_ref, acc_ref):
+def half_copies(w_ref, half_ref, sems, core):
+    width = w_ref.shape[0]
+    return [
+        pltpu.make_async_copy(
+            w_ref.at[:, pl.ds(pl.multiple_of((2 * i + core) * width, width), width)], half_ref.at[i], sems.at[i]
+        )
+        for i in range(LINE)
+    ]
+
+
+def stage_kernel(w_ref, half_ref, sems):
+    _, core = spec_and_core()
+    copies = half_copies(w_ref, half_ref, sems, core)
+    for copy in copies:
+        copy.start()
+    for copy in copies:
+        copy.wait()
+
+
+def stage(w):
+    return pl.pallas_call(
+        stage_kernel,
+        out_shape=pltpu.VMEM((LINE, w.shape[0], w.shape[0]), w.dtype),
+        in_specs=[HBM_SPEC],
+        out_specs=VMEM_SPEC,
+        scratch_shapes=[pltpu.SemaphoreType.DMA((LINE,))],
+        compiler_params=pltpu.CompilerParams(vmem_limit_bytes=VMEM),
+        cost_estimate=cost(0, w.size * 2),
+    )(in_hbm(w))
+
+
+def near_back_kernel(g_ref, half_ref, w_ref, acc_ref, next_ref, sems):
     rows = acc_ref.shape[1]
     _, core = spec_and_core()
+    copies = half_copies(w_ref, next_ref, sems, 1 - core)
+    for copy in copies:
+        copy.start()
     acc = None
     for i in range(LINE):
         both = jnp.concatenate([g_ref[0, i, :rows], g_ref[1, i, :rows]], axis=0)
-        part = against(both, columns(w_ref, i, core))
+        part = against(both, half_ref[i])
         acc = part if acc is None else acc + part
     acc_ref[0] = acc[:rows]
     acc_ref[1] = acc[rows:]
-
-
-def near_back(g, w):
+    for copy in copies:
+        copy.wait()
+
+
+def near_back(g, half, w):
     _, _, high, width = g.shape
     rows = high - 8
     return pl.pallas_call(
         near_back_kernel,
-        out_shape=pltpu.VMEM((2, rows, width), jnp.float32),
-        in_specs=[VMEM_SPEC, VMEM_SPEC],
-        out_specs=VMEM_SPEC,
+        out_shape=(pltpu.VMEM((2, rows, width), jnp.float32), pltpu.VMEM(half.shape, w.dtype)),
+        in_specs=[VMEM_SPEC, VMEM_SPEC, HBM_SPEC],
+        out_specs=(VMEM_SPEC, VMEM_SPEC),
+        scratch_shapes=[pltpu.SemaphoreType.DMA((LINE,))],
         compiler_params=pltpu.CompilerParams(vmem_limit_bytes=VMEM),
         cost_estimate=cost(2 * 2 * rows * width * width * LINE, width * width * LINE * 2),
-    )(in_vmem(g), in_vmem(w))
-
-
-def far_rows(which, core, g_ref, w_ref, acc_ref):
+    )(in_vmem(g), in_vmem(half), in_hbm(w))
+
+
+def far_rows(which, g_ref, half_ref, acc_ref):
     rows = acc_ref.shape[1]
     acc = acc_ref[which]
     for i in range(LINE):
-        acc = acc + against(g_ref[which, i, :rows], columns(w_ref, i, 1 - core))
+        acc = acc + against(g_ref[which, i, :rows], half_ref[i])
     return acc
 
 
 def send_kernel(g_ref, near_ref, w_ref, acc_ref, back_ref, send_ref, bias_ref):
     rows, width = acc_ref.shape[1:]
-    own, core = spec_and_core()
+    own, _ = spec_and_core()
     other = 1 - own
-    send_ref[0:rows] = far_rows(other, core, g_ref, w_ref, acc_ref).astype(jnp.bfloat16)
+    send_ref[0:rows] = far_rows(other, g_ref, w_ref, acc_ref).astype(jnp.bfloat16)
     bias = []
     for k in range(2):
         lines = jnp.zeros((8, width), jnp.float32)
@@ -263,8 +300,8 @@
 
 
 def keep_kernel(g_ref, w_ref, acc_ref, back_ref, keep_ref, relaxed_ref):
-    own, core = spec_and_core()
-    keep_ref[...] = far_rows(own, core, g_ref, w_ref, acc_ref)
+    own, _ = spec_and_core()
+    keep_ref[...] = far_rows(own, g_ref, w_ref, acc_ref)
     relaxed_ref[...] = as_boxes(back_ref[: keep_ref.shape[0]], relaxed_ref)
 
 
@@ -334,15 +371,16 @@
     grad, back = middle(pre, ops)
 
     grads = lax.all_to_all(grad, "neuron", 0, 0, axis_index_groups=SAME_CORE, tiled=True)
+    back = lax.ppermute(back, BOTH, MIDDLE_SWAP)
+    half = stage(weight)
     grads, back = lax.optimization_barrier((grads, back))
     far_grads = lax.ppermute(grads, "neuron", CORE_SWAP)
-    back = lax.ppermute(back, BOTH, MIDDLE_SWAP)
     four = (2, LINE, rows + 8, width)
     grads, far_grads = grads.reshape(four), far_grads.reshape(four)
-    acc = near_back(grads, weight)
-    send, bias = send_rows(far_grads, grads, weight, acc, back)
+    acc, rest = near_back(grads, half, weight)
+    send, bias = send_rows(far_grads, grads, rest, acc, back)
     recv = lax.ppermute(send, "spec", SPEC_SWAP)
-    keep, new_coeff = keep_rows(far_grads, weight, acc, back, coeff.shape)
+    keep, new_coeff = keep_rows(far_grads, rest, acc, back, coeff.shape)
     coeff_grad, offset, slope_grad = finish(keep, recv, bias, back, nboxes)
     return new_coeff, offset.T, slope_grad, coeff_grad
 

time: 73.3 us -> 73.9 us (level)
  the two profiles are of different devices: /device:TPU:8 before, /device:TPU:1 now
where the time goes in v6:
time: 73.9 us; the launch traced here: 73.4 us
  waiting for transfers between devices  31.8 us (43%)
  starting transfers between devices  27.5 us (37%)
  Pallas kernels  11.8 us (16%)
  other arithmetic  1.46 us (2%)
  between operations  0.79 us (1%)
    all_to_all x1, waiting for transfers between devices, step(): lax.all_to_all(grad, 'neuron', 0, 0, axis_index_groups=SAME_CORE, tiled=T...  13 us
    all_to_all x1, waiting for transfers between devices, step(): lax.all_to_all(chunks, 'neuron', 0, 0, axis_index_groups=SAME_CORE, tiled...  12.3 us
    ppermute x1, starting transfers between devices, step(): came = lax.ppermute(away, 'neuron', CORE_SWAP)  8.85 us
    ppermute x1, starting transfers between devices, step(): other = lax.ppermute(coeff, 'spec', SPEC_SWAP)  5.64 us
    ppermute x1, waiting for transfers between devices, step(): recv = lax.ppermute(send, 'spec', SPEC_SWAP)  5.18 us
    all_to_all x1, starting transfers between devices, step(): lax.all_to_all(grad, 'neuron', 0, 0, axis_index_groups=SAME_CORE, tiled=T...  3.55 us
    all_to_all x1, starting transfers between devices, step(): lax.all_to_all(chunks, 'neuron', 0, 0, axis_index_groups=SAME_CORE, tiled...  3.55 us
    ppermute x1, starting transfers between devices, step(): far_grads = lax.ppermute(grads, 'neuron', CORE_SWAP)  2.68 us
  transfers between devices with their start and end apart: 8, of which 4 were waited for; matrix products, arithmetic and copies ran while one was open for 0% of the time, Pallas kernels for 11%

profile of v6, /device:TPU:1, one launch (start us, length us, event | category | flops | bytes accessed | tf_op | source)
XLA Modules:
  0.0 73.4 jit_solution(1519021088288869447)
XLA Ops:
  0.6 5.6 %collective-permute-start = (bf16[24,4,512]{2,1,0:T(4,128)(2,1)}, bf16[24,4,512]{2,1,0:T(4,128)(2,1)S(1)}, u32[]{:S(2)}, u32[]{:S(2)}) collective-permute-start(bf16[24,4,512]{2,1,0:T(4,128)(2,1)} %refs_6_.1), channel_id=1, source_target_pairs={{0,1},{1,0},{2,3},{3,2},{4,5},{5,4},{6,7},{7,6},{8,9},{9,8},{10,11... | collective-permute-start | bytes 294920 | tf_op jit(solution)/shard_map/ppermute | solution.py:359
  6.3 2.4 %shard_map.102 = (bf16[512,4096]{1,0:T(8,128)(2,1)S(1)}, bf16[240,512]{1,0:T(8,128)(2,1)S(1)}, bf16[96,512]{1,0:T(8,128)(2,1)S(1)}) custom-call(bf16[512,4096]{1,0:T(8,128)(2,1)} %w_ref.3, f32[24,512]{1,0:T(8,128)} %refs_1_.1, f32[24,512]{1,0:T(8,128)} %refs_2_.1, f32[24,512]{1,0:T(8,128)} %refs_3_.1, s32[24,512]{1,0:T(8,128)} %refs_4_.1, ...), custom_call_target="tpu_custom_call" | custom-call | bytes 4194304 | tf_op jit(solution)/shard_map/pallas_call | solution.py:125
  8.7 0.6 shard_map.104
  9.3 0.2 convert_element_type.12
  9.5 8.9 %collective-permute-start.1 = (f16[8,96,512]{2,1,0:T(8,128)(2,1)S(1)}, f16[8,96,512]{2,1,0:T(8,128)(2,1)S(1)}, u32[]{:S(2)}, u32[]{:S(2)}) collective-permute-start(f16[8,96,512]{2,1,0:T(8,128)(2,1)S(1)} %convert_element_type.12), channel_id=1, source_target_pairs={{0,32},{32,0},{64,96},{96,64},{128,160},{160,128},{192,224},{224,1... | collective-permute-start | bytes 2359304 | tf_op jit(solution)/shard_map/ppermute | solution.py:365
  18.4 0.6 shard_map.103
  19.0 1.3 %collective-permute-done.1 = f16[8,96,512]{2,1,0:T(8,128)(2,1)S(1)} collective-permute-done((f16[8,96,512]{2,1,0:T(8,128)(2,1)S(1)}, f16[8,96,512]{2,1,0:T(8,128)(2,1)S(1)}, u32[]{:S(2)}, u32[]{:S(2)}) %collective-permute-start.1) | collective-permute-done | bytes 786464 | tf_op jit(solution)/shard_map/ppermute | solution.py:365
  20.3 1.2 %add_convert_fusion = f16[8,96,512]{2,1,0:T(8,128)(2,1)} fusion(f32[8,96,512]{2,1,0:T(8,128)S(1)} %shard_map.103, f16[8,96,512]{2,1,0:T(8,128)(2,1)S(1)} %collective-permute-done.1), kind=kLoop, calls=%fused_computation.1 | loop fusion | flops 1179648 | bytes 3145728 | tf_op jit(solution)/shard_map/convert_element_type | solution.py:367
  21.4 3.5 %all-to-all-start = ((f16[8,96,512]{2,1,0:T(8,128)(2,1)}), f16[8,96,512]{2,1,0:T(8,128)(2,1)S(1)}, u32[]{:S(2)}, u32[]{:S(2)}) async-start(f16[8,96,512]{2,1,0:T(8,128)(2,1)} %add_convert_fusion), calls=%async_computation | async-start | bytes 1572864 | tf_op jit(solution)/shard_map/all_to_all | solution.py:369
  25.0 0.7 collective-permute-start.2
  25.7 12.3 %all-to-all-done = f16[8,96,512]{2,1,0:T(8,128)(2,1)S(1)} async-done(((f16[8,96,512]{2,1,0:T(8,128)(2,1)}), f16[8,96,512]{2,1,0:T(8,128)(2,1)S(1)}, u32[]{:S(2)}, u32[]{:S(2)}) %all-to-all-start) | async-done | bytes 786464 | tf_op jit(solution)/shard_map/all_to_all | solution.py:369
  38.0 0.1 convert_reduce_fusion
  38.1 1.6 %shard_map.105 = (bf16[8,104,512]{2,1,0:T(8,128)(2,1)}, bf16[120,512]{1,0:T(8,128)(2,1)S(1)}) custom-call(f32[96,512]{1,0:T(8,128)S(1)} %broadcast_multiply_fusion.r_ref, bf16[240,512]{1,0:T(8,128)(2,1)S(1)} %collective-permute-done.2.ops_ref), custom_call_target="tpu_custom_call" | custom-call | flops 1474560 | bytes 1572864 | tf_op jit(solution)/shard_map/pallas_call | solution.py:178
  39.7 3.5 %all-to-all-start.1 = ((bf16[8,104,512]{2,1,0:T(8,128)(2,1)}), bf16[8,104,512]{2,1,0:T(8,128)(2,1)S(1)}, u32[]{:S(2)}, u32[]{:S(2)}) async-start(bf16[8,104,512]{2,1,0:T(8,128)(2,1)} %get-tuple-element.23), calls=%async_computation.1 | async-start | bytes 1703936 | tf_op jit(solution)/shard_map/all_to_all | solution.py:373
  43.3 0.7 collective-permute-start.3
  44.0 13.0 %all-to-all-done.1 = bf16[8,104,512]{2,1,0:T(8,128)(2,1)S(1)} async-done(((bf16[8,104,512]{2,1,0:T(8,128)(2,1)}), bf16[8,104,512]{2,1,0:T(8,128)(2,1)S(1)}, u32[]{:S(2)}, u32[]{:S(2)}) %all-to-all-start.1) | async-done | bytes 852000 | tf_op jit(solution)/shard_map/all_to_all | solution.py:373
  57.0 2.7 %collective-permute-start.4 = (bf16[8,104,512]{2,1,0:T(8,128)(2,1)S(1)}, bf16[8,104,512]{2,1,0:T(8,128)(2,1)S(1)}, u32[]{:S(2)}, u32[]{:S(2)}) collective-permute-start(bf16[8,104,512]{2,1,0:T(8,128)(2,1)S(1)} %all-to-all-done.1), channel_id=1, source_target_pairs={{0,32},{32,0},{64,96},{96,64},{128,160},{160,128},{192,224},{224,1... | collective-permute-start | bytes 2555912 | tf_op jit(solution)/shard_map/ppermute | solution.py:377
  59.7 1.6 %shard_map.106.half_ref = bf16[4,512,512]{2,1,0:T(8,128)(2,1)S(1)} custom-call(bf16[512,4096]{1,0:T(8,128)(2,1)} %w_ref.3), custom_call_target="tpu_custom_call" | custom-call | bytes 4194304 | tf_op jit(solution)/shard_map/pallas_call | solution.py:215
  61.2 2.2 %shard_map.107 = (f32[2,96,512]{2,1,0:T(8,128)S(1)}, bf16[4,512,512]{2,1,0:T(8,128)(2,1)S(1)}) custom-call(bf16[2,4,104,512]{3,2,1,0:T(8,128)(2,1)S(1)} %bitcast.3, bf16[4,512,512]{2,1,0:T(8,128)(2,1)S(1)} %shard_map.106.half_ref, bf16[512,4096]{1,0:T(8,128)(2,1)} %w_ref.3), custom_call_target="tpu_custom_call" | custom-call | flops 402653184 | bytes 2097152 | tf_op jit(solution)/shard_map/pallas_call | solution.py:246
  63.4 0.8 %shard_map.109 = (bf16[128,512]{1,0:T(8,128)(2,1)S(1)}, f32[8,512]{1,0:T(8,128)S(1)}) custom-call(bf16[2,4,104,512]{3,2,1,0:T(8,128)(2,1)S(1)} %bitcast.5, bf16[2,4,104,512]{3,2,1,0:T(8,128)(2,1)S(1)} %bitcast.4, bf16[4,512,512]{2,1,0:T(8,128)(2,1)S(1)} %get-tuple-element.26.w_ref, f32[2,96,512]{2,1,0:T(8,128)S(1)} %get-tuple-element.27.acc_ref, ...), custom_call_target="tpu_custom_call" | custom-call | flops 201326592 | bytes 2097152 | tf_op jit(solution)/shard_map/pallas_call | solution.py:285
  64.2 1.9 %collective-permute-start.5 = (bf16[128,512]{1,0:T(8,128)(2,1)S(1)}, bf16[128,512]{1,0:T(8,128)(2,1)S(1)}, u32[]{:S(2)}, u32[]{:S(2)}) collective-permute-start(bf16[128,512]{1,0:T(8,128)(2,1)S(1)} %get-tuple-element.31), channel_id=1, source_target_pairs={{0,1},{1,0},{2,3},{3,2},{4,5},{5,4},{6,7},{7,6},{8,9},{9,8},{10,11... | collective-permute-start | bytes 393224 | tf_op jit(solution)/shard_map/ppermute | solution.py:382
  66.1 1.3 %shard_map.108 = (f32[96,512]{1,0:T(8,128)S(1)}, bf16[24,4,512]{2,1,0:T(4,128)(2,1)}) custom-call(bf16[2,4,104,512]{3,2,1,0:T(8,128)(2,1)S(1)} %bitcast.6, bf16[4,512,512]{2,1,0:T(8,128)(2,1)S(1)} %get-tuple-element.26.w_ref, f32[2,96,512]{2,1,0:T(8,128)S(1)} %get-tuple-element.27.acc_ref, bf16[120,512]{1,0:T(8,128)(2,1)S(1)} %collective-permute-done.3.back_ref), custom_call_target="tpu_custom_call" | custom-call | flops 201326592 | bytes 2097152 | tf_op jit(solution)/shard_map/pallas_call | solution.py:310
  67.5 5.2 %collective-permute-done.5.recv_ref = bf16[128,512]{1,0:T(8,128)(2,1)S(1)} collective-permute-done((bf16[128,512]{1,0:T(8,128)(2,1)S(1)}, bf16[128,512]{1,0:T(8,128)(2,1)S(1)}, u32[]{:S(2)}, u32[]{:S(2)}) %collective-permute-start.5) | collective-permute-done | bytes 131104 | tf_op jit(solution)/shard_map/ppermute | solution.py:382
  72.6 0.8 %shard_map.110 = (bf16[24,4,512]{2,1,0:T(4,128)(2,1)}, f32[4,24]{1,0:T(4,128)}, f32[24,512]{1,0:T(8,128)}) custom-call(f32[96,512]{1,0:T(8,128)S(1)} %get-tuple-element.30.keep_ref, bf16[128,512]{1,0:T(8,128)(2,1)S(1)} %collective-permute-done.5.recv_ref, f32[8,512]{1,0:T(8,128)S(1)} %get-tuple-element.32.bias_ref, ...), custom_call_target="tpu_custom_call" | custom-call | bytes 196608 | tf_op jit(solution)/shard_map/pallas_call | solution.py:342
  (5 shorter events, 0.0 us)
Async XLA Ops:
  0.6 8.1 %collective-permute-start = (bf16[24,4,512]{2,1,0:T(4,128)(2,1)}, bf16[24,4,512]{2,1,0:T(4,128)(2,1)S(1)}, u32[]{:S(2)}, u32[]{:S(2)}) collective-permute-start(bf16[24,4,512]{2,1,0:T(4,128)(2,1)} %refs_6_.1), channel_id=1, source_target_pairs={{0,1},{1,0},{2,3},{3,2},{4,5},{5,4},{6,7},{7,6},{8,9},{9,8},{10,11... | collective-permute-start | bytes 294920 | tf_op jit(solution)/shard_map/ppermute | solution.py:359
  9.5 10.8 %collective-permute-start.1 = (f16[8,96,512]{2,1,0:T(8,128)(2,1)S(1)}, f16[8,96,512]{2,1,0:T(8,128)(2,1)S(1)}, u32[]{:S(2)}, u32[]{:S(2)}) collective-permute-start(f16[8,96,512]{2,1,0:T(8,128)(2,1)S(1)} %convert_element_type.12), channel_id=1, source_target_pairs={{0,32},{32,0},{64,96},{96,64},{128,160},{160,128},{192,224},{224,1... | collective-permute-start | bytes 2359304 | tf_op jit(solution)/shard_map/ppermute | solution.py:365
  21.4 16.6 %all-to-all-start = ((f16[8,96,512]{2,1,0:T(8,128)(2,1)}), f16[8,96,512]{2,1,0:T(8,128)(2,1)S(1)}, u32[]{:S(2)}, u32[]{:S(2)}) async-start(f16[8,96,512]{2,1,0:T(8,128)(2,1)} %add_convert_fusion), calls=%async_computation | async-start | bytes 1572864 | tf_op jit(solution)/shard_map/all_to_all | solution.py:369
  25.0 13.1 %collective-permute-start.2 = (bf16[240,512]{1,0:T(8,128)(2,1)S(1)}, bf16[240,512]{1,0:T(8,128)(2,1)S(1)}, u32[]{:S(2)}, u32[]{:S(2)}) collective-permute-start(bf16[240,512]{1,0:T(8,128)(2,1)S(1)} %get-tuple-element.22), channel_id=1, source_target_pairs={{0,0},{1,256},{32,32},{33,288},{64,64},{65,320},{96,96},{97,352},{... | collective-permute-start | bytes 737288 | tf_op jit(solution)/shard_map/ppermute | solution.py:361
  39.7 17.3 %all-to-all-start.1 = ((bf16[8,104,512]{2,1,0:T(8,128)(2,1)}), bf16[8,104,512]{2,1,0:T(8,128)(2,1)S(1)}, u32[]{:S(2)}, u32[]{:S(2)}) async-start(bf16[8,104,512]{2,1,0:T(8,128)(2,1)} %get-tuple-element.23), calls=%async_computation.1 | async-start | bytes 1703936 | tf_op jit(solution)/shard_map/all_to_all | solution.py:373
  43.3 0.7 collective-permute-start.3
  57.0 6.5 %collective-permute-start.4 = (bf16[8,104,512]{2,1,0:T(8,128)(2,1)S(1)}, bf16[8,104,512]{2,1,0:T(8,128)(2,1)S(1)}, u32[]{:S(2)}, u32[]{:S(2)}) collective-permute-start(bf16[8,104,512]{2,1,0:T(8,128)(2,1)S(1)} %all-to-all-done.1), channel_id=1, source_target_pairs={{0,32},{32,0},{64,96},{96,64},{128,160},{160,128},{192,224},{224,1... | collective-permute-start | bytes 2555912 | tf_op jit(solution)/shard_map/ppermute | solution.py:377
  64.2 8.4 %collective-permute-start.5 = (bf16[128,512]{1,0:T(8,128)(2,1)S(1)}, bf16[128,512]{1,0:T(8,128)(2,1)S(1)}, u32[]{:S(2)}, u32[]{:S(2)}) collective-permute-start(bf16[128,512]{1,0:T(8,128)(2,1)S(1)} %get-tuple-element.31), channel_id=1, source_target_pairs={{0,1},{1,0},{2,3},{3,2},{4,5},{5,4},{6,7},{7,6},{8,9},{9,8},{10,11... | collective-permute-start | bytes 393224 | tf_op jit(solution)/shard_map/ppermute | solution.py:382

commit v7 on v6

--- a/solution.py
+++ b/solution.py
@@ -137,7 +137,7 @@
     )(*map(in_hbm, (w, *given)))
 
 
-def middle_kernel(r_ref, ops_ref, g_ref, back_ref):
+def middle_kernel(r_ref, ops_ref, g_ref, back_ref, tile_ref, sems):
     pre = r_ref[...]
     rows, width = pre.shape
     boxes = (ops_ref.shape[0] - rows) // 6
@@ -149,13 +149,9 @@
         return jnp.broadcast_to(value[:, None, :], (boxes, specs, width)).reshape(rows, width)
 
     a, b, c = operand(0), operand(1), operand(2)
-    positive = jnp.maximum(pre, 0.0)
     negative = jnp.minimum(pre, 0.0)
     cot = ops_ref[0:rows].astype(jnp.float32)
-    back_ref[0:rows] = (a * positive + b * negative).astype(jnp.bfloat16)
-    grad = (cot * jnp.where(pre > 0.0, a, b)).astype(jnp.bfloat16)
-    for k in range(CHIPS):
-        g_ref[k, 0:rows] = grad
+    tile_ref[0:rows] = (cot * jnp.where(pre > 0.0, a, b)).astype(jnp.bfloat16)
     line = lax.dot_general(
         jnp.ones((8, width), jnp.float32),
         negative * c,
@@ -166,11 +162,17 @@
     high = line.astype(jnp.bfloat16).astype(jnp.float32)
     row = lax.broadcasted_iota(jnp.int32, line.shape, 0)
     tile = jnp.where(row == 0, high, jnp.where(row == 1, line - high, 0.0))
-    tile = jnp.concatenate([tile, jnp.zeros((8, width - rows), jnp.float32)], axis=1).astype(jnp.bfloat16)
-    for k in range(CHIPS):
-        g_ref[k, rows : rows + 8] = tile
+    tile = jnp.concatenate([tile, jnp.zeros((8, width - rows), jnp.float32)], axis=1)
+    tile_ref[rows : rows + 8] = tile.astype(jnp.bfloat16)
+    copies = [pltpu.make_async_copy(tile_ref, g_ref.at[k], sems.at[k]) for k in range(CHIPS)]
+    for copy in copies:
+        copy.start()
+    positive = jnp.maximum(pre, 0.0)
+    back_ref[0:rows] = (a * positive + b * negative).astype(jnp.bfloat16)
     slope = jnp.where(c > 0.0, cot * positive, 0.0).reshape(boxes, specs, width)
     back_ref[rows : rows + boxes] = jnp.sum(slope, axis=1).astype(jnp.bfloat16)
+    for copy in copies:
+        copy.wait()
 
 
 def middle(r, ops):
@@ -178,11 +180,12 @@
     return pl.pallas_call(
         middle_kernel,
         out_shape=(
-            jax.ShapeDtypeStruct((CHIPS, rows + 8, width), jnp.bfloat16),
-            jax.ShapeDtypeStruct((rows + rows // 4, width), jnp.bfloat16),
+            pltpu.HBM((CHIPS, rows + 8, width), jnp.bfloat16),
+            pltpu.VMEM((rows + rows // 4, width), jnp.bfloat16),
         ),
         in_specs=[VMEM_SPEC] * 2,
-        out_specs=(VMEM_SPEC,) * 2,
+        out_specs=(HBM_SPEC, VMEM_SPEC),
+        scratch_shapes=[pltpu.VMEM((rows + 8, width), jnp.bfloat16), pltpu.SemaphoreType.DMA((CHIPS,))],
         compiler_params=pltpu.CompilerParams(vmem_limit_bytes=VMEM),
         cost_estimate=cost(30 * rows * width, 8 * rows * width * 4),
     )(r, ops)

time: 73.9 us -> 73.9 us (level)
  no operation moved by 1% of the time
where the time goes in v7:
time: 73.9 us; the launch traced here: 73.5 us
  waiting for transfers between devices  31.8 us (43%)
  starting transfers between devices  27.5 us (37%)
  Pallas kernels  11.9 us (16%)
  other arithmetic  1.46 us (2%)
  between operations  0.8 us (1%)
    all_to_all x1, waiting for transfers between devices, step(): lax.all_to_all(grad, 'neuron', 0, 0, axis_index_groups=SAME_CORE, tiled=T...  13 us
    all_to_all x1, waiting for transfers between devices, step(): lax.all_to_all(chunks, 'neuron', 0, 0, axis_index_groups=SAME_CORE, tiled...  12.3 us
    ppermute x1, starting transfers between devices, step(): came = lax.ppermute(away, 'neuron', CORE_SWAP)  8.85 us
    ppermute x1, starting transfers between devices, step(): other = lax.ppermute(coeff, 'spec', SPEC_SWAP)  5.64 us
    ppermute x1, waiting for transfers between devices, step(): recv = lax.ppermute(send, 'spec', SPEC_SWAP)  5.19 us
    all_to_all x1, starting transfers between devices, step(): lax.all_to_all(grad, 'neuron', 0, 0, axis_index_groups=SAME_CORE, tiled=T...  3.56 us
    all_to_all x1, starting transfers between devices, step(): lax.all_to_all(chunks, 'neuron', 0, 0, axis_index_groups=SAME_CORE, tiled...  3.55 us
    ppermute x1, starting transfers between devices, step(): far_grads = lax.ppermute(grads, 'neuron', CORE_SWAP)  2.68 us
  transfers between devices with their start and end apart: 8, of which 4 were waited for; matrix products, arithmetic and copies ran while one was open for 0% of the time, Pallas kernels for 11%

profile of v7, /device:TPU:1, one launch (start us, length us, event | category | flops | bytes accessed | tf_op | source)
XLA Modules:
  0.0 73.5 jit_solution(17509428541369567851)
XLA Ops:
  0.6 5.6 %collective-permute-start = (bf16[24,4,512]{2,1,0:T(4,128)(2,1)}, bf16[24,4,512]{2,1,0:T(4,128)(2,1)S(1)}, u32[]{:S(2)}, u32[]{:S(2)}) collective-permute-start(bf16[24,4,512]{2,1,0:T(4,128)(2,1)} %refs_6_.1), channel_id=1, source_target_pairs={{0,1},{1,0},{2,3},{3,2},{4,5},{5,4},{6,7},{7,6},{8,9},{9,8},{10,11... | collective-permute-start | bytes 294920 | tf_op jit(solution)/shard_map/ppermute | solution.py:362
  6.3 2.4 %shard_map.102 = (bf16[512,4096]{1,0:T(8,128)(2,1)S(1)}, bf16[240,512]{1,0:T(8,128)(2,1)S(1)}, bf16[96,512]{1,0:T(8,128)(2,1)S(1)}) custom-call(bf16[512,4096]{1,0:T(8,128)(2,1)} %w_ref.3, f32[24,512]{1,0:T(8,128)} %refs_1_.1, f32[24,512]{1,0:T(8,128)} %refs_2_.1, f32[24,512]{1,0:T(8,128)} %refs_3_.1, s32[24,512]{1,0:T(8,128)} %refs_4_.1, ...), custom_call_target="tpu_custom_call" | custom-call | bytes 4194304 | tf_op jit(solution)/shard_map/pallas_call | solution.py:125
  8.7 0.6 shard_map.104
  9.3 0.2 convert_element_type.12
  9.5 8.9 %collective-permute-start.1 = (f16[8,96,512]{2,1,0:T(8,128)(2,1)S(1)}, f16[8,96,512]{2,1,0:T(8,128)(2,1)S(1)}, u32[]{:S(2)}, u32[]{:S(2)}) collective-permute-start(f16[8,96,512]{2,1,0:T(8,128)(2,1)S(1)} %convert_element_type.12), channel_id=1, source_target_pairs={{0,32},{32,0},{64,96},{96,64},{128,160},{160,128},{192,224},{224,1... | collective-permute-start | bytes 2359304 | tf_op jit(solution)/shard_map/ppermute | solution.py:368
  18.4 0.6 shard_map.103
  19.0 1.3 %collective-permute-done.1 = f16[8,96,512]{2,1,0:T(8,128)(2,1)S(1)} collective-permute-done((f16[8,96,512]{2,1,0:T(8,128)(2,1)S(1)}, f16[8,96,512]{2,1,0:T(8,128)(2,1)S(1)}, u32[]{:S(2)}, u32[]{:S(2)}) %collective-permute-start.1) | collective-permute-done | bytes 786464 | tf_op jit(solution)/shard_map/ppermute | solution.py:368
  20.3 1.2 %add_convert_fusion = f16[8,96,512]{2,1,0:T(8,128)(2,1)} fusion(f32[8,96,512]{2,1,0:T(8,128)S(1)} %shard_map.103, f16[8,96,512]{2,1,0:T(8,128)(2,1)S(1)} %collective-permute-done.1), kind=kLoop, calls=%fused_computation.1 | loop fusion | flops 1179648 | bytes 3145728 | tf_op jit(solution)/shard_map/convert_element_type | solution.py:370
  21.4 3.5 %all-to-all-start = ((f16[8,96,512]{2,1,0:T(8,128)(2,1)}), f16[8,96,512]{2,1,0:T(8,128)(2,1)S(1)}, u32[]{:S(2)}, u32[]{:S(2)}) async-start(f16[8,96,512]{2,1,0:T(8,128)(2,1)} %add_convert_fusion), calls=%async_computation | async-start | bytes 1572864 | tf_op jit(solution)/shard_map/all_to_all | solution.py:372
  25.0 0.7 collective-permute-start.2
  25.7 12.3 %all-to-all-done = f16[8,96,512]{2,1,0:T(8,128)(2,1)S(1)} async-done(((f16[8,96,512]{2,1,0:T(8,128)(2,1)}), f16[8,96,512]{2,1,0:T(8,128)(2,1)S(1)}, u32[]{:S(2)}, u32[]{:S(2)}) %all-to-all-start) | async-done | bytes 786464 | tf_op jit(solution)/shard_map/all_to_all | solution.py:372
  38.0 0.1 convert_reduce_fusion
  38.1 1.6 %shard_map.105 = (bf16[8,104,512]{2,1,0:T(8,128)(2,1)}, bf16[120,512]{1,0:T(8,128)(2,1)S(1)}) custom-call(f32[96,512]{1,0:T(8,128)S(1)} %broadcast_multiply_fusion.r_ref, bf16[240,512]{1,0:T(8,128)(2,1)S(1)} %collective-permute-done.2.ops_ref), custom_call_target="tpu_custom_call" | custom-call | flops 1474560 | bytes 1572864 | tf_op jit(solution)/shard_map/pallas_call | solution.py:180
  39.8 3.6 %all-to-all-start.1 = ((bf16[8,104,512]{2,1,0:T(8,128)(2,1)}), bf16[8,104,512]{2,1,0:T(8,128)(2,1)S(1)}, u32[]{:S(2)}, u32[]{:S(2)}) async-start(bf16[8,104,512]{2,1,0:T(8,128)(2,1)} %get-tuple-element.23), calls=%async_computation.1 | async-start | bytes 1703936 | tf_op jit(solution)/shard_map/all_to_all | solution.py:376
  43.4 0.7 collective-permute-start.3
  44.0 13.0 %all-to-all-done.1 = bf16[8,104,512]{2,1,0:T(8,128)(2,1)S(1)} async-done(((bf16[8,104,512]{2,1,0:T(8,128)(2,1)}), bf16[8,104,512]{2,1,0:T(8,128)(2,1)S(1)}, u32[]{:S(2)}, u32[]{:S(2)}) %all-to-all-start.1) | async-done | bytes 852000 | tf_op jit(solution)/shard_map/all_to_all | solution.py:376
  57.1 2.7 %collective-permute-start.4 = (bf16[8,104,512]{2,1,0:T(8,128)(2,1)S(1)}, bf16[8,104,512]{2,1,0:T(8,128)(2,1)S(1)}, u32[]{:S(2)}, u32[]{:S(2)}) collective-permute-start(bf16[8,104,512]{2,1,0:T(8,128)(2,1)S(1)} %all-to-all-done.1), channel_id=1, source_target_pairs={{0,32},{32,0},{64,96},{96,64},{128,160},{160,128},{192,224},{224,1... | collective-permute-start | bytes 2555912 | tf_op jit(solution)/shard_map/ppermute | solution.py:380
  59.7 1.6 %shard_map.106.half_ref = bf16[4,512,512]{2,1,0:T(8,128)(2,1)S(1)} custom-call(bf16[512,4096]{1,0:T(8,128)(2,1)} %w_ref.3), custom_call_target="tpu_custom_call" | custom-call | bytes 4194304 | tf_op jit(solution)/shard_map/pallas_call | solution.py:218
  61.3 2.2 %shard_map.107 = (f32[2,96,512]{2,1,0:T(8,128)S(1)}, bf16[4,512,512]{2,1,0:T(8,128)(2,1)S(1)}) custom-call(bf16[2,4,104,512]{3,2,1,0:T(8,128)(2,1)S(1)} %bitcast.3, bf16[4,512,512]{2,1,0:T(8,128)(2,1)S(1)} %shard_map.106.half_ref, bf16[512,4096]{1,0:T(8,128)(2,1)} %w_ref.3), custom_call_target="tpu_custom_call" | custom-call | flops 402653184 | bytes 2097152 | tf_op jit(solution)/shard_map/pallas_call | solution.py:249
  63.5 0.8 %shard_map.109 = (bf16[128,512]{1,0:T(8,128)(2,1)S(1)}, f32[8,512]{1,0:T(8,128)S(1)}) custom-call(bf16[2,4,104,512]{3,2,1,0:T(8,128)(2,1)S(1)} %bitcast.5, bf16[2,4,104,512]{3,2,1,0:T(8,128)(2,1)S(1)} %bitcast.4, bf16[4,512,512]{2,1,0:T(8,128)(2,1)S(1)} %get-tuple-element.26.w_ref, f32[2,96,512]{2,1,0:T(8,128)S(1)} %get-tuple-element.27.acc_ref, ...), custom_call_target="tpu_custom_call" | custom-call | flops 201326592 | bytes 2097152 | tf_op jit(solution)/shard_map/pallas_call | solution.py:288
  64.3 1.9 %collective-permute-start.5 = (bf16[128,512]{1,0:T(8,128)(2,1)S(1)}, bf16[128,512]{1,0:T(8,128)(2,1)S(1)}, u32[]{:S(2)}, u32[]{:S(2)}) collective-permute-start(bf16[128,512]{1,0:T(8,128)(2,1)S(1)} %get-tuple-element.31), channel_id=1, source_target_pairs={{0,1},{1,0},{2,3},{3,2},{4,5},{5,4},{6,7},{7,6},{8,9},{9,8},{10,11... | collective-permute-start | bytes 393224 | tf_op jit(solution)/shard_map/ppermute | solution.py:385
  66.2 1.3 %shard_map.108 = (f32[96,512]{1,0:T(8,128)S(1)}, bf16[24,4,512]{2,1,0:T(4,128)(2,1)}) custom-call(bf16[2,4,104,512]{3,2,1,0:T(8,128)(2,1)S(1)} %bitcast.6, bf16[4,512,512]{2,1,0:T(8,128)(2,1)S(1)} %get-tuple-element.26.w_ref, f32[2,96,512]{2,1,0:T(8,128)S(1)} %get-tuple-element.27.acc_ref, bf16[120,512]{1,0:T(8,128)(2,1)S(1)} %collective-permute-done.3.back_ref), custom_call_target="tpu_custom_call" | custom-call | flops 201326592 | bytes 2097152 | tf_op jit(solution)/shard_map/pallas_call | solution.py:313
  67.5 5.2 %collective-permute-done.5.recv_ref = bf16[128,512]{1,0:T(8,128)(2,1)S(1)} collective-permute-done((bf16[128,512]{1,0:T(8,128)(2,1)S(1)}, bf16[128,512]{1,0:T(8,128)(2,1)S(1)}, u32[]{:S(2)}, u32[]{:S(2)}) %collective-permute-start.5) | collective-permute-done | bytes 131104 | tf_op jit(solution)/shard_map/ppermute | solution.py:385
  72.7 0.8 %shard_map.110 = (bf16[24,4,512]{2,1,0:T(4,128)(2,1)}, f32[4,24]{1,0:T(4,128)}, f32[24,512]{1,0:T(8,128)}) custom-call(f32[96,512]{1,0:T(8,128)S(1)} %get-tuple-element.30.keep_ref, bf16[128,512]{1,0:T(8,128)(2,1)S(1)} %collective-permute-done.5.recv_ref, f32[8,512]{1,0:T(8,128)S(1)} %get-tuple-element.32.bias_ref, ...), custom_call_target="tpu_custom_call" | custom-call | bytes 196608 | tf_op jit(solution)/shard_map/pallas_call | solution.py:345
  (5 shorter events, 0.0 us)
Async XLA Ops:
  0.6 8.1 %collective-permute-start = (bf16[24,4,512]{2,1,0:T(4,128)(2,1)}, bf16[24,4,512]{2,1,0:T(4,128)(2,1)S(1)}, u32[]{:S(2)}, u32[]{:S(2)}) collective-permute-start(bf16[24,4,512]{2,1,0:T(4,128)(2,1)} %refs_6_.1), channel_id=1, source_target_pairs={{0,1},{1,0},{2,3},{3,2},{4,5},{5,4},{6,7},{7,6},{8,9},{9,8},{10,11... | collective-permute-start | bytes 294920 | tf_op jit(solution)/shard_map/ppermute | solution.py:362
  9.5 10.8 %collective-permute-start.1 = (f16[8,96,512]{2,1,0:T(8,128)(2,1)S(1)}, f16[8,96,512]{2,1,0:T(8,128)(2,1)S(1)}, u32[]{:S(2)}, u32[]{:S(2)}) collective-permute-start(f16[8,96,512]{2,1,0:T(8,128)(2,1)S(1)} %convert_element_type.12), channel_id=1, source_target_pairs={{0,32},{32,0},{64,96},{96,64},{128,160},{160,128},{192,224},{224,1... | collective-permute-start | bytes 2359304 | tf_op jit(solution)/shard_map/ppermute | solution.py:368
  21.4 16.6 %all-to-all-start = ((f16[8,96,512]{2,1,0:T(8,128)(2,1)}), f16[8,96,512]{2,1,0:T(8,128)(2,1)S(1)}, u32[]{:S(2)}, u32[]{:S(2)}) async-start(f16[8,96,512]{2,1,0:T(8,128)(2,1)} %add_convert_fusion), calls=%async_computation | async-start | bytes 1572864 | tf_op jit(solution)/shard_map/all_to_all | solution.py:372
  25.0 13.1 %collective-permute-start.2 = (bf16[240,512]{1,0:T(8,128)(2,1)S(1)}, bf16[240,512]{1,0:T(8,128)(2,1)S(1)}, u32[]{:S(2)}, u32[]{:S(2)}) collective-permute-start(bf16[240,512]{1,0:T(8,128)(2,1)S(1)} %get-tuple-element.22), channel_id=1, source_target_pairs={{0,0},{1,256},{32,32},{33,288},{64,64},{65,320},{96,96},{97,352},{... | collective-permute-start | bytes 737288 | tf_op jit(solution)/shard_map/ppermute | solution.py:364
  39.8 17.3 %all-to-all-start.1 = ((bf16[8,104,512]{2,1,0:T(8,128)(2,1)}), bf16[8,104,512]{2,1,0:T(8,128)(2,1)S(1)}, u32[]{:S(2)}, u32[]{:S(2)}) async-start(bf16[8,104,512]{2,1,0:T(8,128)(2,1)} %get-tuple-element.23), calls=%async_computation.1 | async-start | bytes 1703936 | tf_op jit(solution)/shard_map/all_to_all | solution.py:376
  43.4 0.7 collective-permute-start.3
  57.1 6.5 %collective-permute-start.4 = (bf16[8,104,512]{2,1,0:T(8,128)(2,1)S(1)}, bf16[8,104,512]{2,1,0:T(8,128)(2,1)S(1)}, u32[]{:S(2)}, u32[]{:S(2)}) collective-permute-start(bf16[8,104,512]{2,1,0:T(8,128)(2,1)S(1)} %all-to-all-done.1), channel_id=1, source_target_pairs={{0,32},{32,0},{64,96},{96,64},{128,160},{160,128},{192,224},{224,1... | collective-permute-start | bytes 2555912 | tf_op jit(solution)/shard_map/ppermute | solution.py:380
  64.3 8.4 %collective-permute-start.5 = (bf16[128,512]{1,0:T(8,128)(2,1)S(1)}, bf16[128,512]{1,0:T(8,128)(2,1)S(1)}, u32[]{:S(2)}, u32[]{:S(2)}) collective-permute-start(bf16[128,512]{1,0:T(8,128)(2,1)S(1)} %get-tuple-element.31), channel_id=1, source_target_pairs={{0,1},{1,0},{2,3},{3,2},{4,5},{5,4},{6,7},{7,6},{8,9},{9,8},{10,11... | collective-permute-start | bytes 393224 | tf_op jit(solution)/shard_map/ppermute | solution.py:385
